TPU v7x, 32 devices: a whole 2x2x4 slice. The times are simulated.
32 devices in a mesh: dom: 8 (over z, y), grp: 4 (over x, core).
Axes of the slice: x: 2, y: 2, z: 4, core: 2. Of those that a mesh axis runs over, the one named last changes fastest.
Arguments:
- state_coeffs: float32 [6, 35, 2048], P(None, None, ('dom', 'grp')), may hold values from -6 to 6
- residual_in: float32 [6, 35, 2048], P(None, None, ('dom', 'grp')), may hold values from -6 to 6
- orders: int32 [2048], P(('dom', 'grp')), may hold values from 1 to 4
- neighbours: int32 [4, 2048], P(None, ('dom', 'grp')), may hold values from -1 to 2047, as said below
- neighbour_face: int32 [4, 2048], P(None, ('dom', 'grp')), may hold values from 0 to 3
- orientation: int32 [4, 2048], P(None, ('dom', 'grp')), may hold values from 0 to 5
- precond: bfloat16 [210, 430080], P(None, ('dom', 'grp'))
- source: float32 [6, 6, 2048], P(None, None, ('dom', 'grp'))
- flux_jacobian: float32 [3, 6, 6, 2048], P(None, None, None, ('dom', 'grp')), may hold values from -1.5 to 1.5
- geometry: float32 [3, 3, 2048], P(None, None, ('dom', 'grp')), may hold values from -3.5 to 3.5
- stiffness: float32 [3, 35, 35], replicated, may hold values from -1 to 1
- trace_matrix: float32 [4, 15, 35], replicated, may hold values from -1 to 1
Outputs:
- solution: float32 [6, 35, 2048], P(None, None, ('dom', 'grp'))
- hessenberg: float32 [7, 6], replicated
Inputs may be any that keep to these rules, and one draw needn't show every extreme that they name: `neighbours`: each entry is -1 or an element other than the face's own, differing from it by at most 64; that difference is reached in every draw.
All inputs are finite; a program needn't handle non-finite values.
Results may differ from a plain program's by a relative error of at most 0.00068.
Values sent between devices are 32-bit elements; how exact they have to be, the bound alone decides.
No kernel may reach another device: no remote copies, remote signals or barrier semaphores. Data moves between devices by JAX's collectives and lax.ppermute only.
A program may use at most 128 MiB of HBM per device.

v0:
```python
import jax
import jax.numpy as jnp
from jax import lax
from jax.sharding import PartitionSpec as P

ITERS = 6


EPSILON = 1e-06


def with_halo(block, sides, width):
    for axis, dim in sides:
        count = lax.axis_size(axis)
        forward = [(i, i + 1) for i in range(count - 1)]
        backward = [(target, source) for source, target in forward]
        low = lax.ppermute(
            lax.slice_in_dim(block, block.shape[dim] - width, None, axis=dim), axis, forward
        )
        high = lax.ppermute(lax.slice_in_dim(block, 0, width, axis=dim), axis, backward)
        block = jnp.concatenate([low, block, high], axis=dim)
    return block


def basis_count(orders):
    return (orders + 1) * (orders + 2) * (orders + 3) // 6


def order_mask(orders, nbasis):
    basis_ids = jnp.arange(nbasis, dtype=jnp.int32)[:, None]
    return (basis_ids < basis_count(orders)[None, :]).astype(jnp.float32)[None]


def point_order(orientation, npoints):
    points = jnp.arange(npoints, dtype=jnp.int32)[None, :, None]
    rotation = orientation[:, None, :] % 3
    reflected = orientation[:, None, :] // 3
    moved = (points + npoints // 3 * rotation) % npoints
    return jnp.where(reflected == 1, npoints - 1 - moved, moved)


def face_traces(field_vec, trace_matrix):
    return jnp.einsum("fqb,vbe->vfqe", trace_matrix, field_vec, precision=lax.Precision.HIGHEST)


def facing(traces_all, target, live_face, neighbour_face, orientation):
    nvar, nface, npts, span_len = traces_all.shape
    flat_traces = traces_all.reshape(nvar, nface * npts * span_len)
    flat_index = (
        neighbour_face[:, None, :] * npts + point_order(orientation, npts)
    ) * span_len + target[:, None, :]
    gathered = jnp.take(flat_traces, flat_index.reshape(-1), axis=1)
    gathered = gathered.reshape(nvar, nface, npts, target.shape[1])
    return gathered * live_face[None, :, None, :]


def operate(
    field_vec, own_traces, other_traces, gain, coupling, source, stiffness, trace_matrix, basis_mask
):
    high = lax.Precision.HIGHEST
    face_term = jnp.einsum(
        "fqb,vfqe->vbe", trace_matrix, gain * (own_traces - other_traces), precision=high
    )
    stiff_moved = jnp.einsum("dcb,vbe->dvce", stiffness, field_vec, precision=high)
    volume_term = jnp.einsum("dwve,dvce->wce", coupling, stiff_moved, precision=high)
    source_term = jnp.einsum("wve,vbe->wbe", source, field_vec, precision=high)
    return (volume_term + source_term + face_term) * basis_mask


def precondition(vector, precond, basis_mask):
    shape_in = vector.shape
    width = shape_in[0] * shape_in[1]
    blocks = precond.reshape(width, shape_in[2], width)
    flat_vec = (vector * basis_mask).astype(jnp.bfloat16).reshape(width, shape_in[2])
    applied = jnp.einsum("iej,je->ie", blocks, flat_vec, preferred_element_type=jnp.float32)
    return applied.reshape(shape_in) * basis_mask


def least_squares(hess, start_value):
    ncols = hess.shape[1]
    upper = [[hess[i, j] for j in range(ncols)] for i in range(ncols + 1)]
    right_vec = [start_value] + [jnp.zeros((), jnp.float32) for i in range(ncols)]
    for k in range(ncols):
        lead = upper[k][k]
        below = upper[k + 1][k]
        radius = jnp.sqrt(lead * lead + below * below)
        cosine = lead / radius
        sine_val = below / radius
        for j in range(k, ncols):
            top_val = upper[k][j]
            low_val = upper[k + 1][j]
            upper[k][j] = cosine * top_val + sine_val * low_val
            upper[k + 1][j] = cosine * low_val - sine_val * top_val
        top_val = right_vec[k]
        low_val = right_vec[k + 1]
        right_vec[k] = cosine * top_val + sine_val * low_val
        right_vec[k + 1] = cosine * low_val - sine_val * top_val
    coeffs = [None] * ncols
    for k in reversed(range(ncols)):
        accum = right_vec[k]
        for j in range(k + 1, ncols):
            accum = accum - upper[k][j] * coeffs[j]
        coeffs[k] = accum / upper[k][k]
    return coeffs


def body(
    state_coeffs,
    residual_in,
    orders,
    neighbours,
    neighbour_face,
    orientation,
    precond,
    source,
    flux_jacobian,
    geometry,
    stiffness,
    trace_matrix,
):
    high = lax.Precision.HIGHEST
    elem_count = state_coeffs.shape[2]
    basis_mask = order_mask(orders, state_coeffs.shape[1])
    offset_base = lax.axis_index(("dom", "grp")) * elem_count - elem_count
    live_face = (neighbours >= 0).astype(jnp.float32)
    target = jnp.clip(neighbours - offset_base, 0, 3 * elem_count - 1)
    coupling = jnp.einsum("dke,dwve->kwve", geometry, flux_jacobian, precision=high)
    start_vec = residual_in * basis_mask
    start_value = jnp.sqrt(lax.psum(jnp.sum(start_vec * start_vec), ("dom", "grp")) + EPSILON)
    basis = [start_vec / start_value]
    search = precondition(basis[0], precond, basis_mask)
    state_ext = with_halo(state_coeffs, ((("dom", "grp"), 2),), elem_count)
    search_ext = with_halo(search, ((("dom", "grp"), 2),), elem_count)
    state_tr = face_traces(state_ext, trace_matrix)
    state_own = state_tr[..., elem_count : 2 * elem_count]
    gain = 1.0 + 0.5 * jnp.abs(
        state_own + facing(state_tr, target, live_face, neighbour_face, orientation)
    )
    hess = jnp.zeros((ITERS + 1, ITERS), jnp.float32)
    searches = []
    for k in range(ITERS):
        if k > 0:
            search = precondition(basis[k], precond, basis_mask)
            search_ext = with_halo(search, ((("dom", "grp"), 2),), elem_count)
        traces_all = face_traces(search_ext, trace_matrix)
        own_traces = traces_all[..., elem_count : 2 * elem_count]
        other = facing(traces_all, target, live_face, neighbour_face, orientation)
        image = operate(
            search, own_traces, other, gain, coupling, source, stiffness, trace_matrix, basis_mask
        )
        krylov_stack = jnp.stack(basis)
        local_proj = jnp.einsum("kvbe,vbe->k", krylov_stack, image, precision=high)
        projection, square_sum = lax.psum((local_proj, jnp.sum(image * image)), ("dom", "grp"))
        image = image - jnp.einsum("k,kvbe->vbe", projection, krylov_stack, precision=high)
        norm_value = jnp.sqrt(square_sum - jnp.sum(projection * projection) + EPSILON)
        hess = hess.at[: k + 1, k].set(projection)
        hess = hess.at[k + 1, k].set(norm_value)
        if k + 1 < ITERS:
            basis.append(image / norm_value)
        searches.append(search)
    coeffs = least_squares(hess, start_value)
    solution = coeffs[0] * searches[0]
    for k in range(1, ITERS):
        solution = solution + coeffs[k] * searches[k]
    return (solution, hess)


def solution(mesh):
    placed = (
        P(None, None, ("dom", "grp")),
        P(None, None, ("dom", "grp")),
        P(("dom", "grp")),
        P(None, ("dom", "grp")),
        P(None, ("dom", "grp")),
        P(None, ("dom", "grp")),
        P(None, ("dom", "grp")),
        P(None, None, ("dom", "grp")),
        P(None, None, None, ("dom", "grp")),
        P(None, None, ("dom", "grp")),
        P(),
        P(),
    )
    return jax.shard_map(
        body,
        mesh=mesh,
        in_specs=placed,
        out_specs=(P(None, None, ("dom", "grp")), P()),
        check_vma=False,
    )
```

profile of v0, /device:TPU:0, one launch (start us, length us, event | category | flops | bytes accessed | tf_op | source)
XLA Modules:
  0.0 689.0 jit_solution(5734043655388363469)
XLA Ops:
  4.6 3.7 collective-permute-start
  8.2 42.4 %psum.91 = f32[]{:T(128)} all-reduce(f32[]{:T(128)} %multiply_reduce_fusion.7), channel_id=1, replica_groups=mesh['dom'=8,'grp'=4] {'dom','grp'}, use_global_device_ids=true, to_apply=%region_1.2 | all-reduce | flops 1 | bytes 8 | tf_op jit(solution)/shard_map/psum | solution.py:129
  51.7 23.2 %reshape.536 = bf16[210,64,210]{2,1,0:T(8,128)(2,1)} reshape(bf16[210,13440]{1,0:T(8,128)(2,1)} %param.44) | data formatting | bytes 11289600 | tf_op jit(solution)/shard_map/reshape | solution.py:73
  75.0 4.8 fusion
  81.6 3.9 collective-permute-start.2
  94.4 1.8 convolution_bitcast_fusion.19
  101.3 3.5 copy.351
  106.4 3.5 copy.349
  109.9 10.6 %gather_fusion.1 = f32[3840,6]{1,0:T(8,128)} fusion(f32[6,11520]{0,1:T(8,128)} %bitcast.457, s32[4096]{0:T(1024)S(1)} %pad_clamp_fusion), kind=kCustom, calls=%fused_computation.1.clone | custom fusion | bytes 199680 | tf_op jit(solution)/shard_map/jit(_take)/gather | solution.py:52
  120.5 10.6 %gather_fusion = f32[3840,6]{1,0:T(8,128)} fusion(f32[6,11520]{0,1:T(8,128)} %bitcast.458, s32[4096]{0:T(1024)S(1)} %pad_clamp_fusion), kind=kCustom, calls=%fused_computation.clone | custom fusion | bytes 199680 | tf_op jit(solution)/shard_map/jit(_take)/gather | solution.py:52
  131.1 4.4 broadcast_select_fusion.5
  135.5 2.9 copy.350
  142.6 2.1 multiply_reduce_fusion.6
  145.4 40.6 %all-reduce.6 = (f32[]{:T(128)}, f32[1]{0:T(128)}) all-reduce(f32[]{:T(128)} %get-tuple-element.226, f32[1]{0:T(128)} %bitcast.42), channel_id=1, replica_groups=mesh['dom'=8,'grp'=4] {'dom','grp'}, use_global_device_ids=true, to_apply=%region_4.6 | all-reduce | flops 2 | bytes 16 | tf_op jit(solution)/shard_map/psum | solution.py:153
  188.8 4.8 fusion.1
  196.0 3.8 collective-permute-start.4
  200.8 1.8 convolution_bitcast_fusion.18
  210.7 3.5 copy.357
  214.2 10.6 %gather_fusion.2 = f32[3840,6]{1,0:T(8,128)} fusion(f32[6,11520]{0,1:T(8,128)} %bitcast.460, s32[4096]{0:T(1024)S(1)} %pad_clamp_fusion), kind=kCustom, calls=%fused_computation.2.clone | custom fusion | bytes 199680 | tf_op jit(solution)/shard_map/jit(_take)/gather | solution.py:52
  224.7 3.5 broadcast_select_fusion.4
  231.3 2.2 multiply_reduce_fusion.5
  233.6 2.0 convolution_bitcast_fusion.26
  235.6 41.1 %all-reduce.5 = (f32[]{:T(128)}, f32[2]{0:T(128)S(1)}) all-reduce(f32[]{:T(128)} %get-tuple-element.228, f32[2]{0:T(128)S(1)} %convolution_bitcast_fusion.26), channel_id=1, replica_groups=mesh['dom'=8,'grp'=4] {'dom','grp'}, use_global_device_ids=true, to_apply=%region_8.10 | all-reduce | flops 3 | bytes 24 | tf_op jit(solution)/shard_map/psum | solution.py:153
  280.3 4.8 fusion.2
  287.4 3.7 collective-permute-start.6
  292.3 1.8 convolution_bitcast_fusion.17
  295.0 1.9 broadcast_select_fusion.11
  303.8 3.5 copy.363
  307.4 10.5 %gather_fusion.3 = f32[3840,6]{1,0:T(8,128)} fusion(f32[6,11520]{0,1:T(8,128)} %bitcast.461, s32[4096]{0:T(1024)S(1)} %pad_clamp_fusion), kind=kCustom, calls=%fused_computation.3.clone | custom fusion | bytes 199680 | tf_op jit(solution)/shard_map/jit(_take)/gather | solution.py:52
  317.9 3.5 broadcast_select_fusion.3
  324.4 2.2 multiply_reduce_fusion.4
  326.8 2.0 convolution_bitcast_fusion.30
  328.8 39.9 %all-reduce.4 = (f32[]{:T(128)}, f32[3]{0:T(128)S(1)}) all-reduce(f32[]{:T(128)} %get-tuple-element.230, f32[3]{0:T(128)S(1)} %convolution_bitcast_fusion.30), channel_id=1, replica_groups=mesh['dom'=8,'grp'=4] {'dom','grp'}, use_global_device_ids=true, to_apply=%region_13.15 | all-reduce | flops 4 | bytes 32 | tf_op jit(solution)/shard_map/psum | solution.py:153
  372.1 4.8 fusion.3
  378.5 3.7 collective-permute-start.8
  386.1 2.3 pad_maximum_fusion
  388.3 2.0 broadcast_select_fusion.10
  396.1 3.5 copy.369
  399.6 10.5 %gather_fusion.4 = f32[3840,6]{1,0:T(8,128)} fusion(f32[6,11520]{0,1:T(8,128)} %bitcast.462, s32[4096]{0:T(1024)S(1)} %pad_clamp_fusion), kind=kCustom, calls=%fused_computation.4.clone | custom fusion | bytes 199680 | tf_op jit(solution)/shard_map/jit(_take)/gather | solution.py:52
  410.2 3.5 broadcast_select_fusion.2
  416.7 2.2 multiply_reduce_fusion.3
  419.1 2.0 convolution_bitcast_fusion.29
  421.0 40.9 %all-reduce.3 = (f32[]{:T(128)}, f32[4]{0:T(128)S(1)}) all-reduce(f32[]{:T(128)} %get-tuple-element.232, f32[4]{0:T(128)S(1)} %convolution_bitcast_fusion.29), channel_id=1, replica_groups=mesh['dom'=8,'grp'=4] {'dom','grp'}, use_global_device_ids=true, to_apply=%region_18.20 | all-reduce | flops 5 | bytes 40 | tf_op jit(solution)/shard_map/psum | solution.py:153
  465.3 4.8 fusion.4
  471.7 3.7 collective-permute-start.10
  476.6 1.8 convolution_bitcast_fusion.15
  478.5 1.9 broadcast_select_fusion.9
  485.9 3.5 copy.375
  489.4 10.5 %gather_fusion.5 = f32[3840,6]{1,0:T(8,128)} fusion(f32[6,11520]{0,1:T(8,128)} %bitcast.463, s32[4096]{0:T(1024)S(1)} %pad_clamp_fusion), kind=kCustom, calls=%fused_computation.5.clone | custom fusion | bytes 199680 | tf_op jit(solution)/shard_map/jit(_take)/gather | solution.py:52
  499.9 3.5 broadcast_select_fusion.1
  506.5 2.2 multiply_reduce_fusion.2
  508.8 2.0 convolution_bitcast_fusion.28
  510.8 39.6 %all-reduce.2 = (f32[]{:T(128)}, f32[5]{0:T(128)S(1)}) all-reduce(f32[]{:T(128)} %get-tuple-element.234, f32[5]{0:T(128)S(1)} %convolution_bitcast_fusion.28), channel_id=1, replica_groups=mesh['dom'=8,'grp'=4] {'dom','grp'}, use_global_device_ids=true, to_apply=%region_23.25 | all-reduce | flops 6 | bytes 48 | tf_op jit(solution)/shard_map/psum | solution.py:153
  553.9 4.8 fusion.5
  560.3 3.7 collective-permute-start.12
  565.1 1.8 convolution_bitcast_fusion.14
  567.1 1.9 broadcast_select_fusion.8
  574.4 3.6 copy.381
  578.0 10.5 %gather_fusion.6 = f32[3840,6]{1,0:T(8,128)} fusion(f32[6,11520]{0,1:T(8,128)} %bitcast.459, s32[4096]{0:T(1024)S(1)} %pad_clamp_fusion), kind=kCustom, calls=%fused_computation.6.clone | custom fusion | bytes 199680 | tf_op jit(solution)/shard_map/jit(_take)/gather | solution.py:52
  588.5 3.5 broadcast_select_fusion
  593.4 2.3 multiply_reduce_fusion.1
  595.9 3.1 convolution_bitcast_fusion.27
  599.0 40.9 %all-reduce.1 = (f32[6]{0:T(128)S(1)}, f32[]{:T(128)}) all-reduce(f32[6]{0:T(128)S(1)} %convolution_bitcast_fusion.27, f32[]{:T(128)} %get-tuple-element.236), channel_id=1, replica_groups=mesh['dom'=8,'grp'=4] {'dom','grp'}, use_global_device_ids=true, to_apply=%region_26.28 | all-reduce | flops 7 | bytes 56 | tf_op jit(solution)/shard_map/psum | solution.py:153
  640.4 2.0 broadcast_select_fusion.7
  (299 shorter events, 104.4 us)
Async XLA Ops:
  0.6 85.5 %copy-start = (f32[3,35,35]{2,1,0:T(8,128)S(1)}, f32[3,35,35]{2,1,0:T(8,128)}, u32[]{:S(2)}) copy-start(f32[3,35,35]{2,1,0:T(8,128)} %param.48) | copy-start | bytes 44104
  0.6 104.2 %collective-permute-start.1 = (f32[6,35,64]{2,1,0:T(8,128)}, f32[6,35,64]{2,1,0:T(8,128)}, u32[]{:S(2)}, u32[]{:S(2)}) collective-permute-start(f32[6,35,64]{2,1,0:T(8,128)} %param.38), channel_id=1, source_target_pairs={{1,0},{2,1},{3,2},{4,3},{5,4},{6,5},{7,6},{8,7},{9,8},{10,9},{11,1... | collective-permute-start | bytes 161288 | tf_op jit(solution)/shard_map/ppermute | solution.py:20
  3.9 71.1 %copy-start.13 = (f32[6,35,64]{1,0,2:T(8,128)}, f32[6,35,64]{1,0,2:T(8,128)S(1)}, u32[]{:S(2)}) copy-start(f32[6,35,64]{1,0,2:T(8,128)S(1)} %copy.138) | copy-start | bytes 161284
  4.6 100.3 %collective-permute-start = (f32[6,35,64]{2,1,0:T(8,128)}, f32[6,35,64]{2,1,0:T(8,128)}, u32[]{:S(2)}, u32[]{:S(2)}) collective-permute-start(f32[6,35,64]{2,1,0:T(8,128)} %param.38), channel_id=1, source_target_pairs={{0,1},{1,2},{2,3},{3,4},{4,5},{5,6},{6,7},{7,8},{8,9},{9,10},{10,1... | collective-permute-start | bytes 161288 | tf_op jit(solution)/shard_map/ppermute | solution.py:17
  75.0 10.6 %copy-start.33 = (s32[4,64]{1,0:T(4,128)S(1)}, s32[4,64]{1,0:T(4,128)}, u32[]{:S(2)}) copy-start(s32[4,64]{1,0:T(4,128)} %param.43) | copy-start | bytes 3076
  75.0 10.7 %copy-start.34 = (s32[4,64]{1,0:T(4,128)S(1)}, s32[4,64]{1,0:T(4,128)}, u32[]{:S(2)}) copy-start(s32[4,64]{1,0:T(4,128)} %param.41) | copy-start | bytes 3076
  75.0 10.8 %copy-start.36 = (s32[4,64]{1,0:T(4,128)S(1)}, s32[4,64]{1,0:T(4,128)}, u32[]{:S(2)}) copy-start(s32[4,64]{1,0:T(4,128)} %param.42) | copy-start | bytes 3076
  79.8 7.4 %copy-start.32 = (f32[3,6,6,64]{3,2,1,0:T(8,128)S(1)}, f32[3,6,6,64]{3,2,1,0:T(8,128)}, u32[]{:S(2)}) copy-start(f32[3,6,6,64]{3,2,1,0:T(8,128)} %param.46) | copy-start | bytes 82948
  80.0 62.5 %copy-start.1 = (f32[6,35,64]{1,0,2:T(8,128)}, f32[6,35,64]{1,0,2:T(8,128)S(1)}, u32[]{:S(2)}) copy-start(f32[6,35,64]{1,0,2:T(8,128)S(1)} %copy.140) | copy-start | bytes 161284
  80.0 7.6 %copy-start.35 = (f32[3,3,64]{2,1,0:T(4,128)S(1)}, f32[3,3,64]{2,1,0:T(4,128)}, u32[]{:S(2)}) copy-start(f32[3,3,64]{2,1,0:T(4,128)} %param.47) | copy-start | bytes 6916
  80.1 8.2 %copy-start.40 = (s32[2]{0:T(128)S(1)}, s32[2]{0:T(128)}, u32[]{:S(2)}) copy-start(s32[2]{0:T(128)} %constant.433.clone.1) | copy-start | bytes 28
  80.1 9.6 %copy-start.39 = (s32[2]{0:T(128)S(1)}, s32[2]{0:T(128)}, u32[]{:S(2)}) copy-start(s32[2]{0:T(128)} %constant.434.clone.1) | copy-start | bytes 28
  80.1 10.8 %copy-start.38 = (s32[2]{0:T(128)S(1)}, s32[2]{0:T(128)}, u32[]{:S(2)}) copy-start(s32[2]{0:T(128)} %constant.435.clone.1) | copy-start | bytes 28
  80.1 12.0 %copy-start.37 = (s32[2]{0:T(128)S(1)}, s32[2]{0:T(128)}, u32[]{:S(2)}) copy-start(s32[2]{0:T(128)} %constant.436.clone.1) | copy-start | bytes 28
  80.1 18.3 %collective-permute-start.3 = (f32[6,35,64]{1,0,2:T(8,128)S(1)}, f32[6,35,64]{1,0,2:T(8,128)}, u32[]{:S(2)}, u32[]{:S(2)}) collective-permute-start(f32[6,35,64]{1,0,2:T(8,128)S(1)} %broadcast_multiply_fusion.5), channel_id=1, source_target_pairs={{1,0},{2,1},{3,2},{4,3},{5,4},{6,5},{7,6},{8,7},{9,8},{10,9},{11,1... | collective-permute-start | bytes 161288 | tf_op jit(solution)/shard_map/ppermute | solution.py:20
  81.6 18.0 %collective-permute-start.2 = (f32[6,35,64]{1,0,2:T(8,128)S(1)}, f32[6,35,64]{1,0,2:T(8,128)}, u32[]{:S(2)}, u32[]{:S(2)}) collective-permute-start(f32[6,35,64]{1,0,2:T(8,128)S(1)} %broadcast_multiply_fusion.5), channel_id=1, source_target_pairs={{0,1},{1,2},{2,3},{3,4},{4,5},{5,6},{6,7},{7,8},{8,9},{9,10},{10,1... | collective-permute-start | bytes 161288 | tf_op jit(solution)/shard_map/ppermute | solution.py:17
  94.3 6.3 copy-start.15
  101.3 3.6 copy-start.18
  101.3 3.6 copy-start.31
  106.4 3.6 copy-start.19
  139.8 4.9 copy-start.14
  193.9 8.7 %copy-start.3 = (f32[6,35,64]{1,0,2:T(8,128)}, f32[6,35,64]{1,0,2:T(8,128)S(1)}, u32[]{:S(2)}) copy-start(f32[6,35,64]{1,0,2:T(8,128)S(1)} %copy.161) | copy-start | bytes 161284
  194.7 13.2 %collective-permute-start.5 = (f32[6,35,64]{1,0,2:T(8,128)}, f32[6,35,64]{1,0,2:T(8,128)}, u32[]{:S(2)}, u32[]{:S(2)}) collective-permute-start(f32[6,35,64]{1,0,2:T(8,128)} %broadcast_multiply_fusion.4), channel_id=1, source_target_pairs={{1,0},{2,1},{3,2},{4,3},{5,4},{6,5},{7,6},{8,7},{9,8},{10,9},{11,1... | collective-permute-start | bytes 161288 | tf_op jit(solution)/shard_map/ppermute | solution.py:20
  196.0 13.0 %collective-permute-start.4 = (f32[6,35,64]{1,0,2:T(8,128)}, f32[6,35,64]{1,0,2:T(8,128)}, u32[]{:S(2)}, u32[]{:S(2)}) collective-permute-start(f32[6,35,64]{1,0,2:T(8,128)} %broadcast_multiply_fusion.4), channel_id=1, source_target_pairs={{0,1},{1,2},{2,3},{3,4},{4,5},{5,6},{6,7},{7,8},{8,9},{9,10},{10,1... | collective-permute-start | bytes 161288 | tf_op jit(solution)/shard_map/ppermute | solution.py:17
  202.9 6.0 copy-start.26
  204.3 9.9 %copy-start.16 = (f32[5,6,35,64]{3,2,1,0:T(8,128)}, f32[5,6,35,64]{3,2,1,0:T(8,128)S(1)}, u32[]{:S(2)}) copy-start(f32[5,6,35,64]{3,2,1,0:T(8,128)S(1)} %get-tuple-element.185) | copy-start | bytes 806404
  210.6 3.5 copy-start.20
  229.6 4.0 copy-start.28
  229.6 4.0 copy-start.29
  285.3 8.7 %copy-start.5 = (f32[6,35,64]{1,0,2:T(8,128)}, f32[6,35,64]{1,0,2:T(8,128)S(1)}, u32[]{:S(2)}) copy-start(f32[6,35,64]{1,0,2:T(8,128)S(1)} %copy.178) | copy-start | bytes 161284
  286.1 14.9 %collective-permute-start.7 = (f32[6,35,64]{1,0,2:T(8,128)}, f32[6,35,64]{1,0,2:T(8,128)}, u32[]{:S(2)}, u32[]{:S(2)}) collective-permute-start(f32[6,35,64]{1,0,2:T(8,128)} %broadcast_multiply_fusion.3), channel_id=1, source_target_pairs={{1,0},{2,1},{3,2},{4,3},{5,4},{6,5},{7,6},{8,7},{9,8},{10,9},{11,1... | collective-permute-start | bytes 161288 | tf_op jit(solution)/shard_map/ppermute | solution.py:20
  287.4 14.7 %collective-permute-start.6 = (f32[6,35,64]{1,0,2:T(8,128)}, f32[6,35,64]{1,0,2:T(8,128)}, u32[]{:S(2)}, u32[]{:S(2)}) collective-permute-start(f32[6,35,64]{1,0,2:T(8,128)} %broadcast_multiply_fusion.3), channel_id=1, source_target_pairs={{0,1},{1,2},{2,3},{3,4},{4,5},{5,6},{6,7},{7,8},{8,9},{9,10},{10,1... | collective-permute-start | bytes 161288 | tf_op jit(solution)/shard_map/ppermute | solution.py:17
  291.2 3.0 copy-start.27
  303.8 3.5 copy-start.21
  322.8 4.0 copy-start.24
  377.1 8.9 %copy-start.7 = (f32[6,35,64]{1,0,2:T(8,128)}, f32[6,35,64]{1,0,2:T(8,128)S(1)}, u32[]{:S(2)}) copy-start(f32[6,35,64]{1,0,2:T(8,128)S(1)} %copy.196) | copy-start | bytes 161284
  377.2 16.1 %collective-permute-start.9 = (f32[6,35,64]{1,0,2:T(8,128)S(1)}, f32[6,35,64]{1,0,2:T(8,128)}, u32[]{:S(2)}, u32[]{:S(2)}) collective-permute-start(f32[6,35,64]{1,0,2:T(8,128)S(1)} %broadcast_multiply_fusion.2), channel_id=1, source_target_pairs={{1,0},{2,1},{3,2},{4,3},{5,4},{6,5},{7,6},{8,7},{9,8},{10,9},{11,1... | collective-permute-start | bytes 161288 | tf_op jit(solution)/shard_map/ppermute | solution.py:20
  378.5 15.9 %collective-permute-start.8 = (f32[6,35,64]{1,0,2:T(8,128)S(1)}, f32[6,35,64]{1,0,2:T(8,128)}, u32[]{:S(2)}, u32[]{:S(2)}) collective-permute-start(f32[6,35,64]{1,0,2:T(8,128)S(1)} %broadcast_multiply_fusion.2), channel_id=1, source_target_pairs={{0,1},{1,2},{2,3},{3,4},{4,5},{5,6},{6,7},{7,8},{8,9},{9,10},{10,1... | collective-permute-start | bytes 161288 | tf_op jit(solution)/shard_map/ppermute | solution.py:17
  383.9 2.1 copy-start.30
  396.1 3.5 copy-start.22
  415.0 4.0 copy-start.25
  470.4 8.0 %copy-start.9 = (f32[6,35,64]{1,0,2:T(8,128)}, f32[6,35,64]{1,0,2:T(8,128)S(1)}, u32[]{:S(2)}) copy-start(f32[6,35,64]{1,0,2:T(8,128)S(1)} %copy.215) | copy-start | bytes 161284
  470.4 12.6 %collective-permute-start.11 = (f32[6,35,64]{1,0,2:T(8,128)S(1)}, f32[6,35,64]{1,0,2:T(8,128)}, u32[]{:S(2)}, u32[]{:S(2)}) collective-permute-start(f32[6,35,64]{1,0,2:T(8,128)S(1)} %broadcast_multiply_fusion.1), channel_id=1, source_target_pairs={{1,0},{2,1},{3,2},{4,3},{5,4},{6,5},{7,6},{8,7},{9,8},{10,9},{11,1... | collective-permute-start | bytes 161288 | tf_op jit(solution)/shard_map/ppermute | solution.py:20
  471.7 12.4 %collective-permute-start.10 = (f32[6,35,64]{1,0,2:T(8,128)S(1)}, f32[6,35,64]{1,0,2:T(8,128)}, u32[]{:S(2)}, u32[]{:S(2)}) collective-permute-start(f32[6,35,64]{1,0,2:T(8,128)S(1)} %broadcast_multiply_fusion.1), channel_id=1, source_target_pairs={{0,1},{1,2},{2,3},{3,4},{4,5},{5,6},{6,7},{7,8},{8,9},{9,10},{10,1... | collective-permute-start | bytes 161288 | tf_op jit(solution)/shard_map/ppermute | solution.py:17
  485.8 3.5 copy-start.23
  504.8 4.0 copy-start.17
  558.9 8.0 %copy-start.11 = (f32[6,35,64]{1,0,2:T(8,128)}, f32[6,35,64]{1,0,2:T(8,128)S(1)}, u32[]{:S(2)}) copy-start(f32[6,35,64]{1,0,2:T(8,128)S(1)} %copy.235) | copy-start | bytes 161284
  559.0 12.7 %collective-permute-start.13 = (f32[6,35,64]{1,0,2:T(8,128)S(1)}, f32[6,35,64]{1,0,2:T(8,128)}, u32[]{:S(2)}, u32[]{:S(2)}) collective-permute-start(f32[6,35,64]{1,0,2:T(8,128)S(1)} %broadcast_multiply_fusion), channel_id=1, source_target_pairs={{1,0},{2,1},{3,2},{4,3},{5,4},{6,5},{7,6},{8,7},{9,8},{10,9},{11,1... | collective-permute-start | bytes 161288 | tf_op jit(solution)/shard_map/ppermute | solution.py:20
  560.3 12.5 %collective-permute-start.12 = (f32[6,35,64]{1,0,2:T(8,128)S(1)}, f32[6,35,64]{1,0,2:T(8,128)}, u32[]{:S(2)}, u32[]{:S(2)}) collective-permute-start(f32[6,35,64]{1,0,2:T(8,128)S(1)} %broadcast_multiply_fusion), channel_id=1, source_target_pairs={{0,1},{1,2},{2,3},{3,4},{4,5},{5,6},{6,7},{7,8},{8,9},{9,10},{10,1... | collective-permute-start | bytes 161288 | tf_op jit(solution)/shard_map/ppermute | solution.py:17
  593.2 94.6 %copy-start.2 = (f32[6,35,64]{1,0,2:T(8,128)S(1)}, f32[6,35,64]{1,0,2:T(8,128)}, u32[]{:S(2)}) copy-start(f32[6,35,64]{1,0,2:T(8,128)} %copy-done.1) | copy-start | bytes 161284
  593.2 94.6 %copy-start.4 = (f32[6,35,64]{1,0,2:T(8,128)S(1)}, f32[6,35,64]{1,0,2:T(8,128)}, u32[]{:S(2)}) copy-start(f32[6,35,64]{1,0,2:T(8,128)} %copy-done.3) | copy-start | bytes 161284
  593.2 94.6 %copy-start.6 = (f32[6,35,64]{1,0,2:T(8,128)S(1)}, f32[6,35,64]{1,0,2:T(8,128)}, u32[]{:S(2)}) copy-start(f32[6,35,64]{1,0,2:T(8,128)} %copy-done.5) | copy-start | bytes 161284
  593.2 94.6 %copy-start.8 = (f32[6,35,64]{1,0,2:T(8,128)S(1)}, f32[6,35,64]{1,0,2:T(8,128)}, u32[]{:S(2)}) copy-start(f32[6,35,64]{1,0,2:T(8,128)} %copy-done.7) | copy-start | bytes 161284
  593.2 94.6 %copy-start.10 = (f32[6,35,64]{1,0,2:T(8,128)S(1)}, f32[6,35,64]{1,0,2:T(8,128)}, u32[]{:S(2)}) copy-start(f32[6,35,64]{1,0,2:T(8,128)} %copy-done.9) | copy-start | bytes 161284
  593.2 94.6 %copy-start.12 = (f32[6,35,64]{1,0,2:T(8,128)S(1)}, f32[6,35,64]{1,0,2:T(8,128)}, u32[]{:S(2)}) copy-start(f32[6,35,64]{1,0,2:T(8,128)} %copy-done.11) | copy-start | bytes 161284
where the time goes:
time: 698 us; the launch traced here: 689 us
  blocking collectives  285 us (41%)
  local copies, waits for them, and re-layouts  183 us (26%)
  other arithmetic  76.3 us (11%)
  matrix products  57 us (8%)
  between operations  52 us (7%)
  starting transfers between devices  35.6 us (5%)
    psum x6, blocking collectives, body(): lax.psum((local_proj, jnp.sum(image * image)), ('dom', 'grp'))  243 us
    gather x7, local copies, waits for them, and re-layouts, facing(): gathered = jnp.take(flat_traces, flat_index.reshape(-1), axis=1)  73.9 us
    psum x1, blocking collectives, body(): lax.psum(jnp.sum(start_vec * start_vec), ('dom', 'grp')) + EPSILON  42.4 us
    dot_general x6, other arithmetic, precondition(): jnp.einsum('iej,je->ie', blocks, flat_vec, preferred_element_type=jnp.flo...  29.1 us
    ppermute x7, starting transfers between devices, with_halo(): lax.ppermute(lax.slice_in_dim(block, block.shape[dim] - width, None, axis...  26.3 us
    reshape x7, local copies, waits for them, and re-layouts, facing(): flat_traces = traces_all.reshape(nvar, nface * npts * span_len)  24.8 us
    reshape x1, local copies, waits for them, and re-layouts, precondition(): blocks = precond.reshape(width, shape_in[2], width)  23.2 us
    select_n x6, other arithmetic, facing(): gathered = jnp.take(flat_traces, flat_index.reshape(-1), axis=1)  21.8 us
  transfers between devices with their start and end apart: 14, of which 0 were waited for; matrix products, arithmetic and copies ran while one was open for 14% of the time, Pallas kernels for 0%

commit v1 on v0

v1 whole, which is shorter than its diff:
```python
import functools

import jax
import jax.numpy as jnp
from jax import lax
from jax.experimental import pallas as pl
from jax.experimental.pallas import tpu as pltpu
from jax.sharding import PartitionSpec as P

ITERS = 6
EPSILON = 1e-06
AXES = ("dom", "grp")
F32 = jnp.float32
BF16 = jnp.bfloat16
VMEM = pl.BlockSpec(memory_space=pltpu.VMEM)
SMEM = pl.BlockSpec(memory_space=pltpu.SMEM)


def ceil_to(n, m):
    return -(-n // m) * m


def iota(shape, dim):
    return lax.broadcasted_iota(jnp.int32, shape, dim)


def split3(x):
    hi = x.astype(BF16).astype(F32)
    rest = x - hi
    mid = rest.astype(BF16).astype(F32)
    return hi, mid, rest - mid


def stack_rhs(parts, axis):
    hi, mid, lo = parts
    return jnp.concatenate([hi, mid, lo, hi, mid, hi], axis=axis).astype(BF16)


def stack_lhs(x):
    hi, mid, lo = split3(x)
    return jnp.concatenate([hi, hi, hi, mid, mid, lo], axis=1).astype(BF16)


def dot(a, b):
    return jnp.dot(a, b, preferred_element_type=F32)


def pad_rows(x, rows):
    return jnp.concatenate([x, jnp.zeros((rows - x.shape[0], x.shape[1]), x.dtype)], axis=0)


class Sizes:
    def __init__(self, nv, nb, ne, nq, peers):
        self.nv, self.nb, self.ne, self.nq, self.peers = nv, nb, ne, nq, peers
        self.nbp = ceil_to(nb, 8)
        self.nqp = ceil_to(nq, 8)
        self.lanes = nv * ne
        self.width = nv * nb
        self.kwidth = ceil_to(self.width, 128)
        self.pair = 2 * ne


def to_wide(read, sz):
    return pad_rows(jnp.concatenate([read(v) for v in range(sz.nv)], axis=1), sz.nbp)


def partial_rows(values, peers):
    lane = iota((1, 128), 1)
    row = jnp.zeros((1, 128), F32)
    for i, val in enumerate(values):
        row = jnp.where(lane == i, val, row)
    return jnp.broadcast_to(row, (peers, 128))


def full_sum(x):
    return jnp.sum(jnp.sum(x, axis=0, keepdims=True), axis=1, keepdims=True)


def total_scalars(red, count):
    row = jnp.sum(red, axis=0, keepdims=True)
    lane = iota((1, 128), 1)
    return [jnp.sum(jnp.where(lane == i, row, 0.0), axis=1, keepdims=True) for i in range(count)]


def init_kernel(
    sz, me_ref, res_ref, state_ref, orders_ref, nbr_ref, face_ref, orient_ref, source_ref, flux_ref, geo_ref,
    stiff_ref, trace_ref, start_ref, state2_ref, mask_ref, hot_ref, coup_ref, sel_ref, own_ref, near_ref, back_ref,
    part_ref,
):
    nv, nb, ne, nq, nbp, nqp = sz.nv, sz.nb, sz.ne, sz.nq, sz.nbp, sz.nqp
    orders = orders_ref[...]
    count = (orders + 1) * (orders + 2) * (orders + 3) // 6
    count = jnp.concatenate([count] * nv, axis=1)
    mask = (iota((nbp, sz.lanes), 0) < count).astype(F32)
    mask_ref[...] = mask
    start = to_wide(lambda v: res_ref[v], sz) * mask
    start_ref[...] = start
    part_ref[...] = partial_rows([full_sum(start * start)], sz.peers)
    state2_ref[...] = to_wide(lambda v: state_ref[v], sz)

    me = me_ref[0]
    nbr = nbr_ref[...]
    rel = jnp.where(nbr >= 0, nbr - me * ne + ne, -4 * ne)
    cols = jnp.concatenate(
        [piece for f in range(4) for piece in (rel[f : f + 1], rel[f : f + 1] + 3 * ne * (rel[f : f + 1] >= 0).astype(jnp.int32))],
        axis=1,
    )
    rows = iota((3 * sz.pair, 4 * sz.pair), 0)
    block = rows // sz.pair
    even = lax.rem(me, 2) == 0
    chip_side = jnp.where(even, 2, 0)
    side = jnp.where(block == 0, 1, jnp.where(block == 1, chip_side, 2 - chip_side))
    inner = rows - block * sz.pair
    parity = (inner >= ne).astype(jnp.int32)
    code = side * ne + inner - parity * ne + 3 * ne * parity
    hot_ref[...] = (code == cols).astype(F32).astype(BF16)

    face = face_ref[...]
    orient = orient_ref[...]
    flip = (orient >= 3).astype(jnp.int32)
    choice = flip * 4 + face
    turn = orient - 3 * flip
    sel_ref[...] = jnp.concatenate([jnp.concatenate([choice, turn], axis=0)] * nv, axis=1)

    for k in range(3):
        pieces = []
        for w in range(nv):
            tile = jnp.zeros((nv, ne), F32)
            for d in range(3):
                tile = tile + geo_ref[d, k : k + 1, :] * flux_ref[d, w]
            pieces.append(tile if w == 0 else jnp.concatenate([tile[w:], tile[:w]], axis=0))
        coup_ref[k] = jnp.concatenate(pieces, axis=1)
    pieces = []
    for w in range(nv):
        tile = source_ref[w]
        pieces.append(tile if w == 0 else jnp.concatenate([tile[w:], tile[:w]], axis=0))
    coup_ref[3] = jnp.concatenate(pieces, axis=1)

    def pad2(x, rows):
        x = jnp.concatenate([x, jnp.zeros((x.shape[0], nbp - x.shape[1]), F32)], axis=1)
        return pad_rows(x, rows)

    traces = [trace_ref[f] for f in range(4)]
    plain = [pad2(t, nqp) for t in traces]
    flipped = [
        pad2(jnp.concatenate([t[q : q + 1] for q in reversed(range(nq))], axis=0), nqp) for t in traces
    ]
    volume = [pad2(stiff_ref[d], nbp) for d in range(3)]
    own_ref[...] = stack_lhs(jnp.concatenate(plain + volume, axis=0))
    near_ref[...] = stack_lhs(jnp.concatenate(plain + flipped, axis=0))
    back_ref[...] = stack_lhs(jnp.concatenate(plain, axis=0).T)


def relay_kernel(sz, p_ref, out_ref):
    width, kwidth, ne = sz.width, sz.kwidth, sz.ne
    total = width * ne
    zeros = jnp.zeros((width, kwidth - width), F32)
    for e in range(ne):
        low = e * width // 128 * 128
        high = min(ceil_to((e + 1) * width, 128), total)
        shift = e * width - low
        window = p_ref[:, low:high].astype(F32)
        piece = window[:, shift : shift + width]
        out_ref[e] = jnp.concatenate([piece, zeros], axis=1).astype(BF16)


def apply_blocks(sz, vec, mask, blocks_ref):
    nb, ne, nv = sz.nb, sz.ne, sz.nv
    tall = jnp.concatenate([vec[:nb, v * ne : (v + 1) * ne] for v in range(nv)], axis=0)
    tall = pad_rows(tall, sz.kwidth)
    lane = iota((1, ne), 1)

    def step(e, acc):
        picked = jnp.where(lane == e, tall, 0.0).astype(BF16)
        return acc + dot(blocks_ref[e], picked)

    acc = lax.fori_loop(0, ne, step, jnp.zeros((sz.width, ne), F32), unroll=4)
    wide = jnp.concatenate([acc[v * nb : (v + 1) * nb] for v in range(nv)], axis=1)
    return pad_rows(wide, sz.nbp) * mask


def precond_kernel(sz, step, *refs):
    red_ref, vec_ref, mask_ref, blocks_ref = refs[:4]
    mask = mask_ref[...]
    vec = vec_ref[...]
    if step == 0:
        state_ref, z_ref, v_ref, h_ref = refs[4:]
        norm = jnp.sqrt(total_scalars(red_ref[...], 1)[0] + EPSILON)
        values = [norm]
    else:
        basis = refs[4 : 4 + step]
        z_ref, v_ref, h_ref = refs[4 + step :]
        scalars = total_scalars(red_ref[...], step + 1)
        proj, square = scalars[:step], scalars[step]
        for h, b in zip(proj, basis):
            vec = vec - h * b[...]
            square = square - h * h
        norm = jnp.sqrt(square + EPSILON)
        values = proj + [norm]
    new = vec / norm
    v_ref[...] = new
    h_ref[...] = partial_rows(values, 1)
    search = apply_blocks(sz, new, mask, blocks_ref)
    if step == 0:
        z_ref[: sz.nbp] = search
        z_ref[sz.nbp :] = state_ref[...]
    else:
        z_ref[...] = search


def roll_blocks(x, blocks, ne):
    shift = blocks * ne
    if shift == 0:
        return x
    return jnp.concatenate([x[:, shift:], x[:, :shift]], axis=1)


def local_kernel(sz, z_ref, own_ref, coup_ref, vol_ref, tr_ref):
    search = z_ref[: sz.nbp]
    out = dot(own_ref[...], stack_rhs(split3(search), 0))
    faces = 4 * sz.nqp
    tr_ref[...] = out[:faces]
    acc = jnp.zeros((sz.nbp, sz.lanes), F32)
    for d in range(4):
        moved = search if d == 3 else out[faces + d * sz.nbp : faces + (d + 1) * sz.nbp]
        for s in range(sz.nv):
            acc = acc + coup_ref[d, s : s + 1, :] * roll_blocks(moved, s, sz.ne)
    vol_ref[...] = acc


def neighbour_traces(sz, own, chip, far, hot_ref, near_ref, sel_ref):
    nbp, nqp, pair = sz.nbp, sz.nqp, sz.pair
    parts = [split3(x) for x in (own, chip, far)]
    pairs = sz.lanes // pair
    lhs = jnp.concatenate(
        [
            jnp.concatenate([parts[side][n][:, p * pair : (p + 1) * pair] for side in range(3)], axis=1)
            for n in range(3)
            for p in range(pairs)
        ],
        axis=0,
    ).astype(BF16)
    got = dot(lhs, hot_ref[...])
    result = []
    for f in range(4):
        picked = [
            jnp.concatenate(
                [
                    got[(n * pairs + p) * nbp : (n * pairs + p + 1) * nbp, f * pair : (f + 1) * pair]
                    for p in range(pairs)
                ],
                axis=1,
            )
            for n in range(3)
        ]
        every = dot(near_ref[...], stack_rhs(picked, 0))
        choice = sel_ref[f : f + 1, :]
        turn = sel_ref[4 + f : 5 + f, :]
        tr = every[:nqp]
        for g in range(1, 8):
            tr = jnp.where(choice == g, every[g * nqp : (g + 1) * nqp], tr)
        nq, third = sz.nq, sz.nq // 3
        fill = tr[nq:]
        once = jnp.concatenate([tr[third:nq], tr[:third], fill], axis=0)
        twice = jnp.concatenate([tr[2 * third : nq], tr[: 2 * third], fill], axis=0)
        result.append(jnp.where(turn == 0, tr, jnp.where(turn == 1, once, twice)))
    return jnp.concatenate(result, axis=0)


def gain_kernel(sz, z_ref, chip_ref, far_ref, hot_ref, near_ref, own_ref, sel_ref, gain_ref):
    nbp = sz.nbp
    state = z_ref[nbp:]
    tr = dot(own_ref[: 4 * sz.nqp], stack_rhs(split3(state), 0))
    other = neighbour_traces(sz, state, chip_ref[nbp:], far_ref[nbp:], hot_ref, near_ref, sel_ref)
    gain_ref[...] = 1.0 + 0.5 * jnp.abs(tr + other)


def image_kernel(sz, step, *refs):
    z_ref, chip_ref, far_ref, hot_ref, near_ref, sel_ref, gain_ref, back_ref, vol_ref, tr_ref, mask_ref = refs[:11]
    basis = refs[11 : 12 + step]
    w_ref, part_ref = refs[12 + step :]
    nbp = sz.nbp
    other = neighbour_traces(sz, z_ref[:nbp], chip_ref[:nbp], far_ref[:nbp], hot_ref, near_ref, sel_ref)
    flux = gain_ref[...] * (tr_ref[...] - other)
    face = dot(back_ref[...], stack_rhs(split3(flux), 0))
    image = (vol_ref[...] + face) * mask_ref[...]
    w_ref[...] = image
    values = [full_sum(b[...] * image) for b in basis] + [full_sum(image * image)]
    part_ref[...] = partial_rows(values, sz.peers)


def finish_kernel(sz, *refs):
    red_ref, heads, searches = refs[0], refs[1 : 1 + ITERS], refs[1 + ITERS : 1 + 2 * ITERS]
    out_ref, hess_ref = refs[1 + 2 * ITERS :]
    lane = iota((1, 128), 1)

    def entry(row, i):
        return jnp.sum(jnp.where(lane == i, row, 0.0), axis=1, keepdims=True)

    start_value = entry(heads[0][...], 0)
    zero = jnp.zeros((1, 1), F32)
    upper = [[zero] * ITERS for _ in range(ITERS + 1)]
    for k in range(ITERS - 1):
        row = heads[k + 1][...]
        for i in range(k + 2):
            upper[i][k] = entry(row, i)
    scalars = total_scalars(red_ref[...], ITERS + 1)
    square = scalars[ITERS]
    for i in range(ITERS):
        upper[i][ITERS - 1] = scalars[i]
        square = square - scalars[i] * scalars[i]
    upper[ITERS][ITERS - 1] = jnp.sqrt(square + EPSILON)
    shape = hess_ref.shape
    row_id, col_id = iota(shape, 0), iota(shape, 1)
    hess = jnp.zeros(shape, F32)
    for i in range(ITERS + 1):
        for k in range(max(i - 1, 0), ITERS):
            hess = jnp.where((row_id == i) & (col_id == k), upper[i][k], hess)
    hess_ref[...] = hess
    right = [start_value] + [zero] * ITERS
    for k in range(ITERS):
        lead, below = upper[k][k], upper[k + 1][k]
        radius = jnp.sqrt(lead * lead + below * below)
        cosine, sine = lead / radius, below / radius
        for j in range(k, ITERS):
            top, low = upper[k][j], upper[k + 1][j]
            upper[k][j] = cosine * top + sine * low
            upper[k + 1][j] = cosine * low - sine * top
        top, low = right[k], right[k + 1]
        right[k] = cosine * top + sine * low
        right[k + 1] = cosine * low - sine * top
    coeffs = [None] * ITERS
    for k in reversed(range(ITERS)):
        acc = right[k]
        for j in range(k + 1, ITERS):
            acc = acc - upper[k][j] * coeffs[j]
        coeffs[k] = acc / upper[k][k]
    total = coeffs[0] * searches[0][: sz.nbp]
    for k in range(1, ITERS):
        total = total + coeffs[k] * searches[k][: sz.nbp]
    for v in range(sz.nv):
        out_ref[v] = total[: sz.nb, v * sz.ne : (v + 1) * sz.ne]


def call(kernel, name, out_shape, *args, smem_first=False, limit=None):
    specs = [VMEM] * len(args)
    if smem_first:
        specs[0] = SMEM
    return pl.pallas_call(
        kernel,
        name=name,
        out_shape=out_shape,
        in_specs=specs,
        out_specs=jax.tree.map(lambda _: VMEM, out_shape),
        compiler_params=pltpu.CompilerParams(vmem_limit_bytes=limit or 32 * 2**20),
    )(*args)


def shape(*dims, dtype=F32):
    return jax.ShapeDtypeStruct(dims, dtype)


def body(
    peers, state_coeffs, residual_in, orders, neighbours, neighbour_face, orientation, precond, source,
    flux_jacobian, geometry, stiffness, trace_matrix,
):
    nv, nb, ne = state_coeffs.shape
    sz = Sizes(nv, nb, ne, trace_matrix.shape[1], peers)
    lanes, nbp, nqp = sz.lanes, sz.nbp, sz.nqp
    me = lax.axis_index(AXES).astype(jnp.int32).reshape(1)
    wide = shape(nbp, lanes)
    parts = shape(peers, 128)
    start, state, mask, hot, coup, sel, own, near, back, part = call(
        functools.partial(init_kernel, sz),
        "init",
        (
            wide, wide, wide,
            shape(3 * sz.pair, 4 * sz.pair, dtype=BF16),
            shape(4, nv, lanes),
            shape(8, lanes, dtype=jnp.int32),
            shape(4 * nqp + 3 * nbp, 6 * nbp, dtype=BF16),
            shape(8 * nqp, 6 * nbp, dtype=BF16),
            shape(nbp, 24 * nqp, dtype=BF16),
            parts,
        ),
        me, residual_in, state_coeffs, orders.reshape(1, ne), neighbours, neighbour_face, orientation, source,
        flux_jacobian, geometry, stiffness, trace_matrix,
        smem_first=True,
    )
    blocks = call(
        functools.partial(relay_kernel, sz), "relay", shape(ne, sz.width, sz.kwidth, dtype=BF16), precond
    )

    def exchange(rows):
        return lax.all_to_all(rows, AXES, 0, 0, tiled=True)

    on_chip = [(i, i ^ 1) for i in range(peers)]
    odd = range(1, peers - 1, 2)
    off_chip = [(i, i + 1) for i in odd] + [(i + 1, i) for i in odd]

    heads, searches, basis = [], [], []
    vec, gain = start, None
    for k in range(ITERS):
        red = exchange(part)
        z_shape = shape(2 * nbp, lanes) if k == 0 else wide
        extra = [state] if k == 0 else basis
        search, new, head = call(
            functools.partial(precond_kernel, sz, k), f"precond{k}", (z_shape, wide, shape(1, 128)),
            red, vec, mask, blocks, *extra,
        )
        basis = basis + [new]
        heads.append(head)
        searches.append(search)
        far = lax.ppermute(search, AXES, off_chip)
        chip = lax.ppermute(search, AXES, on_chip)
        vol, tr = call(
            functools.partial(local_kernel, sz), "local", (wide, shape(4 * nqp, lanes)), search, own, coup
        )
        if k == 0:
            gain = call(
                functools.partial(gain_kernel, sz), "gain", shape(4 * nqp, lanes),
                search, chip, far, hot, near, own, sel,
            )
        vec, part = call(
            functools.partial(image_kernel, sz, k), f"image{k}", (wide, parts),
            search, chip, far, hot, near, sel, gain, back, vol, tr, mask, *basis,
        )
    red = exchange(part)
    return call(
        functools.partial(finish_kernel, sz), "finish", (shape(nv, nb, ne), shape(ITERS + 1, ITERS)),
        red, *heads, *searches,
    )


def solution(mesh):
    placed = (
        P(None, None, AXES),
        P(None, None, AXES),
        P(AXES),
        P(None, AXES),
        P(None, AXES),
        P(None, AXES),
        P(None, AXES),
        P(None, None, AXES),
        P(None, None, None, AXES),
        P(None, None, AXES),
        P(),
        P(),
    )
    peers = 1
    for axis in AXES:
        peers *= mesh.shape[axis]
    return jax.shard_map(
        functools.partial(body, peers),
        mesh=mesh,
        in_specs=placed,
        out_specs=(P(None, None, AXES), P()),
        check_vma=False,
    )
```

time: 698 us -> 162 us (0.23); the launches traced: 689 us -> 161 us
  blocking collectives: 285 us -> 74 us
  local copies, waits for them, and re-layouts: 183 us -> 16.9 us
  other arithmetic: 76.3 us -> 0 us
  matrix products: 57 us -> 0 us
  between operations: 52 us -> 0.87 us
  Pallas kernels: 0 us -> 41.6 us
  starting transfers between devices: 35.6 us -> 24.3 us
    psum x7 -> x0, blocking collectives: 285 us -> none  [the longest x6 243 us: body(): lax.psum((local_proj, jnp.sum(image * image)), ('dom', 'grp'))]
    all_to_all x0 -> x6, blocking collectives: none -> 74 us  [exchange(): return lax.all_to_all(rows, AXES, 0, 0, tiled=True)]
    gather x7 -> x0, local copies, waits for them, and re-layouts: 73.9 us -> none  [facing(): gathered = jnp.take(flat_traces, flat_index.reshape(-1), axis=1)]
    reshape x33 -> x0, local copies, waits for them, and re-layouts: 60.4 us -> none  [the longest x7 24.8 us: facing(): flat_traces = traces_all.reshape(nvar, nface * npts * span_len)]
    dot_general x41 -> x0, matrix products: 57 us -> none  [the longest x6 13.3 us: operate(): source_term = jnp.einsum('wve,vbe->wbe', source, field_vec, precision=high)]
    pallas_call x0 -> x22, Pallas kernels: none -> 41.6 us  [call(): pl.pallas_call(kernel, name=name, out_shape=out_shape, in_specs=specs, ou...]
    dot_general x7 -> x0, other arithmetic: 29.7 us -> none  [the longest x6 29.1 us: precondition(): jnp.einsum('iej,je->ie', blocks, flat_vec, preferred_element_type=jnp.flo...]
    select_n x7 -> x0, other arithmetic: 22.5 us -> none  [the longest x6 21.8 us: facing(): gathered = jnp.take(flat_traces, flat_index.reshape(-1), axis=1)]
  transfers between devices with their start and end apart: 14 -> 13, of which waited for: 0 -> 6; matrix products, arithmetic and copies ran while one was open for 14% -> 0% of each run, Pallas kernels for 0% -> 3%
where the time goes in v1:
time: 162 us; the launch traced here: 161 us
  blocking collectives  74 us (46%)
  Pallas kernels  41.6 us (26%)
  starting transfers between devices  24.3 us (15%)
  local copies, waits for them, and re-layouts  16.9 us (10%)
  waiting for transfers between devices  3.29 us (2%)
    all_to_all x6, blocking collectives, exchange(): return lax.all_to_all(rows, AXES, 0, 0, tiled=True)  74 us
    pallas_call x22, Pallas kernels, call(): pl.pallas_call(kernel, name=name, out_shape=out_shape, in_specs=specs, ou...  41.6 us
    unnamed x29, local copies, waits for them, and re-layouts  16.9 us
    ppermute x6, starting transfers between devices, body(): chip = lax.ppermute(search, AXES, on_chip)  13 us
    all_to_all x1, starting transfers between devices, exchange(): return lax.all_to_all(rows, AXES, 0, 0, tiled=True)  7.33 us
    ppermute x6, starting transfers between devices, body(): far = lax.ppermute(search, AXES, off_chip)  3.99 us
    ppermute x6, waiting for transfers between devices, body(): chip = lax.ppermute(search, AXES, on_chip)  3.27 us
  transfers between devices with their start and end apart: 13, of which 6 were waited for; matrix products, arithmetic and copies ran while one was open for 0% of the time, Pallas kernels for 3%

profile of v1, /device:TPU:0, one launch (start us, length us, event | category | flops | bytes accessed | tf_op | source)
XLA Modules:
  0.0 160.9 jit_solution(2300468810148101126)
XLA Ops:
  0.6 0.8 copy.15.trace_ref
  1.4 0.9 copy-done.4
  2.3 0.9 copy-done.5
  3.2 0.9 copy-done.6
  4.1 0.8 copy-done.7
  4.9 0.7 copy-done.8
  5.7 0.7 copy-done.9
  6.3 0.7 copy-done.10
  7.0 0.7 copy-done.11
  7.7 0.7 copy-done.12
  8.4 0.7 copy-done.13
  9.0 0.9 init.1
  10.0 7.3 %all-to-all-start = ((f32[32,1,128]{2,1,0:T(1,128)}), f32[32,1,128]{2,1,0:T(1,128)S(1)}, u32[]{:S(2)}, u32[]{:S(2)}) async-start(f32[32,1,128]{2,1,0:T(1,128)} %bitcast.3), calls=%async_computation | async-start | bytes 32768 | tf_op jit(solution)/shard_map/all_to_all | solution.py:395
  17.3 0.0 copy-start.3
  17.3 2.6 %copy-done.3 = bf16[210,13440]{1,0:T(8,128)(2,1)S(1)} copy-done((bf16[210,13440]{1,0:T(8,128)(2,1)S(1)}, bf16[210,13440]{1,0:T(8,128)(2,1)}, u32[]{:S(2)}) %copy-start.3) | copy-done | bytes 5644824
  20.0 2.4 %relay.1.refs_3_ = bf16[64,210,256]{2,1,0:T(8,128)(2,1)S(1)} custom-call(bf16[210,13440]{1,0:T(8,128)(2,1)S(1)} %copy-done.3), custom_call_target="tpu_custom_call" | custom-call | tf_op jit(solution)/shard_map/relay/pallas_call | solution.py:349
  22.4 2.8 %copy-done = bf16[64,210,256]{2,1,0:T(8,128)(2,1)} copy-done((bf16[64,210,256]{2,1,0:T(8,128)(2,1)}, bf16[64,210,256]{2,1,0:T(8,128)(2,1)S(1)}, u32[]{:S(2)}) %copy-start) | copy-done | bytes 6881304
  25.3 3.0 %copy-done.1 = bf16[64,210,256]{2,1,0:T(8,128)(2,1)S(1)} copy-done((bf16[64,210,256]{2,1,0:T(8,128)(2,1)S(1)}, bf16[64,210,256]{2,1,0:T(8,128)(2,1)}, u32[]{:S(2)}) %copy-start.1) | copy-done | bytes 6881304
  28.3 4.7 %precond0.1 = (f32[80,384]{1,0:T(8,128)S(1)}, f32[40,384]{1,0:T(8,128)S(1)}, f32[1,128]{1,0:T(1,128)S(1)}) custom-call(f32[32,128]{1,0:T(8,128)S(1)} %bitcast.30, f32[40,384]{1,0:T(8,128)S(1)} %get-tuple-element.54.refs_1_, f32[40,384]{1,0:T(8,128)S(1)} %get-tuple-element.55.refs_2_.refs_10_, bf16[64,210,256]{2,1,0:T(8,128)(2,1)S(1)} %copy-done.1, ...), custom_call_target="tpu_custom_call" | custom-call | tf_op jit(solution)/shard_map/precond0/pallas_call | solution.py:349
  33.0 0.7 collective-permute-start.1
  33.7 3.2 %collective-permute-start = (f32[80,384]{1,0:T(8,128)S(1)}, f32[80,384]{1,0:T(8,128)S(1)}, u32[]{:S(2)}, u32[]{:S(2)}) collective-permute-start(f32[80,384]{1,0:T(8,128)S(1)} %get-tuple-element.57.z_ref.refs_0_.refs_7_), channel_id=1, source_target_pairs={{0,1},{1,0},{2,3},{3,2},{4,5},{5,4},{6,7},{7,6},{8,9},{9,8},{10,11... | collective-permute-start | bytes 368648 | tf_op jit(solution)/shard_map/ppermute | solution.py:415
  36.9 0.3 local.6
  37.2 0.0 collective-permute-done.1.far_ref.refs_2_
  37.2 0.6 collective-permute-done.chip_ref.refs_1_
  37.9 0.7 gain.1.refs_6_
  38.5 0.9 image0.1
  39.5 15.2 %all_to_all.77 = f32[32,1,128]{2,1,0:T(1,128)S(1)} all-to-all(f32[32,1,128]{2,1,0:T(1,128)S(1)} %bitcast.38), channel_id=1, replica_groups=mesh['dom'=8,'grp'=4] {'dom','grp'}, dimensions={0} | all-to-all | bytes 32768 | tf_op jit(solution)/shard_map/all_to_all | solution.py:395
  54.7 4.7 %precond1.1 = (f32[40,384]{1,0:T(8,128)S(1)}, f32[40,384]{1,0:T(8,128)S(1)}, f32[1,128]{1,0:T(1,128)S(1)}) custom-call(f32[32,128]{1,0:T(8,128)S(1)} %bitcast.32, f32[40,384]{1,0:T(8,128)S(1)} %get-tuple-element.68.refs_1_, f32[40,384]{1,0:T(8,128)S(1)} %get-tuple-element.55.refs_2_.refs_10_, bf16[64,210,256]{2,1,0:T(8,128)(2,1)S(1)} %copy-done.2, ...), custom_call_target="tpu_custom_call" | custom-call | tf_op jit(solution)/shard_map/precond1/pallas_call | solution.py:349
  59.4 0.7 collective-permute-start.3
  60.1 2.0 %collective-permute-start.2 = (f32[40,384]{1,0:T(8,128)S(1)}, f32[40,384]{1,0:T(8,128)S(1)}, u32[]{:S(2)}, u32[]{:S(2)}) collective-permute-start(f32[40,384]{1,0:T(8,128)S(1)} %get-tuple-element.69.z_ref.refs_0_.refs_8_), channel_id=1, source_target_pairs={{0,1},{1,0},{2,3},{3,2},{4,5},{5,4},{6,7},{7,6},{8,9},{9,8},{10,11... | collective-permute-start | bytes 184328 | tf_op jit(solution)/shard_map/ppermute | solution.py:415
  62.0 0.3 local.7
  62.4 0.0 collective-permute-done.3.refs_2_
  62.4 0.5 collective-permute-done.2.refs_1_
  62.9 0.9 image1.1
  63.8 11.8 %all_to_all.78 = f32[32,1,128]{2,1,0:T(1,128)S(1)} all-to-all(f32[32,1,128]{2,1,0:T(1,128)S(1)} %bitcast.39), channel_id=1, replica_groups=mesh['dom'=8,'grp'=4] {'dom','grp'}, dimensions={0} | all-to-all | bytes 32768 | tf_op jit(solution)/shard_map/all_to_all | solution.py:395
  75.6 4.7 %precond2.1 = (f32[40,384]{1,0:T(8,128)S(1)}, f32[40,384]{1,0:T(8,128)S(1)}, f32[1,128]{1,0:T(1,128)S(1)}) custom-call(f32[32,128]{1,0:T(8,128)S(1)} %bitcast.33, f32[40,384]{1,0:T(8,128)S(1)} %get-tuple-element.74.refs_1_, f32[40,384]{1,0:T(8,128)S(1)} %get-tuple-element.55.refs_2_.refs_10_, bf16[64,210,256]{2,1,0:T(8,128)(2,1)S(1)} %copy-done.2, ...), custom_call_target="tpu_custom_call" | custom-call | tf_op jit(solution)/shard_map/precond2/pallas_call | solution.py:349
  80.3 0.7 collective-permute-start.5
  81.0 2.0 %collective-permute-start.4 = (f32[40,384]{1,0:T(8,128)S(1)}, f32[40,384]{1,0:T(8,128)S(1)}, u32[]{:S(2)}, u32[]{:S(2)}) collective-permute-start(f32[40,384]{1,0:T(8,128)S(1)} %get-tuple-element.75.z_ref.refs_0_.refs_9_), channel_id=1, source_target_pairs={{0,1},{1,0},{2,3},{3,2},{4,5},{5,4},{6,7},{7,6},{8,9},{9,8},{10,11... | collective-permute-start | bytes 184328 | tf_op jit(solution)/shard_map/ppermute | solution.py:415
  83.0 0.3 local.8
  83.3 0.5 collective-permute-done.4.refs_1_
  83.9 0.9 image2.1
  84.8 11.8 %all_to_all.79 = f32[32,1,128]{2,1,0:T(1,128)S(1)} all-to-all(f32[32,1,128]{2,1,0:T(1,128)S(1)} %bitcast.40), channel_id=1, replica_groups=mesh['dom'=8,'grp'=4] {'dom','grp'}, dimensions={0} | all-to-all | bytes 32768 | tf_op jit(solution)/shard_map/all_to_all | solution.py:395
  96.6 4.7 %precond3.1 = (f32[40,384]{1,0:T(8,128)S(1)}, f32[40,384]{1,0:T(8,128)S(1)}, f32[1,128]{1,0:T(1,128)S(1)}) custom-call(f32[32,128]{1,0:T(8,128)S(1)} %bitcast.34, f32[40,384]{1,0:T(8,128)S(1)} %get-tuple-element.80.refs_1_, f32[40,384]{1,0:T(8,128)S(1)} %get-tuple-element.55.refs_2_.refs_10_, bf16[64,210,256]{2,1,0:T(8,128)(2,1)S(1)} %copy-done.2, ...), custom_call_target="tpu_custom_call" | custom-call | tf_op jit(solution)/shard_map/precond3/pallas_call | solution.py:349
  101.3 0.7 collective-permute-start.7
  101.9 2.0 %collective-permute-start.6 = (f32[40,384]{1,0:T(8,128)S(1)}, f32[40,384]{1,0:T(8,128)S(1)}, u32[]{:S(2)}, u32[]{:S(2)}) collective-permute-start(f32[40,384]{1,0:T(8,128)S(1)} %get-tuple-element.81.z_ref.refs_0_.refs_10_), channel_id=1, source_target_pairs={{0,1},{1,0},{2,3},{3,2},{4,5},{5,4},{6,7},{7,6},{8,9},{9,8},{10,11... | collective-permute-start | bytes 184328 | tf_op jit(solution)/shard_map/ppermute | solution.py:415
  103.9 0.3 local.9
  104.3 0.5 collective-permute-done.6.refs_1_
  104.8 0.9 image3.1
  105.7 11.8 %all_to_all.80 = f32[32,1,128]{2,1,0:T(1,128)S(1)} all-to-all(f32[32,1,128]{2,1,0:T(1,128)S(1)} %bitcast.41), channel_id=1, replica_groups=mesh['dom'=8,'grp'=4] {'dom','grp'}, dimensions={0} | all-to-all | bytes 32768 | tf_op jit(solution)/shard_map/all_to_all | solution.py:395
  117.5 4.7 %precond4.1 = (f32[40,384]{1,0:T(8,128)S(1)}, f32[40,384]{1,0:T(8,128)S(1)}, f32[1,128]{1,0:T(1,128)S(1)}) custom-call(f32[32,128]{1,0:T(8,128)S(1)} %bitcast.35, f32[40,384]{1,0:T(8,128)S(1)} %get-tuple-element.86.refs_1_, f32[40,384]{1,0:T(8,128)S(1)} %get-tuple-element.55.refs_2_.refs_10_, bf16[64,210,256]{2,1,0:T(8,128)(2,1)S(1)} %copy-done.2, ...), custom_call_target="tpu_custom_call" | custom-call | tf_op jit(solution)/shard_map/precond4/pallas_call | solution.py:349
  122.2 0.7 collective-permute-start.9
  122.9 2.0 %collective-permute-start.8 = (f32[40,384]{1,0:T(8,128)S(1)}, f32[40,384]{1,0:T(8,128)S(1)}, u32[]{:S(2)}, u32[]{:S(2)}) collective-permute-start(f32[40,384]{1,0:T(8,128)S(1)} %get-tuple-element.87.z_ref.refs_0_.refs_11_), channel_id=1, source_target_pairs={{0,1},{1,0},{2,3},{3,2},{4,5},{5,4},{6,7},{7,6},{8,9},{9,8},{10,11... | collective-permute-start | bytes 184328 | tf_op jit(solution)/shard_map/ppermute | solution.py:415
  124.8 0.3 local.10
  125.2 0.5 collective-permute-done.8.refs_1_
  125.7 0.9 image4.1
  126.7 11.8 %all_to_all.81 = f32[32,1,128]{2,1,0:T(1,128)S(1)} all-to-all(f32[32,1,128]{2,1,0:T(1,128)S(1)} %bitcast.42), channel_id=1, replica_groups=mesh['dom'=8,'grp'=4] {'dom','grp'}, dimensions={0} | all-to-all | bytes 32768 | tf_op jit(solution)/shard_map/all_to_all | solution.py:395
  138.4 4.7 %precond5.1 = (f32[40,384]{1,0:T(8,128)S(1)}, f32[40,384]{1,0:T(8,128)S(1)}, f32[1,128]{1,0:T(1,128)S(1)}) custom-call(f32[32,128]{1,0:T(8,128)S(1)} %bitcast.31, f32[40,384]{1,0:T(8,128)S(1)} %get-tuple-element.92.refs_1_, f32[40,384]{1,0:T(8,128)S(1)} %get-tuple-element.55.refs_2_.refs_10_, bf16[64,210,256]{2,1,0:T(8,128)(2,1)S(1)} %copy-done.2, ...), custom_call_target="tpu_custom_call" | custom-call | tf_op jit(solution)/shard_map/precond5/pallas_call | solution.py:349
  143.2 0.7 collective-permute-start.11
  143.8 2.0 %collective-permute-start.10 = (f32[40,384]{1,0:T(8,128)S(1)}, f32[40,384]{1,0:T(8,128)S(1)}, u32[]{:S(2)}, u32[]{:S(2)}) collective-permute-start(f32[40,384]{1,0:T(8,128)S(1)} %get-tuple-element.93.z_ref.refs_0_.refs_12_), channel_id=1, source_target_pairs={{0,1},{1,0},{2,3},{3,2},{4,5},{5,4},{6,7},{7,6},{8,9},{9,8},{10,11... | collective-permute-start | bytes 184328 | tf_op jit(solution)/shard_map/ppermute | solution.py:415
  145.8 0.3 local.11
  146.2 0.5 collective-permute-done.10.refs_1_
  146.7 1.5 image5.1
  148.2 11.7 %all_to_all.82 = f32[32,1,128]{2,1,0:T(1,128)S(1)} all-to-all(f32[32,1,128]{2,1,0:T(1,128)S(1)} %bitcast.37), channel_id=1, replica_groups=mesh['dom'=8,'grp'=4] {'dom','grp'}, dimensions={0} | all-to-all | bytes 32768 | tf_op jit(solution)/shard_map/all_to_all | solution.py:395
  159.9 1.0 finish.1
  (19 shorter events, 0.0 us)
Async XLA Ops:
  1.4 0.9 copy-start.4
  2.3 0.9 copy-start.5
  3.2 0.9 copy-start.6
  4.1 0.8 copy-start.7
  4.9 0.7 copy-start.8
  5.6 0.7 copy-start.9
  6.3 0.7 copy-start.10
  7.0 0.7 copy-start.11
  7.7 0.7 copy-start.12
  8.4 0.7 copy-start.13
  10.0 15.3 %all-to-all-start = ((f32[32,1,128]{2,1,0:T(1,128)}), f32[32,1,128]{2,1,0:T(1,128)S(1)}, u32[]{:S(2)}, u32[]{:S(2)}) async-start(f32[32,1,128]{2,1,0:T(1,128)} %bitcast.3), calls=%async_computation | async-start | bytes 32768 | tf_op jit(solution)/shard_map/all_to_all | solution.py:395
  17.3 2.6 %copy-start.3 = (bf16[210,13440]{1,0:T(8,128)(2,1)S(1)}, bf16[210,13440]{1,0:T(8,128)(2,1)}, u32[]{:S(2)}) copy-start(bf16[210,13440]{1,0:T(8,128)(2,1)} %p_ref.1) | copy-start | bytes 16934404
  22.4 2.8 %copy-start = (bf16[64,210,256]{2,1,0:T(8,128)(2,1)}, bf16[64,210,256]{2,1,0:T(8,128)(2,1)S(1)}, u32[]{:S(2)}) copy-start(bf16[64,210,256]{2,1,0:T(8,128)(2,1)S(1)} %relay.1.refs_3_) | copy-start | bytes 20643844
  25.3 3.0 %copy-start.1 = (bf16[64,210,256]{2,1,0:T(8,128)(2,1)S(1)}, bf16[64,210,256]{2,1,0:T(8,128)(2,1)}, u32[]{:S(2)}) copy-start(bf16[64,210,256]{2,1,0:T(8,128)(2,1)} %copy-done) | copy-start | bytes 20643844
  28.3 26.4 %copy-start.2 = (bf16[64,210,256]{2,1,0:T(8,128)(2,1)S(1)}, bf16[64,210,256]{2,1,0:T(8,128)(2,1)}, u32[]{:S(2)}) copy-start(bf16[64,210,256]{2,1,0:T(8,128)(2,1)} %copy-done) | copy-start | bytes 20643844
  33.0 4.2 %collective-permute-start.1 = (f32[80,384]{1,0:T(8,128)S(1)}, f32[80,384]{1,0:T(8,128)S(1)}, u32[]{:S(2)}, u32[]{:S(2)}) collective-permute-start(f32[80,384]{1,0:T(8,128)S(1)} %get-tuple-element.57.z_ref.refs_0_.refs_7_), channel_id=1, source_target_pairs={{1,2},{3,4},{5,6},{7,8},{9,10},{11,12},{13,14},{15,16},{17,18},{19... | collective-permute-start | bytes 368648 | tf_op jit(solution)/shard_map/ppermute | solution.py:414
  33.7 4.2 %collective-permute-start = (f32[80,384]{1,0:T(8,128)S(1)}, f32[80,384]{1,0:T(8,128)S(1)}, u32[]{:S(2)}, u32[]{:S(2)}) collective-permute-start(f32[80,384]{1,0:T(8,128)S(1)} %get-tuple-element.57.z_ref.refs_0_.refs_7_), channel_id=1, source_target_pairs={{0,1},{1,0},{2,3},{3,2},{4,5},{5,4},{6,7},{7,6},{8,9},{9,8},{10,11... | collective-permute-start | bytes 368648 | tf_op jit(solution)/shard_map/ppermute | solution.py:415
  59.4 3.0 %collective-permute-start.3 = (f32[40,384]{1,0:T(8,128)S(1)}, f32[40,384]{1,0:T(8,128)S(1)}, u32[]{:S(2)}, u32[]{:S(2)}) collective-permute-start(f32[40,384]{1,0:T(8,128)S(1)} %get-tuple-element.69.z_ref.refs_0_.refs_8_), channel_id=1, source_target_pairs={{1,2},{3,4},{5,6},{7,8},{9,10},{11,12},{13,14},{15,16},{17,18},{19... | collective-permute-start | bytes 184328 | tf_op jit(solution)/shard_map/ppermute | solution.py:414
  60.1 2.9 %collective-permute-start.2 = (f32[40,384]{1,0:T(8,128)S(1)}, f32[40,384]{1,0:T(8,128)S(1)}, u32[]{:S(2)}, u32[]{:S(2)}) collective-permute-start(f32[40,384]{1,0:T(8,128)S(1)} %get-tuple-element.69.z_ref.refs_0_.refs_8_), channel_id=1, source_target_pairs={{0,1},{1,0},{2,3},{3,2},{4,5},{5,4},{6,7},{7,6},{8,9},{9,8},{10,11... | collective-permute-start | bytes 184328 | tf_op jit(solution)/shard_map/ppermute | solution.py:415
  80.3 3.0 %collective-permute-start.5 = (f32[40,384]{1,0:T(8,128)S(1)}, f32[40,384]{1,0:T(8,128)S(1)}, u32[]{:S(2)}, u32[]{:S(2)}) collective-permute-start(f32[40,384]{1,0:T(8,128)S(1)} %get-tuple-element.75.z_ref.refs_0_.refs_9_), channel_id=1, source_target_pairs={{1,2},{3,4},{5,6},{7,8},{9,10},{11,12},{13,14},{15,16},{17,18},{19... | collective-permute-start | bytes 184328 | tf_op jit(solution)/shard_map/ppermute | solution.py:414
  81.0 2.9 %collective-permute-start.4 = (f32[40,384]{1,0:T(8,128)S(1)}, f32[40,384]{1,0:T(8,128)S(1)}, u32[]{:S(2)}, u32[]{:S(2)}) collective-permute-start(f32[40,384]{1,0:T(8,128)S(1)} %get-tuple-element.75.z_ref.refs_0_.refs_9_), channel_id=1, source_target_pairs={{0,1},{1,0},{2,3},{3,2},{4,5},{5,4},{6,7},{7,6},{8,9},{9,8},{10,11... | collective-permute-start | bytes 184328 | tf_op jit(solution)/shard_map/ppermute | solution.py:415
  101.3 3.0 %collective-permute-start.7 = (f32[40,384]{1,0:T(8,128)S(1)}, f32[40,384]{1,0:T(8,128)S(1)}, u32[]{:S(2)}, u32[]{:S(2)}) collective-permute-start(f32[40,384]{1,0:T(8,128)S(1)} %get-tuple-element.81.z_ref.refs_0_.refs_10_), channel_id=1, source_target_pairs={{1,2},{3,4},{5,6},{7,8},{9,10},{11,12},{13,14},{15,16},{17,18},{19... | collective-permute-start | bytes 184328 | tf_op jit(solution)/shard_map/ppermute | solution.py:414
  101.9 2.9 %collective-permute-start.6 = (f32[40,384]{1,0:T(8,128)S(1)}, f32[40,384]{1,0:T(8,128)S(1)}, u32[]{:S(2)}, u32[]{:S(2)}) collective-permute-start(f32[40,384]{1,0:T(8,128)S(1)} %get-tuple-element.81.z_ref.refs_0_.refs_10_), channel_id=1, source_target_pairs={{0,1},{1,0},{2,3},{3,2},{4,5},{5,4},{6,7},{7,6},{8,9},{9,8},{10,11... | collective-permute-start | bytes 184328 | tf_op jit(solution)/shard_map/ppermute | solution.py:415
  122.2 3.0 %collective-permute-start.9 = (f32[40,384]{1,0:T(8,128)S(1)}, f32[40,384]{1,0:T(8,128)S(1)}, u32[]{:S(2)}, u32[]{:S(2)}) collective-permute-start(f32[40,384]{1,0:T(8,128)S(1)} %get-tuple-element.87.z_ref.refs_0_.refs_11_), channel_id=1, source_target_pairs={{1,2},{3,4},{5,6},{7,8},{9,10},{11,12},{13,14},{15,16},{17,18},{19... | collective-permute-start | bytes 184328 | tf_op jit(solution)/shard_map/ppermute | solution.py:414
  122.9 2.9 %collective-permute-start.8 = (f32[40,384]{1,0:T(8,128)S(1)}, f32[40,384]{1,0:T(8,128)S(1)}, u32[]{:S(2)}, u32[]{:S(2)}) collective-permute-start(f32[40,384]{1,0:T(8,128)S(1)} %get-tuple-element.87.z_ref.refs_0_.refs_11_), channel_id=1, source_target_pairs={{0,1},{1,0},{2,3},{3,2},{4,5},{5,4},{6,7},{7,6},{8,9},{9,8},{10,11... | collective-permute-start | bytes 184328 | tf_op jit(solution)/shard_map/ppermute | solution.py:415
  143.2 3.0 %collective-permute-start.11 = (f32[40,384]{1,0:T(8,128)S(1)}, f32[40,384]{1,0:T(8,128)S(1)}, u32[]{:S(2)}, u32[]{:S(2)}) collective-permute-start(f32[40,384]{1,0:T(8,128)S(1)} %get-tuple-element.93.z_ref.refs_0_.refs_12_), channel_id=1, source_target_pairs={{1,2},{3,4},{5,6},{7,8},{9,10},{11,12},{13,14},{15,16},{17,18},{19... | collective-permute-start | bytes 184328 | tf_op jit(solution)/shard_map/ppermute | solution.py:414
  143.8 2.9 %collective-permute-start.10 = (f32[40,384]{1,0:T(8,128)S(1)}, f32[40,384]{1,0:T(8,128)S(1)}, u32[]{:S(2)}, u32[]{:S(2)}) collective-permute-start(f32[40,384]{1,0:T(8,128)S(1)} %get-tuple-element.93.z_ref.refs_0_.refs_12_), channel_id=1, source_target_pairs={{0,1},{1,0},{2,3},{3,2},{4,5},{5,4},{6,7},{7,6},{8,9},{9,8},{10,11... | collective-permute-start | bytes 184328 | tf_op jit(solution)/shard_map/ppermute | solution.py:415

commit v2 on v1

--- a/solution.py
+++ b/solution.py
@@ -12,7 +12,9 @@
 AXES = ("dom", "grp")
 F32 = jnp.float32
 BF16 = jnp.bfloat16
+CHUNK = 256
 VMEM = pl.BlockSpec(memory_space=pltpu.VMEM)
+ANY = pl.BlockSpec(memory_space=pl.ANY)
 SMEM = pl.BlockSpec(memory_space=pltpu.SMEM)
 
 
@@ -82,20 +84,32 @@
     return [jnp.sum(jnp.where(lane == i, row, 0.0), axis=1, keepdims=True) for i in range(count)]
 
 
-def init_kernel(
-    sz, me_ref, res_ref, state_ref, orders_ref, nbr_ref, face_ref, orient_ref, source_ref, flux_ref, geo_ref,
-    stiff_ref, trace_ref, start_ref, state2_ref, mask_ref, hot_ref, coup_ref, sel_ref, own_ref, near_ref, back_ref,
-    part_ref,
-):
-    nv, nb, ne, nq, nbp, nqp = sz.nv, sz.nb, sz.ne, sz.nq, sz.nbp, sz.nqp
+def fetch(pairs, sems):
+    copies = [pltpu.make_async_copy(src, dst, sems.at[i]) for i, (src, dst) in enumerate(pairs)]
+    for copy in copies:
+        copy.start()
+    for copy in copies:
+        copy.wait()
+
+
+def begin_kernel(sz, res_hbm, orders_hbm, start_ref, mask_ref, part_ref, res_ref, orders_ref, sems):
+    fetch([(res_hbm, res_ref), (orders_hbm, orders_ref)], sems)
     orders = orders_ref[...]
     count = (orders + 1) * (orders + 2) * (orders + 3) // 6
-    count = jnp.concatenate([count] * nv, axis=1)
-    mask = (iota((nbp, sz.lanes), 0) < count).astype(F32)
+    count = jnp.concatenate([count] * sz.nv, axis=1)
+    mask = (iota((sz.nbp, sz.lanes), 0) < count).astype(F32)
     mask_ref[...] = mask
     start = to_wide(lambda v: res_ref[v], sz) * mask
     start_ref[...] = start
     part_ref[...] = partial_rows([full_sum(start * start)], sz.peers)
+
+
+def init_kernel(sz, me_ref, *refs):
+    args, outs, held, sems = refs[:9], refs[9:16], refs[16:25], refs[25]
+    fetch(list(zip(args, held)), sems)
+    state_ref, nbr_ref, face_ref, orient_ref, source_ref, flux_ref, geo_ref, stiff_ref, trace_ref = held
+    state2_ref, hot_ref, coup_ref, sel_ref, own_ref, near_ref, back_ref = outs
+    nv, nb, ne, nq, nbp, nqp = sz.nv, sz.nb, sz.ne, sz.nq, sz.nbp, sz.nqp
     state2_ref[...] = to_wide(lambda v: state_ref[v], sz)
 
     me = me_ref[0]
@@ -140,7 +154,7 @@
         x = jnp.concatenate([x, jnp.zeros((x.shape[0], nbp - x.shape[1]), F32)], axis=1)
         return pad_rows(x, rows)
 
-    traces = [trace_ref[f] for f in range(4)]
+    traces = [trace_ref[:, f, :] for f in range(4)]
     plain = [pad2(t, nqp) for t in traces]
     flipped = [
         pad2(jnp.concatenate([t[q : q + 1] for q in reversed(range(nq))], axis=0), nqp) for t in traces
@@ -151,61 +165,76 @@
     back_ref[...] = stack_lhs(jnp.concatenate(plain, axis=0).T)
 
 
-def relay_kernel(sz, p_ref, out_ref):
-    width, kwidth, ne = sz.width, sz.kwidth, sz.ne
-    total = width * ne
-    zeros = jnp.zeros((width, kwidth - width), F32)
-    for e in range(ne):
-        low = e * width // 128 * 128
-        high = min(ceil_to((e + 1) * width, 128), total)
-        shift = e * width - low
-        window = p_ref[:, low:high].astype(F32)
-        piece = window[:, shift : shift + width]
-        out_ref[e] = jnp.concatenate([piece, zeros], axis=1).astype(BF16)
-
-
-def apply_blocks(sz, vec, mask, blocks_ref):
-    nb, ne, nv = sz.nb, sz.ne, sz.nv
+def apply_blocks(sz, vec, mask, blocks_ref, ready):
+    nb, ne, nv, width = sz.nb, sz.ne, sz.nv, sz.width
     tall = jnp.concatenate([vec[:nb, v * ne : (v + 1) * ne] for v in range(nv)], axis=0)
-    tall = pad_rows(tall, sz.kwidth)
-    lane = iota((1, ne), 1)
-
-    def step(e, acc):
-        picked = jnp.where(lane == e, tall, 0.0).astype(BF16)
-        return acc + dot(blocks_ref[e], picked)
-
-    acc = lax.fori_loop(0, ne, step, jnp.zeros((sz.width, ne), F32), unroll=4)
-    wide = jnp.concatenate([acc[v * nb : (v + 1) * nb] for v in range(nv)], axis=1)
+    turned = pad_rows(tall, CHUNK).T
+    amount = lax.rem(iota((ne, 1), 0) * width, CHUNK)
+    bit = 1
+    while bit < CHUNK:
+        if any(e * width % CHUNK & bit for e in range(ne)):
+            turned = jnp.where((amount & bit) != 0, pltpu.roll(turned, bit, 1), turned)
+        bit *= 2
+    total = ne * width
+    acc = [jnp.zeros((8, width), F32)] * (ne // 8)
+    for low in range(0, total, CHUNK):
+        high = min(low + CHUNK, total)
+        ready(high)
+        first, last = low // width // 8, (high - 1) // width // 8 + 1
+        size = (8 * (last - first), high - low)
+        entry = iota(size, 1) + low - (iota(size, 0) + 8 * first) * width
+        lhs = jnp.where((entry >= 0) & (entry < width), turned[8 * first : 8 * last, : high - low], 0.0)
+        out = lax.dot_general(
+            lhs.astype(BF16), blocks_ref[:, low:high], (((1,), (1,)), ((), ())), preferred_element_type=F32
+        )
+        for g in range(first, last):
+            acc[g] = acc[g] + out[8 * (g - first) : 8 * (g - first + 1)]
+    done = jnp.concatenate(acc, axis=0)
+    done = jnp.concatenate([done, jnp.zeros((ne, CHUNK - width), F32)], axis=1).T
+    wide = jnp.concatenate([done[v * nb : (v + 1) * nb] for v in range(nv)], axis=1)
     return pad_rows(wide, sz.nbp) * mask
+
+
+def precond_start_kernel(sz, red_ref, vec_ref, mask_ref, state_ref, p_hbm, z_ref, v_ref, h_ref, blocks_ref, sems):
+    total, count = sz.ne * sz.width, sems.shape[0]
+    step = ceil_to(-(-total // count), 128)
+    edges = [(low, min(low + step, total)) for low in range(0, total, step)]
+    copies = [
+        pltpu.make_async_copy(p_hbm.at[:, low:high], blocks_ref.at[:, low:high], sems.at[i])
+        for i, (low, high) in enumerate(edges)
+    ]
+    for copy in copies:
+        copy.start()
+    norm = jnp.sqrt(total_scalars(red_ref[...], 1)[0] + EPSILON)
+    new = vec_ref[...] / norm
+    v_ref[...] = new
+    h_ref[...] = partial_rows([norm], 1)
+    waited = []
+
+    def ready(high):
+        while len(waited) < len(edges) and edges[len(waited)][0] < high:
+            copies[len(waited)].wait()
+            waited.append(True)
+
+    z_ref[: sz.nbp] = apply_blocks(sz, new, mask_ref[...], blocks_ref, ready)
+    z_ref[sz.nbp :] = state_ref[...]
 
 
 def precond_kernel(sz, step, *refs):
     red_ref, vec_ref, mask_ref, blocks_ref = refs[:4]
-    mask = mask_ref[...]
+    basis = refs[4 : 4 + step]
+    z_ref, v_ref, h_ref = refs[4 + step :]
     vec = vec_ref[...]
-    if step == 0:
-        state_ref, z_ref, v_ref, h_ref = refs[4:]
-        norm = jnp.sqrt(total_scalars(red_ref[...], 1)[0] + EPSILON)
-        values = [norm]
-    else:
-        basis = refs[4 : 4 + step]
-        z_ref, v_ref, h_ref = refs[4 + step :]
-        scalars = total_scalars(red_ref[...], step + 1)
-        proj, square = scalars[:step], scalars[step]
-        for h, b in zip(proj, basis):
-            vec = vec - h * b[...]
-            square = square - h * h
-        norm = jnp.sqrt(square + EPSILON)
-        values = proj + [norm]
+    scalars = total_scalars(red_ref[...], step + 1)
+    proj, square = scalars[:step], scalars[step]
+    for h, b in zip(proj, basis):
+        vec = vec - h * b[...]
+        square = square - h * h
+    norm = jnp.sqrt(square + EPSILON)
     new = vec / norm
     v_ref[...] = new
-    h_ref[...] = partial_rows(values, 1)
-    search = apply_blocks(sz, new, mask, blocks_ref)
-    if step == 0:
-        z_ref[: sz.nbp] = search
-        z_ref[sz.nbp :] = state_ref[...]
-    else:
-        z_ref[...] = search
+    h_ref[...] = partial_rows(proj + [norm], 1)
+    z_ref[...] = apply_blocks(sz, new, mask_ref[...], blocks_ref, lambda high: None)
 
 
 def roll_blocks(x, blocks, ne):
@@ -342,22 +371,25 @@
         out_ref[v] = total[: sz.nb, v * sz.ne : (v + 1) * sz.ne]
 
 
-def call(kernel, name, out_shape, *args, smem_first=False, limit=None):
-    specs = [VMEM] * len(args)
-    if smem_first:
-        specs[0] = SMEM
+def call(kernel, name, out_shape, *args, specs=None, scratch=(), cost=None):
     return pl.pallas_call(
         kernel,
         name=name,
         out_shape=out_shape,
-        in_specs=specs,
+        in_specs=specs or [VMEM] * len(args),
         out_specs=jax.tree.map(lambda _: VMEM, out_shape),
-        compiler_params=pltpu.CompilerParams(vmem_limit_bytes=limit or 32 * 2**20),
+        scratch_shapes=list(scratch),
+        cost_estimate=cost,
+        compiler_params=pltpu.CompilerParams(vmem_limit_bytes=24 * 2**20),
     )(*args)
 
 
 def shape(*dims, dtype=F32):
     return jax.ShapeDtypeStruct(dims, dtype)
+
+
+def copied(arrays):
+    return [pltpu.VMEM(a.shape, a.dtype) for a in arrays] + [pltpu.SemaphoreType.DMA((len(arrays),))]
 
 
 def body(
@@ -370,25 +402,28 @@
     me = lax.axis_index(AXES).astype(jnp.int32).reshape(1)
     wide = shape(nbp, lanes)
     parts = shape(peers, 128)
-    start, state, mask, hot, coup, sel, own, near, back, part = call(
+    fetched = [residual_in, orders.reshape(1, ne)]
+    start, mask, part = call(
+        functools.partial(begin_kernel, sz), "begin", (wide, wide, parts), *fetched,
+        specs=[ANY] * 2, scratch=copied(fetched),
+    )
+    fetched = [
+        state_coeffs, neighbours, neighbour_face, orientation, source, flux_jacobian, geometry, stiffness,
+        jnp.transpose(trace_matrix, (1, 0, 2)),
+    ]
+    state, hot, coup, sel, own, near, back = call(
         functools.partial(init_kernel, sz),
         "init",
         (
-            wide, wide, wide,
+            wide,
             shape(3 * sz.pair, 4 * sz.pair, dtype=BF16),
             shape(4, nv, lanes),
             shape(8, lanes, dtype=jnp.int32),
             shape(4 * nqp + 3 * nbp, 6 * nbp, dtype=BF16),
             shape(8 * nqp, 6 * nbp, dtype=BF16),
             shape(nbp, 24 * nqp, dtype=BF16),
-            parts,
         ),
-        me, residual_in, state_coeffs, orders.reshape(1, ne), neighbours, neighbour_face, orientation, source,
-        flux_jacobian, geometry, stiffness, trace_matrix,
-        smem_first=True,
-    )
-    blocks = call(
-        functools.partial(relay_kernel, sz), "relay", shape(ne, sz.width, sz.kwidth, dtype=BF16), precond
+        me, *fetched, specs=[SMEM] + [ANY] * len(fetched), scratch=copied(fetched),
     )
 
     def exchange(rows):
@@ -402,12 +437,18 @@
     vec, gain = start, None
     for k in range(ITERS):
         red = exchange(part)
-        z_shape = shape(2 * nbp, lanes) if k == 0 else wide
-        extra = [state] if k == 0 else basis
-        search, new, head = call(
-            functools.partial(precond_kernel, sz, k), f"precond{k}", (z_shape, wide, shape(1, 128)),
-            red, vec, mask, blocks, *extra,
-        )
+        if k == 0:
+            search, new, head, blocks = call(
+                functools.partial(precond_start_kernel, sz), "precond0",
+                (shape(2 * nbp, lanes), wide, shape(1, 128), shape(*precond.shape, dtype=BF16)),
+                red, vec, mask, state, precond, specs=[VMEM] * 4 + [ANY],
+                scratch=[pltpu.SemaphoreType.DMA((7,))],
+            )
+        else:
+            search, new, head = call(
+                functools.partial(precond_kernel, sz, k), f"precond{k}", (wide, wide, shape(1, 128)),
+                red, vec, mask, blocks, *basis,
+            )
         basis = basis + [new]
         heads.append(head)
         searches.append(search)

time: 162 us -> 143 us (0.88)
  Pallas kernels: 41.6 us -> 28.8 us
  local copies, waits for them, and re-layouts: 16.9 us -> 11 us
    pallas_call x22, Pallas kernels: 41.6 us -> 28.8 us  [call(): pl.pallas_call(kernel, name=name, out_shape=out_shape, in_specs=specs or...]
    unnamed x29 -> x24, local copies, waits for them, and re-layouts: 16.9 us -> 11 us
  transfers between devices with their start and end apart: 13 -> 13, of which waited for: 6 -> 6; matrix products, arithmetic and copies ran while one was open for 0% -> 0% of each run, Pallas kernels for 3% -> 2%
where the time goes in v2:
time: 143 us; the launch traced here: 142 us
  blocking collectives  74 us (52%)
  Pallas kernels  28.8 us (20%)
  starting transfers between devices  24.3 us (17%)
  local copies, waits for them, and re-layouts  11 us (8%)
  waiting for transfers between devices  3.31 us (2%)
    all_to_all x6, blocking collectives, exchange(): return lax.all_to_all(rows, AXES, 0, 0, tiled=True)  74 us
    pallas_call x22, Pallas kernels, call(): pl.pallas_call(kernel, name=name, out_shape=out_shape, in_specs=specs or...  28.8 us
    ppermute x6, starting transfers between devices, body(): chip = lax.ppermute(search, AXES, on_chip)  13 us
    unnamed x24, local copies, waits for them, and re-layouts  11 us
    all_to_all x1, starting transfers between devices, exchange(): return lax.all_to_all(rows, AXES, 0, 0, tiled=True)  7.33 us
    ppermute x6, starting transfers between devices, body(): far = lax.ppermute(search, AXES, off_chip)  3.99 us
    ppermute x6, waiting for transfers between devices, body(): chip = lax.ppermute(search, AXES, on_chip)  3.29 us
  transfers between devices with their start and end apart: 13, of which 6 were waited for; matrix products, arithmetic and copies ran while one was open for 0% of the time, Pallas kernels for 2%

profile of v2, /device:TPU:0, one launch (start us, length us, event | category | flops | bytes accessed | tf_op | source)
XLA Modules:
  0.0 142.3 jit_solution(15214106156601496118)
XLA Ops:
  0.6 0.9 copy-done.1
  1.5 0.7 copy-done.11
  2.2 0.8 begin.1
  3.0 7.3 %all-to-all-start = ((f32[32,1,128]{2,1,0:T(1,128)}), f32[32,1,128]{2,1,0:T(1,128)S(1)}, u32[]{:S(2)}, u32[]{:S(2)}) async-start(f32[32,1,128]{2,1,0:T(1,128)} %bitcast.2), calls=%async_computation | async-start | bytes 32768 | tf_op jit(solution)/shard_map/all_to_all | solution.py:430
  10.4 0.0 copy-start.2
  10.4 0.9 copy-done.2
  11.3 0.9 copy-done.3
  12.2 0.8 copy-done.4
  13.0 0.8 copy-done.5
  13.7 0.7 copy-done.6
  14.5 0.7 copy-done.7
  15.2 0.7 copy-done.8
  15.8 0.7 copy-done.9
  16.5 0.7 copy-done.10
  17.2 0.5 init.1
  17.7 0.0 all-to-all-done
  17.8 0.0 copy-start
  17.8 2.6 %copy-done = bf16[210,13440]{1,0:T(8,128)(2,1)S(1)} copy-done((bf16[210,13440]{1,0:T(8,128)(2,1)S(1)}, bf16[210,13440]{1,0:T(8,128)(2,1)}, u32[]{:S(2)}) %copy-start) | copy-done | bytes 5644824
  20.4 4.2 %precond0.1 = (f32[80,384]{1,0:T(8,128)S(1)}, f32[40,384]{1,0:T(8,128)S(1)}, f32[1,128]{1,0:T(1,128)S(1)}, bf16[210,13440]{1,0:T(8,128)(2,1)S(1)}) custom-call(f32[32,128]{1,0:T(8,128)S(1)} %bitcast.31, f32[40,384]{1,0:T(8,128)S(1)} %get-tuple-element.55.vec_ref, f32[40,384]{1,0:T(8,128)S(1)} %get-tuple-element.56.mask_ref.refs_10_.refs_2_, ...), custom_call_target="tpu_custom_call" | custom-call | tf_op jit(solution)/shard_map/precond0/pallas_call | solution.py:375
  24.7 0.7 collective-permute-start.1
  25.3 3.2 %collective-permute-start = (f32[80,384]{1,0:T(8,128)S(1)}, f32[80,384]{1,0:T(8,128)S(1)}, u32[]{:S(2)}, u32[]{:S(2)}) collective-permute-start(f32[80,384]{1,0:T(8,128)S(1)} %get-tuple-element.58.z_ref.refs_0_.refs_7_), channel_id=1, source_target_pairs={{0,1},{1,0},{2,3},{3,2},{4,5},{5,4},{6,7},{7,6},{8,9},{9,8},{10,11... | collective-permute-start | bytes 368648 | tf_op jit(solution)/shard_map/ppermute | solution.py:456
  28.5 0.3 local.6
  28.9 0.6 collective-permute-done.chip_ref.refs_1_
  29.5 0.7 gain.1.refs_6_
  30.2 0.9 image0.1
  31.1 15.2 %all_to_all.77 = f32[32,1,128]{2,1,0:T(1,128)S(1)} all-to-all(f32[32,1,128]{2,1,0:T(1,128)S(1)} %bitcast.40), channel_id=1, replica_groups=mesh['dom'=8,'grp'=4] {'dom','grp'}, dimensions={0} | all-to-all | bytes 32768 | tf_op jit(solution)/shard_map/all_to_all | solution.py:430
  46.3 2.7 %precond1.1 = (f32[40,384]{1,0:T(8,128)S(1)}, f32[40,384]{1,0:T(8,128)S(1)}, f32[1,128]{1,0:T(1,128)S(1)}) custom-call(f32[32,128]{1,0:T(8,128)S(1)} %bitcast.33, f32[40,384]{1,0:T(8,128)S(1)} %get-tuple-element.69.refs_1_, f32[40,384]{1,0:T(8,128)S(1)} %get-tuple-element.56.mask_ref.refs_10_.refs_2_, bf16[210,13440]{1,0:T(8,128)(2,1)S(1)} %get-tuple-element.70.refs_3_, ...), custom_call_target="tpu_custom_call" | custom-call | tf_op jit(solution)/shard_map/precond1/pallas_call | solution.py:375
  49.0 0.7 collective-permute-start.3
  49.7 2.0 %collective-permute-start.2 = (f32[40,384]{1,0:T(8,128)S(1)}, f32[40,384]{1,0:T(8,128)S(1)}, u32[]{:S(2)}, u32[]{:S(2)}) collective-permute-start(f32[40,384]{1,0:T(8,128)S(1)} %get-tuple-element.71.z_ref.refs_0_.refs_8_), channel_id=1, source_target_pairs={{0,1},{1,0},{2,3},{3,2},{4,5},{5,4},{6,7},{7,6},{8,9},{9,8},{10,11... | collective-permute-start | bytes 184328 | tf_op jit(solution)/shard_map/ppermute | solution.py:456
  51.6 0.3 local.7
  52.0 0.5 collective-permute-done.2.refs_1_
  52.5 0.9 image1.1
  53.4 11.8 %all_to_all.78 = f32[32,1,128]{2,1,0:T(1,128)S(1)} all-to-all(f32[32,1,128]{2,1,0:T(1,128)S(1)} %bitcast.41), channel_id=1, replica_groups=mesh['dom'=8,'grp'=4] {'dom','grp'}, dimensions={0} | all-to-all | bytes 32768 | tf_op jit(solution)/shard_map/all_to_all | solution.py:430
  65.2 2.7 %precond2.1 = (f32[40,384]{1,0:T(8,128)S(1)}, f32[40,384]{1,0:T(8,128)S(1)}, f32[1,128]{1,0:T(1,128)S(1)}) custom-call(f32[32,128]{1,0:T(8,128)S(1)} %bitcast.34, f32[40,384]{1,0:T(8,128)S(1)} %get-tuple-element.76.refs_1_, f32[40,384]{1,0:T(8,128)S(1)} %get-tuple-element.56.mask_ref.refs_10_.refs_2_, bf16[210,13440]{1,0:T(8,128)(2,1)S(1)} %get-tuple-element.70.refs_3_, ...), custom_call_target="tpu_custom_call" | custom-call | tf_op jit(solution)/shard_map/precond2/pallas_call | solution.py:375
  67.9 0.7 collective-permute-start.5
  68.5 2.0 %collective-permute-start.4 = (f32[40,384]{1,0:T(8,128)S(1)}, f32[40,384]{1,0:T(8,128)S(1)}, u32[]{:S(2)}, u32[]{:S(2)}) collective-permute-start(f32[40,384]{1,0:T(8,128)S(1)} %get-tuple-element.77.z_ref.refs_0_.refs_9_), channel_id=1, source_target_pairs={{0,1},{1,0},{2,3},{3,2},{4,5},{5,4},{6,7},{7,6},{8,9},{9,8},{10,11... | collective-permute-start | bytes 184328 | tf_op jit(solution)/shard_map/ppermute | solution.py:456
  70.5 0.3 local.8
  70.9 0.0 collective-permute-done.5.refs_2_
  70.9 0.5 collective-permute-done.4.refs_1_
  71.4 0.9 image2.1
  72.3 11.8 %all_to_all.79 = f32[32,1,128]{2,1,0:T(1,128)S(1)} all-to-all(f32[32,1,128]{2,1,0:T(1,128)S(1)} %bitcast.42), channel_id=1, replica_groups=mesh['dom'=8,'grp'=4] {'dom','grp'}, dimensions={0} | all-to-all | bytes 32768 | tf_op jit(solution)/shard_map/all_to_all | solution.py:430
  84.1 2.7 %precond3.1 = (f32[40,384]{1,0:T(8,128)S(1)}, f32[40,384]{1,0:T(8,128)S(1)}, f32[1,128]{1,0:T(1,128)S(1)}) custom-call(f32[32,128]{1,0:T(8,128)S(1)} %bitcast.35, f32[40,384]{1,0:T(8,128)S(1)} %get-tuple-element.82.refs_1_, f32[40,384]{1,0:T(8,128)S(1)} %get-tuple-element.56.mask_ref.refs_10_.refs_2_, bf16[210,13440]{1,0:T(8,128)(2,1)S(1)} %get-tuple-element.70.refs_3_, ...), custom_call_target="tpu_custom_call" | custom-call | tf_op jit(solution)/shard_map/precond3/pallas_call | solution.py:375
  86.8 0.7 collective-permute-start.7
  87.4 2.0 %collective-permute-start.6 = (f32[40,384]{1,0:T(8,128)S(1)}, f32[40,384]{1,0:T(8,128)S(1)}, u32[]{:S(2)}, u32[]{:S(2)}) collective-permute-start(f32[40,384]{1,0:T(8,128)S(1)} %get-tuple-element.83.z_ref.refs_0_.refs_10_), channel_id=1, source_target_pairs={{0,1},{1,0},{2,3},{3,2},{4,5},{5,4},{6,7},{7,6},{8,9},{9,8},{10,11... | collective-permute-start | bytes 184328 | tf_op jit(solution)/shard_map/ppermute | solution.py:456
  89.4 0.3 local.9
  89.7 0.5 collective-permute-done.6.refs_1_
  90.3 0.9 image3.1
  91.2 11.7 %all_to_all.80 = f32[32,1,128]{2,1,0:T(1,128)S(1)} all-to-all(f32[32,1,128]{2,1,0:T(1,128)S(1)} %bitcast.43), channel_id=1, replica_groups=mesh['dom'=8,'grp'=4] {'dom','grp'}, dimensions={0} | all-to-all | bytes 32768 | tf_op jit(solution)/shard_map/all_to_all | solution.py:430
  103.0 2.7 %precond4.1 = (f32[40,384]{1,0:T(8,128)S(1)}, f32[40,384]{1,0:T(8,128)S(1)}, f32[1,128]{1,0:T(1,128)S(1)}) custom-call(f32[32,128]{1,0:T(8,128)S(1)} %bitcast.36, f32[40,384]{1,0:T(8,128)S(1)} %get-tuple-element.88.refs_1_, f32[40,384]{1,0:T(8,128)S(1)} %get-tuple-element.56.mask_ref.refs_10_.refs_2_, bf16[210,13440]{1,0:T(8,128)(2,1)S(1)} %get-tuple-element.70.refs_3_, ...), custom_call_target="tpu_custom_call" | custom-call | tf_op jit(solution)/shard_map/precond4/pallas_call | solution.py:375
  105.7 0.7 collective-permute-start.9
  106.3 2.0 %collective-permute-start.8 = (f32[40,384]{1,0:T(8,128)S(1)}, f32[40,384]{1,0:T(8,128)S(1)}, u32[]{:S(2)}, u32[]{:S(2)}) collective-permute-start(f32[40,384]{1,0:T(8,128)S(1)} %get-tuple-element.89.z_ref.refs_0_.refs_11_), channel_id=1, source_target_pairs={{0,1},{1,0},{2,3},{3,2},{4,5},{5,4},{6,7},{7,6},{8,9},{9,8},{10,11... | collective-permute-start | bytes 184328 | tf_op jit(solution)/shard_map/ppermute | solution.py:456
  108.3 0.3 local.10
  108.6 0.0 collective-permute-done.9.refs_2_
  108.6 0.5 collective-permute-done.8.refs_1_
  109.2 0.9 image4.1
  110.1 11.8 %all_to_all.81 = f32[32,1,128]{2,1,0:T(1,128)S(1)} all-to-all(f32[32,1,128]{2,1,0:T(1,128)S(1)} %bitcast.44), channel_id=1, replica_groups=mesh['dom'=8,'grp'=4] {'dom','grp'}, dimensions={0} | all-to-all | bytes 32768 | tf_op jit(solution)/shard_map/all_to_all | solution.py:430
  121.9 2.7 %precond5.1 = (f32[40,384]{1,0:T(8,128)S(1)}, f32[40,384]{1,0:T(8,128)S(1)}, f32[1,128]{1,0:T(1,128)S(1)}) custom-call(f32[32,128]{1,0:T(8,128)S(1)} %bitcast.32, f32[40,384]{1,0:T(8,128)S(1)} %get-tuple-element.94.refs_1_, f32[40,384]{1,0:T(8,128)S(1)} %get-tuple-element.56.mask_ref.refs_10_.refs_2_, bf16[210,13440]{1,0:T(8,128)(2,1)S(1)} %get-tuple-element.70.refs_3_, ...), custom_call_target="tpu_custom_call" | custom-call | tf_op jit(solution)/shard_map/precond5/pallas_call | solution.py:375
  124.6 0.7 collective-permute-start.11
  125.2 2.0 %collective-permute-start.10 = (f32[40,384]{1,0:T(8,128)S(1)}, f32[40,384]{1,0:T(8,128)S(1)}, u32[]{:S(2)}, u32[]{:S(2)}) collective-permute-start(f32[40,384]{1,0:T(8,128)S(1)} %get-tuple-element.95.z_ref.refs_0_.refs_12_), channel_id=1, source_target_pairs={{0,1},{1,0},{2,3},{3,2},{4,5},{5,4},{6,7},{7,6},{8,9},{9,8},{10,11... | collective-permute-start | bytes 184328 | tf_op jit(solution)/shard_map/ppermute | solution.py:456
  127.2 0.3 local.11
  127.5 0.5 collective-permute-done.10.refs_1_
  128.1 1.5 %image5.1 = (f32[40,384]{1,0:T(8,128)}, f32[32,128]{1,0:T(8,128)S(1)}) custom-call(f32[40,384]{1,0:T(8,128)S(1)} %get-tuple-element.95.z_ref.refs_0_.refs_12_, f32[40,384]{1,0:T(8,128)S(1)} %collective-permute-done.10.refs_1_, f32[40,384]{1,0:T(8,128)S(1)} %collective-permute-done.11.refs_2_, bf16[384,512]{1,0:T(8,128)(2,1)S(1)} %get-tuple-element.59.hot_ref.refs_3_, ...), custom_call_target="tpu_custom_call" | custom-call | tf_op jit(solution)/shard_map/image5/pallas_call | solution.py:375
  129.6 11.7 %all_to_all.82 = f32[32,1,128]{2,1,0:T(1,128)S(1)} all-to-all(f32[32,1,128]{2,1,0:T(1,128)S(1)} %bitcast.39), channel_id=1, replica_groups=mesh['dom'=8,'grp'=4] {'dom','grp'}, dimensions={0} | all-to-all | bytes 32768 | tf_op jit(solution)/shard_map/all_to_all | solution.py:430
  141.3 1.0 finish.1
  (14 shorter events, 0.0 us)
Async XLA Ops:
  0.6 0.9 copy-start.1
  1.5 0.7 copy-start.11
  3.0 14.7 %all-to-all-start = ((f32[32,1,128]{2,1,0:T(1,128)}), f32[32,1,128]{2,1,0:T(1,128)S(1)}, u32[]{:S(2)}, u32[]{:S(2)}) async-start(f32[32,1,128]{2,1,0:T(1,128)} %bitcast.2), calls=%async_computation | async-start | bytes 32768 | tf_op jit(solution)/shard_map/all_to_all | solution.py:430
  10.4 0.9 copy-start.2
  11.3 0.9 copy-start.3
  12.2 0.8 copy-start.4
  13.0 0.8 copy-start.5
  13.7 0.7 copy-start.6
  14.5 0.7 copy-start.7
  15.2 0.7 copy-start.8
  15.8 0.7 copy-start.9
  16.5 0.7 copy-start.10
  17.8 2.6 %copy-start = (bf16[210,13440]{1,0:T(8,128)(2,1)S(1)}, bf16[210,13440]{1,0:T(8,128)(2,1)}, u32[]{:S(2)}) copy-start(bf16[210,13440]{1,0:T(8,128)(2,1)} %p_hbm.1) | copy-start | bytes 16934404
  24.7 4.2 %collective-permute-start.1 = (f32[80,384]{1,0:T(8,128)S(1)}, f32[80,384]{1,0:T(8,128)S(1)}, u32[]{:S(2)}, u32[]{:S(2)}) collective-permute-start(f32[80,384]{1,0:T(8,128)S(1)} %get-tuple-element.58.z_ref.refs_0_.refs_7_), channel_id=1, source_target_pairs={{1,2},{3,4},{5,6},{7,8},{9,10},{11,12},{13,14},{15,16},{17,18},{19... | collective-permute-start | bytes 368648 | tf_op jit(solution)/shard_map/ppermute | solution.py:455
  25.3 4.2 %collective-permute-start = (f32[80,384]{1,0:T(8,128)S(1)}, f32[80,384]{1,0:T(8,128)S(1)}, u32[]{:S(2)}, u32[]{:S(2)}) collective-permute-start(f32[80,384]{1,0:T(8,128)S(1)} %get-tuple-element.58.z_ref.refs_0_.refs_7_), channel_id=1, source_target_pairs={{0,1},{1,0},{2,3},{3,2},{4,5},{5,4},{6,7},{7,6},{8,9},{9,8},{10,11... | collective-permute-start | bytes 368648 | tf_op jit(solution)/shard_map/ppermute | solution.py:456
  49.0 3.0 %collective-permute-start.3 = (f32[40,384]{1,0:T(8,128)S(1)}, f32[40,384]{1,0:T(8,128)S(1)}, u32[]{:S(2)}, u32[]{:S(2)}) collective-permute-start(f32[40,384]{1,0:T(8,128)S(1)} %get-tuple-element.71.z_ref.refs_0_.refs_8_), channel_id=1, source_target_pairs={{1,2},{3,4},{5,6},{7,8},{9,10},{11,12},{13,14},{15,16},{17,18},{19... | collective-permute-start | bytes 184328 | tf_op jit(solution)/shard_map/ppermute | solution.py:455
  49.7 2.9 %collective-permute-start.2 = (f32[40,384]{1,0:T(8,128)S(1)}, f32[40,384]{1,0:T(8,128)S(1)}, u32[]{:S(2)}, u32[]{:S(2)}) collective-permute-start(f32[40,384]{1,0:T(8,128)S(1)} %get-tuple-element.71.z_ref.refs_0_.refs_8_), channel_id=1, source_target_pairs={{0,1},{1,0},{2,3},{3,2},{4,5},{5,4},{6,7},{7,6},{8,9},{9,8},{10,11... | collective-permute-start | bytes 184328 | tf_op jit(solution)/shard_map/ppermute | solution.py:456
  67.9 3.0 %collective-permute-start.5 = (f32[40,384]{1,0:T(8,128)S(1)}, f32[40,384]{1,0:T(8,128)S(1)}, u32[]{:S(2)}, u32[]{:S(2)}) collective-permute-start(f32[40,384]{1,0:T(8,128)S(1)} %get-tuple-element.77.z_ref.refs_0_.refs_9_), channel_id=1, source_target_pairs={{1,2},{3,4},{5,6},{7,8},{9,10},{11,12},{13,14},{15,16},{17,18},{19... | collective-permute-start | bytes 184328 | tf_op jit(solution)/shard_map/ppermute | solution.py:455
  68.5 2.9 %collective-permute-start.4 = (f32[40,384]{1,0:T(8,128)S(1)}, f32[40,384]{1,0:T(8,128)S(1)}, u32[]{:S(2)}, u32[]{:S(2)}) collective-permute-start(f32[40,384]{1,0:T(8,128)S(1)} %get-tuple-element.77.z_ref.refs_0_.refs_9_), channel_id=1, source_target_pairs={{0,1},{1,0},{2,3},{3,2},{4,5},{5,4},{6,7},{7,6},{8,9},{9,8},{10,11... | collective-permute-start | bytes 184328 | tf_op jit(solution)/shard_map/ppermute | solution.py:456
  86.8 3.0 %collective-permute-start.7 = (f32[40,384]{1,0:T(8,128)S(1)}, f32[40,384]{1,0:T(8,128)S(1)}, u32[]{:S(2)}, u32[]{:S(2)}) collective-permute-start(f32[40,384]{1,0:T(8,128)S(1)} %get-tuple-element.83.z_ref.refs_0_.refs_10_), channel_id=1, source_target_pairs={{1,2},{3,4},{5,6},{7,8},{9,10},{11,12},{13,14},{15,16},{17,18},{19... | collective-permute-start | bytes 184328 | tf_op jit(solution)/shard_map/ppermute | solution.py:455
  87.4 2.9 %collective-permute-start.6 = (f32[40,384]{1,0:T(8,128)S(1)}, f32[40,384]{1,0:T(8,128)S(1)}, u32[]{:S(2)}, u32[]{:S(2)}) collective-permute-start(f32[40,384]{1,0:T(8,128)S(1)} %get-tuple-element.83.z_ref.refs_0_.refs_10_), channel_id=1, source_target_pairs={{0,1},{1,0},{2,3},{3,2},{4,5},{5,4},{6,7},{7,6},{8,9},{9,8},{10,11... | collective-permute-start | bytes 184328 | tf_op jit(solution)/shard_map/ppermute | solution.py:456
  105.7 3.0 %collective-permute-start.9 = (f32[40,384]{1,0:T(8,128)S(1)}, f32[40,384]{1,0:T(8,128)S(1)}, u32[]{:S(2)}, u32[]{:S(2)}) collective-permute-start(f32[40,384]{1,0:T(8,128)S(1)} %get-tuple-element.89.z_ref.refs_0_.refs_11_), channel_id=1, source_target_pairs={{1,2},{3,4},{5,6},{7,8},{9,10},{11,12},{13,14},{15,16},{17,18},{19... | collective-permute-start | bytes 184328 | tf_op jit(solution)/shard_map/ppermute | solution.py:455
  106.3 2.9 %collective-permute-start.8 = (f32[40,384]{1,0:T(8,128)S(1)}, f32[40,384]{1,0:T(8,128)S(1)}, u32[]{:S(2)}, u32[]{:S(2)}) collective-permute-start(f32[40,384]{1,0:T(8,128)S(1)} %get-tuple-element.89.z_ref.refs_0_.refs_11_), channel_id=1, source_target_pairs={{0,1},{1,0},{2,3},{3,2},{4,5},{5,4},{6,7},{7,6},{8,9},{9,8},{10,11... | collective-permute-start | bytes 184328 | tf_op jit(solution)/shard_map/ppermute | solution.py:456
  124.6 3.0 %collective-permute-start.11 = (f32[40,384]{1,0:T(8,128)S(1)}, f32[40,384]{1,0:T(8,128)S(1)}, u32[]{:S(2)}, u32[]{:S(2)}) collective-permute-start(f32[40,384]{1,0:T(8,128)S(1)} %get-tuple-element.95.z_ref.refs_0_.refs_12_), channel_id=1, source_target_pairs={{1,2},{3,4},{5,6},{7,8},{9,10},{11,12},{13,14},{15,16},{17,18},{19... | collective-permute-start | bytes 184328 | tf_op jit(solution)/shard_map/ppermute | solution.py:455
  125.2 2.9 %collective-permute-start.10 = (f32[40,384]{1,0:T(8,128)S(1)}, f32[40,384]{1,0:T(8,128)S(1)}, u32[]{:S(2)}, u32[]{:S(2)}) collective-permute-start(f32[40,384]{1,0:T(8,128)S(1)} %get-tuple-element.95.z_ref.refs_0_.refs_12_), channel_id=1, source_target_pairs={{0,1},{1,0},{2,3},{3,2},{4,5},{5,4},{6,7},{7,6},{8,9},{9,8},{10,11... | collective-permute-start | bytes 184328 | tf_op jit(solution)/shard_map/ppermute | solution.py:456

commit v3 on v2

--- a/solution.py
+++ b/solution.py
@@ -92,24 +92,22 @@
         copy.wait()
 
 
-def begin_kernel(sz, res_hbm, orders_hbm, start_ref, mask_ref, part_ref, res_ref, orders_ref, sems):
-    fetch([(res_hbm, res_ref), (orders_hbm, orders_ref)], sems)
+def init_kernel(sz, me_ref, p_hbm, *refs):
+    args, outs, held, sems, p_sem = refs[:11], refs[11:22], refs[22:33], refs[33], refs[34]
+    blocks = pltpu.make_async_copy(p_hbm, outs[10], p_sem)
+    blocks.start()
+    fetch(list(zip(args, held)), sems)
+    (res_ref, orders_ref, state_ref, nbr_ref, face_ref, orient_ref, source_ref, flux_ref, geo_ref, stiff_ref, trace_ref) = held
+    start_ref, mask_ref, part_ref, state2_ref, hot_ref, coup_ref, sel_ref, own_ref, near_ref, back_ref = outs[:10]
+    nv, nb, ne, nq, nbp, nqp = sz.nv, sz.nb, sz.ne, sz.nq, sz.nbp, sz.nqp
     orders = orders_ref[...]
     count = (orders + 1) * (orders + 2) * (orders + 3) // 6
-    count = jnp.concatenate([count] * sz.nv, axis=1)
-    mask = (iota((sz.nbp, sz.lanes), 0) < count).astype(F32)
+    count = jnp.concatenate([count] * nv, axis=1)
+    mask = (iota((nbp, sz.lanes), 0) < count).astype(F32)
     mask_ref[...] = mask
     start = to_wide(lambda v: res_ref[v], sz) * mask
     start_ref[...] = start
     part_ref[...] = partial_rows([full_sum(start * start)], sz.peers)
-
-
-def init_kernel(sz, me_ref, *refs):
-    args, outs, held, sems = refs[:9], refs[9:16], refs[16:25], refs[25]
-    fetch(list(zip(args, held)), sems)
-    state_ref, nbr_ref, face_ref, orient_ref, source_ref, flux_ref, geo_ref, stiff_ref, trace_ref = held
-    state2_ref, hot_ref, coup_ref, sel_ref, own_ref, near_ref, back_ref = outs
-    nv, nb, ne, nq, nbp, nqp = sz.nv, sz.nb, sz.ne, sz.nq, sz.nbp, sz.nqp
     state2_ref[...] = to_wide(lambda v: state_ref[v], sz)
 
     me = me_ref[0]
@@ -163,9 +161,10 @@
     own_ref[...] = stack_lhs(jnp.concatenate(plain + volume, axis=0))
     near_ref[...] = stack_lhs(jnp.concatenate(plain + flipped, axis=0))
     back_ref[...] = stack_lhs(jnp.concatenate(plain, axis=0).T)
-
-
-def apply_blocks(sz, vec, mask, blocks_ref, ready):
+    blocks.wait()
+
+
+def apply_blocks(sz, vec, mask, blocks_ref):
     nb, ne, nv, width = sz.nb, sz.ne, sz.nv, sz.width
     tall = jnp.concatenate([vec[:nb, v * ne : (v + 1) * ne] for v in range(nv)], axis=0)
     turned = pad_rows(tall, CHUNK).T
@@ -179,7 +178,6 @@
     acc = [jnp.zeros((8, width), F32)] * (ne // 8)
     for low in range(0, total, CHUNK):
         high = min(low + CHUNK, total)
-        ready(high)
         first, last = low // width // 8, (high - 1) // width // 8 + 1
         size = (8 * (last - first), high - low)
         entry = iota(size, 1) + low - (iota(size, 0) + 8 * first) * width
@@ -195,28 +193,12 @@
     return pad_rows(wide, sz.nbp) * mask
 
 
-def precond_start_kernel(sz, red_ref, vec_ref, mask_ref, state_ref, p_hbm, z_ref, v_ref, h_ref, blocks_ref, sems):
-    total, count = sz.ne * sz.width, sems.shape[0]
-    step = ceil_to(-(-total // count), 128)
-    edges = [(low, min(low + step, total)) for low in range(0, total, step)]
-    copies = [
-        pltpu.make_async_copy(p_hbm.at[:, low:high], blocks_ref.at[:, low:high], sems.at[i])
-        for i, (low, high) in enumerate(edges)
-    ]
-    for copy in copies:
-        copy.start()
+def precond_start_kernel(sz, red_ref, vec_ref, mask_ref, blocks_ref, state_ref, z_ref, v_ref, h_ref):
     norm = jnp.sqrt(total_scalars(red_ref[...], 1)[0] + EPSILON)
     new = vec_ref[...] / norm
     v_ref[...] = new
     h_ref[...] = partial_rows([norm], 1)
-    waited = []
-
-    def ready(high):
-        while len(waited) < len(edges) and edges[len(waited)][0] < high:
-            copies[len(waited)].wait()
-            waited.append(True)
-
-    z_ref[: sz.nbp] = apply_blocks(sz, new, mask_ref[...], blocks_ref, ready)
+    z_ref[: sz.nbp] = apply_blocks(sz, new, mask_ref[...], blocks_ref)
     z_ref[sz.nbp :] = state_ref[...]
 
 
@@ -234,7 +216,7 @@
     new = vec / norm
     v_ref[...] = new
     h_ref[...] = partial_rows(proj + [norm], 1)
-    z_ref[...] = apply_blocks(sz, new, mask_ref[...], blocks_ref, lambda high: None)
+    z_ref[...] = apply_blocks(sz, new, mask_ref[...], blocks_ref)
 
 
 def roll_blocks(x, blocks, ne):
@@ -371,7 +353,7 @@
         out_ref[v] = total[: sz.nb, v * sz.ne : (v + 1) * sz.ne]
 
 
-def call(kernel, name, out_shape, *args, specs=None, scratch=(), cost=None):
+def call(kernel, name, out_shape, *args, specs=None, scratch=(), limit=24 * 2**20):
     return pl.pallas_call(
         kernel,
         name=name,
@@ -379,8 +361,7 @@
         in_specs=specs or [VMEM] * len(args),
         out_specs=jax.tree.map(lambda _: VMEM, out_shape),
         scratch_shapes=list(scratch),
-        cost_estimate=cost,
-        compiler_params=pltpu.CompilerParams(vmem_limit_bytes=24 * 2**20),
+        compiler_params=pltpu.CompilerParams(vmem_limit_bytes=limit),
     )(*args)
 
 
@@ -402,28 +383,25 @@
     me = lax.axis_index(AXES).astype(jnp.int32).reshape(1)
     wide = shape(nbp, lanes)
     parts = shape(peers, 128)
-    fetched = [residual_in, orders.reshape(1, ne)]
-    start, mask, part = call(
-        functools.partial(begin_kernel, sz), "begin", (wide, wide, parts), *fetched,
-        specs=[ANY] * 2, scratch=copied(fetched),
-    )
     fetched = [
-        state_coeffs, neighbours, neighbour_face, orientation, source, flux_jacobian, geometry, stiffness,
-        jnp.transpose(trace_matrix, (1, 0, 2)),
+        residual_in, orders.reshape(1, ne), state_coeffs, neighbours, neighbour_face, orientation, source, flux_jacobian,
+        geometry, stiffness, jnp.transpose(trace_matrix, (1, 0, 2)),
     ]
-    state, hot, coup, sel, own, near, back = call(
+    start, mask, part, state, hot, coup, sel, own, near, back, blocks = call(
         functools.partial(init_kernel, sz),
         "init",
         (
-            wide,
+            wide, wide, parts, wide,
             shape(3 * sz.pair, 4 * sz.pair, dtype=BF16),
             shape(4, nv, lanes),
             shape(8, lanes, dtype=jnp.int32),
             shape(4 * nqp + 3 * nbp, 6 * nbp, dtype=BF16),
             shape(8 * nqp, 6 * nbp, dtype=BF16),
             shape(nbp, 24 * nqp, dtype=BF16),
+            shape(*precond.shape, dtype=BF16),
         ),
-        me, *fetched, specs=[SMEM] + [ANY] * len(fetched), scratch=copied(fetched),
+        me, *[pltpu.with_memory_space_constraint(a, pltpu.HBM) for a in [precond] + fetched],
+        specs=[SMEM] + [ANY] * (1 + len(fetched)), scratch=copied(fetched) + [pltpu.SemaphoreType.DMA],
     )
 
     def exchange(rows):
@@ -437,18 +415,12 @@
     vec, gain = start, None
     for k in range(ITERS):
         red = exchange(part)
-        if k == 0:
-            search, new, head, blocks = call(
-                functools.partial(precond_start_kernel, sz), "precond0",
-                (shape(2 * nbp, lanes), wide, shape(1, 128), shape(*precond.shape, dtype=BF16)),
-                red, vec, mask, state, precond, specs=[VMEM] * 4 + [ANY],
-                scratch=[pltpu.SemaphoreType.DMA((7,))],
-            )
-        else:
-            search, new, head = call(
-                functools.partial(precond_kernel, sz, k), f"precond{k}", (wide, wide, shape(1, 128)),
-                red, vec, mask, blocks, *basis,
-            )
+        kernel = functools.partial(precond_kernel, sz, k) if k else functools.partial(precond_start_kernel, sz)
+        extra = basis if k else [state]
+        search, new, head = call(
+            kernel, f"precond{k}", (shape(nbp if k else 2 * nbp, lanes), wide, shape(1, 128)),
+            red, vec, mask, blocks, *extra,
+        )
         basis = basis + [new]
         heads.append(head)
         searches.append(search)

time: 143 us -> 135 us (0.944)
  blocking collectives: 74 us -> 85.6 us
  local copies, waits for them, and re-layouts: 11 us -> 0 us
  starting transfers between devices: 24.3 us -> 15.9 us
    all_to_all x6 -> x7, blocking collectives: 74 us -> 85.6 us  [exchange(): return lax.all_to_all(rows, AXES, 0, 0, tiled=True)]
    unnamed x24 -> x0, local copies, waits for them, and re-layouts: 11 us -> none
    all_to_all x1 -> x0, starting transfers between devices: 7.33 us -> none  [exchange(): return lax.all_to_all(rows, AXES, 0, 0, tiled=True)]
    pallas_call x22 -> x21, Pallas kernels: 28.8 us -> 29 us  [call(): pl.pallas_call(kernel, name=name, out_shape=out_shape, in_specs=specs or...]
  transfers between devices with their start and end apart: 13 -> 12, of which waited for: 6 -> 6; matrix products, arithmetic and copies ran while one was open for 0% -> 0% of each run, Pallas kernels for 2% -> 2%
where the time goes in v3:
time: 135 us
  blocking collectives  85.6 us (63%)
  Pallas kernels  29 us (21%)
  starting transfers between devices  15.9 us (12%)
  waiting for transfers between devices  3.31 us (2%)
    all_to_all x7, blocking collectives, exchange(): return lax.all_to_all(rows, AXES, 0, 0, tiled=True)  85.6 us
    pallas_call x21, Pallas kernels, call(): pl.pallas_call(kernel, name=name, out_shape=out_shape, in_specs=specs or...  29 us
    ppermute x6, starting transfers between devices, body(): chip = lax.ppermute(search, AXES, on_chip)  11.7 us
    ppermute x6, starting transfers between devices, body(): far = lax.ppermute(search, AXES, off_chip)  4.17 us
    ppermute x6, waiting for transfers between devices, body(): chip = lax.ppermute(search, AXES, on_chip)  3.29 us
  transfers between devices with their start and end apart: 12, of which 6 were waited for; matrix products, arithmetic and copies ran while one was open for 0% of the time, Pallas kernels for 2%

profile of v3, /device:TPU:0, one launch (start us, length us, event | category | flops | bytes accessed | tf_op | source)
XLA Modules:
  0.0 134.7 jit_solution(2141654692135146906)
XLA Ops:
  0.6 3.2 %init.1 = (f32[40,384]{1,0:T(8,128)S(1)}, f32[40,384]{1,0:T(8,128)S(1)}, f32[32,128]{1,0:T(8,128)S(1)}, f32[40,384]{1,0:T(8,128)S(1)}, bf16[384,512]{1,0:T(8,128...) custom-call(s32[1]{0:T(128)} %bitcast.me_ref, ...), custom_call_target="tpu_custom_call" | custom-call | tf_op jit(solution)/shard_map/init/pallas_call | solution.py:357
  3.9 14.3 %all_to_all.77 = f32[32,1,128]{2,1,0:T(1,128)S(1)} all-to-all(f32[32,1,128]{2,1,0:T(1,128)S(1)} %bitcast.39), channel_id=1, replica_groups=mesh['dom'=8,'grp'=4] {'dom','grp'}, dimensions={0} | all-to-all | bytes 32768 | tf_op jit(solution)/shard_map/all_to_all | solution.py:408
  18.2 2.7 %precond0.1 = (f32[80,384]{1,0:T(8,128)S(1)}, f32[40,384]{1,0:T(8,128)S(1)}, f32[1,128]{1,0:T(1,128)S(1)}) custom-call(f32[32,128]{1,0:T(8,128)S(1)} %bitcast.32, f32[40,384]{1,0:T(8,128)S(1)} %get-tuple-element.55.vec_ref, f32[40,384]{1,0:T(8,128)S(1)} %get-tuple-element.56.mask_ref.refs_10_.refs_2_, ...), custom_call_target="tpu_custom_call" | custom-call | tf_op jit(solution)/shard_map/precond0/pallas_call | solution.py:357
  20.8 0.7 collective-permute-start.1
  21.5 2.0 %collective-permute-start = (f32[80,384]{1,0:T(8,128)S(1)}, f32[80,384]{1,0:T(8,128)S(1)}, u32[]{:S(2)}, u32[]{:S(2)}) collective-permute-start(f32[80,384]{1,0:T(8,128)S(1)} %get-tuple-element.59.z_ref.refs_0_.refs_7_), channel_id=1, source_target_pairs={{0,1},{1,0},{2,3},{3,2},{4,5},{5,4},{6,7},{7,6},{8,9},{9,8},{10,11... | collective-permute-start | bytes 368648 | tf_op jit(solution)/shard_map/ppermute | solution.py:428
  23.5 0.3 local.6
  23.8 0.0 collective-permute-done.1.far_ref.refs_2_
  23.8 0.6 collective-permute-done.chip_ref.refs_1_
  24.4 0.7 gain.1.refs_6_
  25.1 0.9 image0.1
  26.0 12.7 %all_to_all.78 = f32[32,1,128]{2,1,0:T(1,128)S(1)} all-to-all(f32[32,1,128]{2,1,0:T(1,128)S(1)} %bitcast.40), channel_id=1, replica_groups=mesh['dom'=8,'grp'=4] {'dom','grp'}, dimensions={0} | all-to-all | bytes 32768 | tf_op jit(solution)/shard_map/all_to_all | solution.py:408
  38.7 2.7 %precond1.1 = (f32[40,384]{1,0:T(8,128)S(1)}, f32[40,384]{1,0:T(8,128)S(1)}, f32[1,128]{1,0:T(1,128)S(1)}) custom-call(f32[32,128]{1,0:T(8,128)S(1)} %bitcast.33, f32[40,384]{1,0:T(8,128)S(1)} %get-tuple-element.70.refs_1_, f32[40,384]{1,0:T(8,128)S(1)} %get-tuple-element.56.mask_ref.refs_10_.refs_2_, ...), custom_call_target="tpu_custom_call" | custom-call | tf_op jit(solution)/shard_map/precond1/pallas_call | solution.py:357
  41.4 0.7 collective-permute-start.3
  42.1 2.0 %collective-permute-start.2 = (f32[40,384]{1,0:T(8,128)S(1)}, f32[40,384]{1,0:T(8,128)S(1)}, u32[]{:S(2)}, u32[]{:S(2)}) collective-permute-start(f32[40,384]{1,0:T(8,128)S(1)} %get-tuple-element.71.z_ref.refs_0_.refs_8_), channel_id=1, source_target_pairs={{0,1},{1,0},{2,3},{3,2},{4,5},{5,4},{6,7},{7,6},{8,9},{9,8},{10,11... | collective-permute-start | bytes 184328 | tf_op jit(solution)/shard_map/ppermute | solution.py:428
  44.0 0.3 local.7
  44.4 0.0 collective-permute-done.3.refs_2_
  44.4 0.5 collective-permute-done.2.refs_1_
  44.9 0.9 image1.1
  45.8 11.8 %all_to_all.79 = f32[32,1,128]{2,1,0:T(1,128)S(1)} all-to-all(f32[32,1,128]{2,1,0:T(1,128)S(1)} %bitcast.41), channel_id=1, replica_groups=mesh['dom'=8,'grp'=4] {'dom','grp'}, dimensions={0} | all-to-all | bytes 32768 | tf_op jit(solution)/shard_map/all_to_all | solution.py:408
  57.6 2.7 %precond2.1 = (f32[40,384]{1,0:T(8,128)S(1)}, f32[40,384]{1,0:T(8,128)S(1)}, f32[1,128]{1,0:T(1,128)S(1)}) custom-call(f32[32,128]{1,0:T(8,128)S(1)} %bitcast.34, f32[40,384]{1,0:T(8,128)S(1)} %get-tuple-element.76.refs_1_, f32[40,384]{1,0:T(8,128)S(1)} %get-tuple-element.56.mask_ref.refs_10_.refs_2_, ...), custom_call_target="tpu_custom_call" | custom-call | tf_op jit(solution)/shard_map/precond2/pallas_call | solution.py:357
  60.3 0.7 collective-permute-start.5
  60.9 2.0 %collective-permute-start.4 = (f32[40,384]{1,0:T(8,128)S(1)}, f32[40,384]{1,0:T(8,128)S(1)}, u32[]{:S(2)}, u32[]{:S(2)}) collective-permute-start(f32[40,384]{1,0:T(8,128)S(1)} %get-tuple-element.77.z_ref.refs_0_.refs_9_), channel_id=1, source_target_pairs={{0,1},{1,0},{2,3},{3,2},{4,5},{5,4},{6,7},{7,6},{8,9},{9,8},{10,11... | collective-permute-start | bytes 184328 | tf_op jit(solution)/shard_map/ppermute | solution.py:428
  62.9 0.3 local.8
  63.3 0.0 collective-permute-done.5.refs_2_
  63.3 0.5 collective-permute-done.4.refs_1_
  63.8 0.9 image2.1
  64.7 11.8 %all_to_all.80 = f32[32,1,128]{2,1,0:T(1,128)S(1)} all-to-all(f32[32,1,128]{2,1,0:T(1,128)S(1)} %bitcast.42), channel_id=1, replica_groups=mesh['dom'=8,'grp'=4] {'dom','grp'}, dimensions={0} | all-to-all | bytes 32768 | tf_op jit(solution)/shard_map/all_to_all | solution.py:408
  76.5 2.7 %precond3.1 = (f32[40,384]{1,0:T(8,128)S(1)}, f32[40,384]{1,0:T(8,128)S(1)}, f32[1,128]{1,0:T(1,128)S(1)}) custom-call(f32[32,128]{1,0:T(8,128)S(1)} %bitcast.35, f32[40,384]{1,0:T(8,128)S(1)} %get-tuple-element.82.refs_1_, f32[40,384]{1,0:T(8,128)S(1)} %get-tuple-element.56.mask_ref.refs_10_.refs_2_, ...), custom_call_target="tpu_custom_call" | custom-call | tf_op jit(solution)/shard_map/precond3/pallas_call | solution.py:357
  79.2 0.7 collective-permute-start.7
  79.8 2.0 %collective-permute-start.6 = (f32[40,384]{1,0:T(8,128)S(1)}, f32[40,384]{1,0:T(8,128)S(1)}, u32[]{:S(2)}, u32[]{:S(2)}) collective-permute-start(f32[40,384]{1,0:T(8,128)S(1)} %get-tuple-element.83.z_ref.refs_0_.refs_10_), channel_id=1, source_target_pairs={{0,1},{1,0},{2,3},{3,2},{4,5},{5,4},{6,7},{7,6},{8,9},{9,8},{10,11... | collective-permute-start | bytes 184328 | tf_op jit(solution)/shard_map/ppermute | solution.py:428
  81.8 0.3 local.9
  82.1 0.0 collective-permute-done.7.refs_2_
  82.1 0.5 collective-permute-done.6.refs_1_
  82.7 0.9 image3.1
  83.6 11.8 %all_to_all.81 = f32[32,1,128]{2,1,0:T(1,128)S(1)} all-to-all(f32[32,1,128]{2,1,0:T(1,128)S(1)} %bitcast.43), channel_id=1, replica_groups=mesh['dom'=8,'grp'=4] {'dom','grp'}, dimensions={0} | all-to-all | bytes 32768 | tf_op jit(solution)/shard_map/all_to_all | solution.py:408
  95.4 2.7 %precond4.1 = (f32[40,384]{1,0:T(8,128)S(1)}, f32[40,384]{1,0:T(8,128)S(1)}, f32[1,128]{1,0:T(1,128)S(1)}) custom-call(f32[32,128]{1,0:T(8,128)S(1)} %bitcast.36, f32[40,384]{1,0:T(8,128)S(1)} %get-tuple-element.88.refs_1_, f32[40,384]{1,0:T(8,128)S(1)} %get-tuple-element.56.mask_ref.refs_10_.refs_2_, ...), custom_call_target="tpu_custom_call" | custom-call | tf_op jit(solution)/shard_map/precond4/pallas_call | solution.py:357
  98.0 0.8 collective-permute-start.9
  98.9 2.0 %collective-permute-start.8 = (f32[40,384]{1,0:T(8,128)S(1)}, f32[40,384]{1,0:T(8,128)S(1)}, u32[]{:S(2)}, u32[]{:S(2)}) collective-permute-start(f32[40,384]{1,0:T(8,128)S(1)} %get-tuple-element.89.z_ref.refs_0_.refs_11_), channel_id=1, source_target_pairs={{0,1},{1,0},{2,3},{3,2},{4,5},{5,4},{6,7},{7,6},{8,9},{9,8},{10,11... | collective-permute-start | bytes 184328 | tf_op jit(solution)/shard_map/ppermute | solution.py:428
  100.8 0.3 local.10
  101.2 0.0 collective-permute-done.9.refs_2_
  101.2 0.5 collective-permute-done.8.refs_1_
  101.7 0.9 image4.1
  102.7 11.6 %all_to_all.82 = f32[32,1,128]{2,1,0:T(1,128)S(1)} all-to-all(f32[32,1,128]{2,1,0:T(1,128)S(1)} %bitcast.44), channel_id=1, replica_groups=mesh['dom'=8,'grp'=4] {'dom','grp'}, dimensions={0} | all-to-all | bytes 32768 | tf_op jit(solution)/shard_map/all_to_all | solution.py:408
  114.3 2.7 %precond5.1 = (f32[40,384]{1,0:T(8,128)S(1)}, f32[40,384]{1,0:T(8,128)S(1)}, f32[1,128]{1,0:T(1,128)S(1)}) custom-call(f32[32,128]{1,0:T(8,128)S(1)} %bitcast.31, f32[40,384]{1,0:T(8,128)S(1)} %get-tuple-element.94.refs_1_, f32[40,384]{1,0:T(8,128)S(1)} %get-tuple-element.56.mask_ref.refs_10_.refs_2_, ...), custom_call_target="tpu_custom_call" | custom-call | tf_op jit(solution)/shard_map/precond5/pallas_call | solution.py:357
  116.9 0.7 collective-permute-start.11
  117.6 2.0 %collective-permute-start.10 = (f32[40,384]{1,0:T(8,128)S(1)}, f32[40,384]{1,0:T(8,128)S(1)}, u32[]{:S(2)}, u32[]{:S(2)}) collective-permute-start(f32[40,384]{1,0:T(8,128)S(1)} %get-tuple-element.95.z_ref.refs_0_.refs_12_), channel_id=1, source_target_pairs={{0,1},{1,0},{2,3},{3,2},{4,5},{5,4},{6,7},{7,6},{8,9},{9,8},{10,11... | collective-permute-start | bytes 184328 | tf_op jit(solution)/shard_map/ppermute | solution.py:428
  119.6 0.3 local.11
  119.9 0.0 collective-permute-done.11.refs_2_
  119.9 0.5 collective-permute-done.10.refs_1_
  120.5 1.5 %image5.1 = (f32[40,384]{1,0:T(8,128)}, f32[32,128]{1,0:T(8,128)S(1)}) custom-call(f32[40,384]{1,0:T(8,128)S(1)} %get-tuple-element.95.z_ref.refs_0_.refs_12_, f32[40,384]{1,0:T(8,128)S(1)} %collective-permute-done.10.refs_1_, f32[40,384]{1,0:T(8,128)S(1)} %collective-permute-done.11.refs_2_, bf16[384,512]{1,0:T(8,128)(2,1)S(1)} %get-tuple-element.60.hot_ref.refs_3_, ...), custom_call_target="tpu_custom_call" | custom-call | tf_op jit(solution)/shard_map/image5/pallas_call | solution.py:357
  121.9 11.8 %all_to_all.83 = f32[32,1,128]{2,1,0:T(1,128)S(1)} all-to-all(f32[32,1,128]{2,1,0:T(1,128)S(1)} %bitcast.38), channel_id=1, replica_groups=mesh['dom'=8,'grp'=4] {'dom','grp'}, dimensions={0} | all-to-all | bytes 32768 | tf_op jit(solution)/shard_map/all_to_all | solution.py:408
  133.7 1.0 finish.1
Async XLA Ops:
  20.8 3.0 %collective-permute-start.1 = (f32[80,384]{1,0:T(8,128)S(1)}, f32[80,384]{1,0:T(8,128)S(1)}, u32[]{:S(2)}, u32[]{:S(2)}) collective-permute-start(f32[80,384]{1,0:T(8,128)S(1)} %get-tuple-element.59.z_ref.refs_0_.refs_7_), channel_id=1, source_target_pairs={{1,2},{3,4},{5,6},{7,8},{9,10},{11,12},{13,14},{15,16},{17,18},{19... | collective-permute-start | bytes 368648 | tf_op jit(solution)/shard_map/ppermute | solution.py:427
  21.5 2.9 %collective-permute-start = (f32[80,384]{1,0:T(8,128)S(1)}, f32[80,384]{1,0:T(8,128)S(1)}, u32[]{:S(2)}, u32[]{:S(2)}) collective-permute-start(f32[80,384]{1,0:T(8,128)S(1)} %get-tuple-element.59.z_ref.refs_0_.refs_7_), channel_id=1, source_target_pairs={{0,1},{1,0},{2,3},{3,2},{4,5},{5,4},{6,7},{7,6},{8,9},{9,8},{10,11... | collective-permute-start | bytes 368648 | tf_op jit(solution)/shard_map/ppermute | solution.py:428
  41.4 3.0 %collective-permute-start.3 = (f32[40,384]{1,0:T(8,128)S(1)}, f32[40,384]{1,0:T(8,128)S(1)}, u32[]{:S(2)}, u32[]{:S(2)}) collective-permute-start(f32[40,384]{1,0:T(8,128)S(1)} %get-tuple-element.71.z_ref.refs_0_.refs_8_), channel_id=1, source_target_pairs={{1,2},{3,4},{5,6},{7,8},{9,10},{11,12},{13,14},{15,16},{17,18},{19... | collective-permute-start | bytes 184328 | tf_op jit(solution)/shard_map/ppermute | solution.py:427
  42.1 2.9 %collective-permute-start.2 = (f32[40,384]{1,0:T(8,128)S(1)}, f32[40,384]{1,0:T(8,128)S(1)}, u32[]{:S(2)}, u32[]{:S(2)}) collective-permute-start(f32[40,384]{1,0:T(8,128)S(1)} %get-tuple-element.71.z_ref.refs_0_.refs_8_), channel_id=1, source_target_pairs={{0,1},{1,0},{2,3},{3,2},{4,5},{5,4},{6,7},{7,6},{8,9},{9,8},{10,11... | collective-permute-start | bytes 184328 | tf_op jit(solution)/shard_map/ppermute | solution.py:428
  60.3 3.0 %collective-permute-start.5 = (f32[40,384]{1,0:T(8,128)S(1)}, f32[40,384]{1,0:T(8,128)S(1)}, u32[]{:S(2)}, u32[]{:S(2)}) collective-permute-start(f32[40,384]{1,0:T(8,128)S(1)} %get-tuple-element.77.z_ref.refs_0_.refs_9_), channel_id=1, source_target_pairs={{1,2},{3,4},{5,6},{7,8},{9,10},{11,12},{13,14},{15,16},{17,18},{19... | collective-permute-start | bytes 184328 | tf_op jit(solution)/shard_map/ppermute | solution.py:427
  60.9 2.9 %collective-permute-start.4 = (f32[40,384]{1,0:T(8,128)S(1)}, f32[40,384]{1,0:T(8,128)S(1)}, u32[]{:S(2)}, u32[]{:S(2)}) collective-permute-start(f32[40,384]{1,0:T(8,128)S(1)} %get-tuple-element.77.z_ref.refs_0_.refs_9_), channel_id=1, source_target_pairs={{0,1},{1,0},{2,3},{3,2},{4,5},{5,4},{6,7},{7,6},{8,9},{9,8},{10,11... | collective-permute-start | bytes 184328 | tf_op jit(solution)/shard_map/ppermute | solution.py:428
  79.2 3.0 %collective-permute-start.7 = (f32[40,384]{1,0:T(8,128)S(1)}, f32[40,384]{1,0:T(8,128)S(1)}, u32[]{:S(2)}, u32[]{:S(2)}) collective-permute-start(f32[40,384]{1,0:T(8,128)S(1)} %get-tuple-element.83.z_ref.refs_0_.refs_10_), channel_id=1, source_target_pairs={{1,2},{3,4},{5,6},{7,8},{9,10},{11,12},{13,14},{15,16},{17,18},{19... | collective-permute-start | bytes 184328 | tf_op jit(solution)/shard_map/ppermute | solution.py:427
  79.8 2.9 %collective-permute-start.6 = (f32[40,384]{1,0:T(8,128)S(1)}, f32[40,384]{1,0:T(8,128)S(1)}, u32[]{:S(2)}, u32[]{:S(2)}) collective-permute-start(f32[40,384]{1,0:T(8,128)S(1)} %get-tuple-element.83.z_ref.refs_0_.refs_10_), channel_id=1, source_target_pairs={{0,1},{1,0},{2,3},{3,2},{4,5},{5,4},{6,7},{7,6},{8,9},{9,8},{10,11... | collective-permute-start | bytes 184328 | tf_op jit(solution)/shard_map/ppermute | solution.py:428
  98.0 3.2 %collective-permute-start.9 = (f32[40,384]{1,0:T(8,128)S(1)}, f32[40,384]{1,0:T(8,128)S(1)}, u32[]{:S(2)}, u32[]{:S(2)}) collective-permute-start(f32[40,384]{1,0:T(8,128)S(1)} %get-tuple-element.89.z_ref.refs_0_.refs_11_), channel_id=1, source_target_pairs={{1,2},{3,4},{5,6},{7,8},{9,10},{11,12},{13,14},{15,16},{17,18},{19... | collective-permute-start | bytes 184328 | tf_op jit(solution)/shard_map/ppermute | solution.py:427
  98.9 2.9 %collective-permute-start.8 = (f32[40,384]{1,0:T(8,128)S(1)}, f32[40,384]{1,0:T(8,128)S(1)}, u32[]{:S(2)}, u32[]{:S(2)}) collective-permute-start(f32[40,384]{1,0:T(8,128)S(1)} %get-tuple-element.89.z_ref.refs_0_.refs_11_), channel_id=1, source_target_pairs={{0,1},{1,0},{2,3},{3,2},{4,5},{5,4},{6,7},{7,6},{8,9},{9,8},{10,11... | collective-permute-start | bytes 184328 | tf_op jit(solution)/shard_map/ppermute | solution.py:428
  116.9 3.0 %collective-permute-start.11 = (f32[40,384]{1,0:T(8,128)S(1)}, f32[40,384]{1,0:T(8,128)S(1)}, u32[]{:S(2)}, u32[]{:S(2)}) collective-permute-start(f32[40,384]{1,0:T(8,128)S(1)} %get-tuple-element.95.z_ref.refs_0_.refs_12_), channel_id=1, source_target_pairs={{1,2},{3,4},{5,6},{7,8},{9,10},{11,12},{13,14},{15,16},{17,18},{19... | collective-permute-start | bytes 184328 | tf_op jit(solution)/shard_map/ppermute | solution.py:427
  117.6 2.9 %collective-permute-start.10 = (f32[40,384]{1,0:T(8,128)S(1)}, f32[40,384]{1,0:T(8,128)S(1)}, u32[]{:S(2)}, u32[]{:S(2)}) collective-permute-start(f32[40,384]{1,0:T(8,128)S(1)} %get-tuple-element.95.z_ref.refs_0_.refs_12_), channel_id=1, source_target_pairs={{0,1},{1,0},{2,3},{3,2},{4,5},{5,4},{6,7},{7,6},{8,9},{9,8},{10,11... | collective-permute-start | bytes 184328 | tf_op jit(solution)/shard_map/ppermute | solution.py:428

commit v4 on v3

--- a/solution.py
+++ b/solution.py
@@ -80,8 +80,7 @@
 
 def total_scalars(red, count):
     row = jnp.sum(red, axis=0, keepdims=True)
-    lane = iota((1, 128), 1)
-    return [jnp.sum(jnp.where(lane == i, row, 0.0), axis=1, keepdims=True) for i in range(count)]
+    return [row[:, i : i + 1] for i in range(count)]
 
 
 def fetch(pairs, sems):
@@ -113,26 +112,24 @@
     me = me_ref[0]
     nbr = nbr_ref[...]
     rel = jnp.where(nbr >= 0, nbr - me * ne + ne, -4 * ne)
-    cols = jnp.concatenate(
-        [piece for f in range(4) for piece in (rel[f : f + 1], rel[f : f + 1] + 3 * ne * (rel[f : f + 1] >= 0).astype(jnp.int32))],
-        axis=1,
-    )
-    rows = iota((3 * sz.pair, 4 * sz.pair), 0)
-    block = rows // sz.pair
-    even = lax.rem(me, 2) == 0
-    chip_side = jnp.where(even, 2, 0)
-    side = jnp.where(block == 0, 1, jnp.where(block == 1, chip_side, 2 - chip_side))
-    inner = rows - block * sz.pair
-    parity = (inner >= ne).astype(jnp.int32)
-    code = side * ne + inner - parity * ne + 3 * ne * parity
-    hot_ref[...] = (code == cols).astype(F32).astype(BF16)
-
-    face = face_ref[...]
-    orient = orient_ref[...]
+    face, orient = face_ref[...], orient_ref[...]
     flip = (orient >= 3).astype(jnp.int32)
-    choice = flip * 4 + face
-    turn = orient - 3 * flip
-    sel_ref[...] = jnp.concatenate([jnp.concatenate([choice, turn], axis=0)] * nv, axis=1)
+    choice, turn = flip * 4 + face, orient - 3 * flip
+
+    def by_face(x):
+        return jnp.concatenate([x[f : f + 1] for f in range(4)], axis=1)
+
+    sel_ref[...] = jnp.concatenate([by_face(choice), by_face(turn)], axis=0)
+    cols = by_face(rel)
+    rows = iota((4 * ne, 4 * ne), 0)
+    block = rows // ne
+    inner = rows - block * ne
+    chip_side = jnp.where(lax.rem(me, 2) == 0, 2, 0)
+    for parity in range(2):
+        own_block, chip_block, far_block = parity, 1 - parity, 2 + parity
+        side = jnp.where(block == own_block, 1, jnp.where(block == chip_block, chip_side, 2 - chip_side))
+        code = jnp.where(block == 5 - far_block, -ne, side * ne + inner)
+        hot_ref[parity] = (code == cols).astype(F32).astype(BF16)
 
     for k in range(3):
         pieces = []
@@ -168,12 +165,12 @@
     nb, ne, nv, width = sz.nb, sz.ne, sz.nv, sz.width
     tall = jnp.concatenate([vec[:nb, v * ne : (v + 1) * ne] for v in range(nv)], axis=0)
     turned = pad_rows(tall, CHUNK).T
-    amount = lax.rem(iota((ne, 1), 0) * width, CHUNK)
-    bit = 1
-    while bit < CHUNK:
-        if any(e * width % CHUNK & bit for e in range(ne)):
-            turned = jnp.where((amount & bit) != 0, pltpu.roll(turned, bit, 1), turned)
-        bit *= 2
+    turned = jnp.concatenate(
+        [pltpu.roll(turned[g : g + 8], g * width % CHUNK, 1) if g else turned[:8] for g in range(0, ne, 8)], axis=0
+    )
+    row = iota((ne, 1), 0)
+    for bit in (1, 2, 4):
+        turned = jnp.where((row & bit) != 0, pltpu.roll(turned, bit * width % CHUNK, 1), turned)
     total = ne * width
     acc = [jnp.zeros((8, width), F32)] * (ne // 8)
     for low in range(0, total, CHUNK):
@@ -195,7 +192,7 @@
 
 def precond_start_kernel(sz, red_ref, vec_ref, mask_ref, blocks_ref, state_ref, z_ref, v_ref, h_ref):
     norm = jnp.sqrt(total_scalars(red_ref[...], 1)[0] + EPSILON)
-    new = vec_ref[...] / norm
+    new = vec_ref[...] * (1.0 / norm)
     v_ref[...] = new
     h_ref[...] = partial_rows([norm], 1)
     z_ref[: sz.nbp] = apply_blocks(sz, new, mask_ref[...], blocks_ref)
@@ -213,7 +210,7 @@
         vec = vec - h * b[...]
         square = square - h * h
     norm = jnp.sqrt(square + EPSILON)
-    new = vec / norm
+    new = vec * (1.0 / norm)
     v_ref[...] = new
     h_ref[...] = partial_rows(proj + [norm], 1)
     z_ref[...] = apply_blocks(sz, new, mask_ref[...], blocks_ref)
@@ -240,41 +237,50 @@
 
 
 def neighbour_traces(sz, own, chip, far, hot_ref, near_ref, sel_ref):
-    nbp, nqp, pair = sz.nbp, sz.nqp, sz.pair
-    parts = [split3(x) for x in (own, chip, far)]
-    pairs = sz.lanes // pair
-    lhs = jnp.concatenate(
-        [
-            jnp.concatenate([parts[side][n][:, p * pair : (p + 1) * pair] for side in range(3)], axis=1)
-            for n in range(3)
-            for p in range(pairs)
-        ],
-        axis=0,
-    ).astype(BF16)
-    got = dot(lhs, hot_ref[...])
-    result = []
-    for f in range(4):
-        picked = [
-            jnp.concatenate(
-                [
-                    got[(n * pairs + p) * nbp : (n * pairs + p + 1) * nbp, f * pair : (f + 1) * pair]
-                    for p in range(pairs)
-                ],
-                axis=1,
-            )
-            for n in range(3)
-        ]
-        every = dot(near_ref[...], stack_rhs(picked, 0))
-        choice = sel_ref[f : f + 1, :]
-        turn = sel_ref[4 + f : 5 + f, :]
-        tr = every[:nqp]
+    nbp, nqp, ne, pair = sz.nbp, sz.nqp, sz.ne, sz.pair
+    pairs, cols = sz.lanes // pair, 4 * ne
+    low_half = iota((1, pair), 1) < ne
+    owns, chips, fars = split3(own), split3(chip), split3(far)
+    lhs = ([], [])
+    for n in range(3):
+        for p in range(pairs):
+            mine, theirs, away = (x[n][:, p * pair : (p + 1) * pair] for x in (owns, chips, fars))
+            theirs = pltpu.roll(theirs, ne, 1)
+            lhs[0].append(jnp.concatenate([jnp.where(low_half, mine, theirs), away], axis=1))
+            lhs[1].append(jnp.concatenate([jnp.where(low_half, theirs, mine), away], axis=1))
+    got = [dot(jnp.concatenate(lhs[i], axis=0).astype(BF16), hot_ref[i]) for i in range(2)]
+    picked = [
+        jnp.concatenate(
+            [got[v % 2][(n * pairs + v // 2) * nbp : (n * pairs + v // 2 + 1) * nbp] for v in range(sz.nv)], axis=1
+        )
+        for n in range(3)
+    ]
+    every = dot(near_ref[...], stack_rhs(picked, 0))
+    choice, turn = sel_ref[0:1, :], sel_ref[1:2, :]
+    is_choice = [choice == g for g in range(8)]
+    nq, third = sz.nq, sz.nq // 3
+    seen = []
+    for v in range(sz.nv):
+        mine = every[:, v * cols : (v + 1) * cols]
+        tr = mine[:nqp]
         for g in range(1, 8):
-            tr = jnp.where(choice == g, every[g * nqp : (g + 1) * nqp], tr)
-        nq, third = sz.nq, sz.nq // 3
+            tr = jnp.where(is_choice[g], mine[g * nqp : (g + 1) * nqp], tr)
         fill = tr[nq:]
         once = jnp.concatenate([tr[third:nq], tr[:third], fill], axis=0)
         twice = jnp.concatenate([tr[2 * third : nq], tr[: 2 * third], fill], axis=0)
-        result.append(jnp.where(turn == 0, tr, jnp.where(turn == 1, once, twice)))
+        seen.append(jnp.where(turn == 0, tr, jnp.where(turn == 1, once, twice)))
+    result = []
+    for f in range(4):
+        start = f // 2 * pair
+        blocks = []
+        for p in range(pairs):
+            first, second = (seen[2 * p + i][:, start : start + pair] for i in range(2))
+            if f % 2 == 0:
+                second = pltpu.roll(second, ne, 1)
+            else:
+                first = pltpu.roll(first, ne, 1)
+            blocks.append(jnp.where(low_half, first, second))
+        result.append(jnp.concatenate(blocks, axis=1))
     return jnp.concatenate(result, axis=0)
 
 
@@ -392,9 +398,9 @@
         "init",
         (
             wide, wide, parts, wide,
-            shape(3 * sz.pair, 4 * sz.pair, dtype=BF16),
+            shape(2, 4 * ne, 4 * ne, dtype=BF16),
             shape(4, nv, lanes),
-            shape(8, lanes, dtype=jnp.int32),
+            shape(2, 4 * ne, dtype=jnp.int32),
             shape(4 * nqp + 3 * nbp, 6 * nbp, dtype=BF16),
             shape(8 * nqp, 6 * nbp, dtype=BF16),
             shape(nbp, 24 * nqp, dtype=BF16),

time: 135 us -> 134 us (level)
  no operation moved by 1% of the time
where the time goes in v4:
time: 134 us; the launch traced here: 133 us
  blocking collectives  85.8 us (64%)
  Pallas kernels  27.8 us (21%)
  starting transfers between devices  15.7 us (12%)
  waiting for transfers between devices  3.3 us (2%)
    all_to_all x7, blocking collectives, exchange(): return lax.all_to_all(rows, AXES, 0, 0, tiled=True)  85.8 us
    pallas_call x21, Pallas kernels, call(): pl.pallas_call(kernel, name=name, out_shape=out_shape, in_specs=specs or...  27.8 us
    ppermute x6, starting transfers between devices, body(): chip = lax.ppermute(search, AXES, on_chip)  11.7 us
    ppermute x6, starting transfers between devices, body(): far = lax.ppermute(search, AXES, off_chip)  3.99 us
    ppermute x6, waiting for transfers between devices, body(): chip = lax.ppermute(search, AXES, on_chip)  3.29 us
  transfers between devices with their start and end apart: 12, of which 6 were waited for; matrix products, arithmetic and copies ran while one was open for 0% of the time, Pallas kernels for 2%

profile of v4, /device:TPU:0, one launch (start us, length us, event | category | flops | bytes accessed | tf_op | source)
XLA Modules:
  0.0 133.4 jit_solution(9353198606440785256)
XLA Ops:
  0.6 3.1 %init.1 = (f32[40,384]{1,0:T(8,128)S(1)}, f32[40,384]{1,0:T(8,128)S(1)}, f32[32,128]{1,0:T(8,128)S(1)}, f32[40,384]{1,0:T(8,128)S(1)}, bf16[2,256,256]{2,1,0:T(8...) custom-call(s32[1]{0:T(128)} %bitcast.me_ref, ...), custom_call_target="tpu_custom_call" | custom-call | tf_op jit(solution)/shard_map/init/pallas_call | solution.py:363
  3.7 14.3 %all_to_all.77 = f32[32,1,128]{2,1,0:T(1,128)S(1)} all-to-all(f32[32,1,128]{2,1,0:T(1,128)S(1)} %bitcast.39), channel_id=1, replica_groups=mesh['dom'=8,'grp'=4] {'dom','grp'}, dimensions={0} | all-to-all | bytes 32768 | tf_op jit(solution)/shard_map/all_to_all | solution.py:414
  18.0 2.3 %precond0.1 = (f32[80,384]{1,0:T(8,128)S(1)}, f32[40,384]{1,0:T(8,128)S(1)}, f32[1,128]{1,0:T(1,128)S(1)}) custom-call(f32[32,128]{1,0:T(8,128)S(1)} %bitcast.32, f32[40,384]{1,0:T(8,128)S(1)} %get-tuple-element.55.vec_ref, f32[40,384]{1,0:T(8,128)S(1)} %get-tuple-element.56.mask_ref.refs_10_.refs_2_, ...), custom_call_target="tpu_custom_call" | custom-call | tf_op jit(solution)/shard_map/precond0/pallas_call | solution.py:363
  20.4 0.7 collective-permute-start.1
  21.1 2.0 %collective-permute-start = (f32[80,384]{1,0:T(8,128)S(1)}, f32[80,384]{1,0:T(8,128)S(1)}, u32[]{:S(2)}, u32[]{:S(2)}) collective-permute-start(f32[80,384]{1,0:T(8,128)S(1)} %get-tuple-element.59.z_ref.refs_0_.refs_7_), channel_id=1, source_target_pairs={{0,1},{1,0},{2,3},{3,2},{4,5},{5,4},{6,7},{7,6},{8,9},{9,8},{10,11... | collective-permute-start | bytes 368648 | tf_op jit(solution)/shard_map/ppermute | solution.py:434
  23.0 0.3 local.6
  23.4 0.0 collective-permute-done.1.far_ref.refs_2_
  23.4 0.6 collective-permute-done.chip_ref.refs_1_
  24.0 0.6 gain.1.refs_6_
  24.6 0.9 image0.1
  25.5 12.7 %all_to_all.78 = f32[32,1,128]{2,1,0:T(1,128)S(1)} all-to-all(f32[32,1,128]{2,1,0:T(1,128)S(1)} %bitcast.40), channel_id=1, replica_groups=mesh['dom'=8,'grp'=4] {'dom','grp'}, dimensions={0} | all-to-all | bytes 32768 | tf_op jit(solution)/shard_map/all_to_all | solution.py:414
  38.2 2.4 %precond1.1 = (f32[40,384]{1,0:T(8,128)S(1)}, f32[40,384]{1,0:T(8,128)S(1)}, f32[1,128]{1,0:T(1,128)S(1)}) custom-call(f32[32,128]{1,0:T(8,128)S(1)} %bitcast.33, f32[40,384]{1,0:T(8,128)S(1)} %get-tuple-element.70.refs_1_, f32[40,384]{1,0:T(8,128)S(1)} %get-tuple-element.56.mask_ref.refs_10_.refs_2_, ...), custom_call_target="tpu_custom_call" | custom-call | tf_op jit(solution)/shard_map/precond1/pallas_call | solution.py:363
  40.7 0.7 collective-permute-start.3
  41.3 2.0 %collective-permute-start.2 = (f32[40,384]{1,0:T(8,128)S(1)}, f32[40,384]{1,0:T(8,128)S(1)}, u32[]{:S(2)}, u32[]{:S(2)}) collective-permute-start(f32[40,384]{1,0:T(8,128)S(1)} %get-tuple-element.71.z_ref.refs_0_.refs_8_), channel_id=1, source_target_pairs={{0,1},{1,0},{2,3},{3,2},{4,5},{5,4},{6,7},{7,6},{8,9},{9,8},{10,11... | collective-permute-start | bytes 184328 | tf_op jit(solution)/shard_map/ppermute | solution.py:434
  43.3 0.3 local.7
  43.6 0.0 collective-permute-done.3.refs_2_
  43.6 0.5 collective-permute-done.2.refs_1_
  44.2 0.9 image1.1
  45.1 11.8 %all_to_all.79 = f32[32,1,128]{2,1,0:T(1,128)S(1)} all-to-all(f32[32,1,128]{2,1,0:T(1,128)S(1)} %bitcast.41), channel_id=1, replica_groups=mesh['dom'=8,'grp'=4] {'dom','grp'}, dimensions={0} | all-to-all | bytes 32768 | tf_op jit(solution)/shard_map/all_to_all | solution.py:414
  56.8 2.5 %precond2.1 = (f32[40,384]{1,0:T(8,128)S(1)}, f32[40,384]{1,0:T(8,128)S(1)}, f32[1,128]{1,0:T(1,128)S(1)}) custom-call(f32[32,128]{1,0:T(8,128)S(1)} %bitcast.34, f32[40,384]{1,0:T(8,128)S(1)} %get-tuple-element.76.refs_1_, f32[40,384]{1,0:T(8,128)S(1)} %get-tuple-element.56.mask_ref.refs_10_.refs_2_, ...), custom_call_target="tpu_custom_call" | custom-call | tf_op jit(solution)/shard_map/precond2/pallas_call | solution.py:363
  59.3 0.7 collective-permute-start.5
  59.9 2.0 %collective-permute-start.4 = (f32[40,384]{1,0:T(8,128)S(1)}, f32[40,384]{1,0:T(8,128)S(1)}, u32[]{:S(2)}, u32[]{:S(2)}) collective-permute-start(f32[40,384]{1,0:T(8,128)S(1)} %get-tuple-element.77.z_ref.refs_0_.refs_9_), channel_id=1, source_target_pairs={{0,1},{1,0},{2,3},{3,2},{4,5},{5,4},{6,7},{7,6},{8,9},{9,8},{10,11... | collective-permute-start | bytes 184328 | tf_op jit(solution)/shard_map/ppermute | solution.py:434
  61.9 0.3 local.8
  62.2 0.0 collective-permute-done.5.refs_2_
  62.3 0.5 collective-permute-done.4.refs_1_
  62.8 0.9 image2.1
  63.7 11.8 %all_to_all.80 = f32[32,1,128]{2,1,0:T(1,128)S(1)} all-to-all(f32[32,1,128]{2,1,0:T(1,128)S(1)} %bitcast.42), channel_id=1, replica_groups=mesh['dom'=8,'grp'=4] {'dom','grp'}, dimensions={0} | all-to-all | bytes 32768 | tf_op jit(solution)/shard_map/all_to_all | solution.py:414
  75.4 2.5 %precond3.1 = (f32[40,384]{1,0:T(8,128)S(1)}, f32[40,384]{1,0:T(8,128)S(1)}, f32[1,128]{1,0:T(1,128)S(1)}) custom-call(f32[32,128]{1,0:T(8,128)S(1)} %bitcast.35, f32[40,384]{1,0:T(8,128)S(1)} %get-tuple-element.82.refs_1_, f32[40,384]{1,0:T(8,128)S(1)} %get-tuple-element.56.mask_ref.refs_10_.refs_2_, ...), custom_call_target="tpu_custom_call" | custom-call | tf_op jit(solution)/shard_map/precond3/pallas_call | solution.py:363
  77.9 0.7 collective-permute-start.7
  78.5 2.0 %collective-permute-start.6 = (f32[40,384]{1,0:T(8,128)S(1)}, f32[40,384]{1,0:T(8,128)S(1)}, u32[]{:S(2)}, u32[]{:S(2)}) collective-permute-start(f32[40,384]{1,0:T(8,128)S(1)} %get-tuple-element.83.z_ref.refs_0_.refs_10_), channel_id=1, source_target_pairs={{0,1},{1,0},{2,3},{3,2},{4,5},{5,4},{6,7},{7,6},{8,9},{9,8},{10,11... | collective-permute-start | bytes 184328 | tf_op jit(solution)/shard_map/ppermute | solution.py:434
  80.5 0.3 local.9
  80.9 0.0 collective-permute-done.7.refs_2_
  80.9 0.5 collective-permute-done.6.refs_1_
  81.4 0.9 image3.1
  82.3 11.8 %all_to_all.81 = f32[32,1,128]{2,1,0:T(1,128)S(1)} all-to-all(f32[32,1,128]{2,1,0:T(1,128)S(1)} %bitcast.43), channel_id=1, replica_groups=mesh['dom'=8,'grp'=4] {'dom','grp'}, dimensions={0} | all-to-all | bytes 32768 | tf_op jit(solution)/shard_map/all_to_all | solution.py:414
  94.0 2.5 %precond4.1 = (f32[40,384]{1,0:T(8,128)S(1)}, f32[40,384]{1,0:T(8,128)S(1)}, f32[1,128]{1,0:T(1,128)S(1)}) custom-call(f32[32,128]{1,0:T(8,128)S(1)} %bitcast.36, f32[40,384]{1,0:T(8,128)S(1)} %get-tuple-element.88.refs_1_, f32[40,384]{1,0:T(8,128)S(1)} %get-tuple-element.56.mask_ref.refs_10_.refs_2_, ...), custom_call_target="tpu_custom_call" | custom-call | tf_op jit(solution)/shard_map/precond4/pallas_call | solution.py:363
  96.5 0.7 collective-permute-start.9
  97.2 2.0 %collective-permute-start.8 = (f32[40,384]{1,0:T(8,128)S(1)}, f32[40,384]{1,0:T(8,128)S(1)}, u32[]{:S(2)}, u32[]{:S(2)}) collective-permute-start(f32[40,384]{1,0:T(8,128)S(1)} %get-tuple-element.89.z_ref.refs_0_.refs_11_), channel_id=1, source_target_pairs={{0,1},{1,0},{2,3},{3,2},{4,5},{5,4},{6,7},{7,6},{8,9},{9,8},{10,11... | collective-permute-start | bytes 184328 | tf_op jit(solution)/shard_map/ppermute | solution.py:434
  99.1 0.3 local.10
  99.5 0.0 collective-permute-done.9.refs_2_
  99.5 0.5 collective-permute-done.8.refs_1_
  100.0 0.9 image4.1
  100.9 11.8 %all_to_all.82 = f32[32,1,128]{2,1,0:T(1,128)S(1)} all-to-all(f32[32,1,128]{2,1,0:T(1,128)S(1)} %bitcast.44), channel_id=1, replica_groups=mesh['dom'=8,'grp'=4] {'dom','grp'}, dimensions={0} | all-to-all | bytes 32768 | tf_op jit(solution)/shard_map/all_to_all | solution.py:414
  112.7 2.5 %precond5.1 = (f32[40,384]{1,0:T(8,128)S(1)}, f32[40,384]{1,0:T(8,128)S(1)}, f32[1,128]{1,0:T(1,128)S(1)}) custom-call(f32[32,128]{1,0:T(8,128)S(1)} %bitcast.31, f32[40,384]{1,0:T(8,128)S(1)} %get-tuple-element.94.refs_1_, f32[40,384]{1,0:T(8,128)S(1)} %get-tuple-element.56.mask_ref.refs_10_.refs_2_, ...), custom_call_target="tpu_custom_call" | custom-call | tf_op jit(solution)/shard_map/precond5/pallas_call | solution.py:363
  115.1 0.7 collective-permute-start.11
  115.8 2.0 %collective-permute-start.10 = (f32[40,384]{1,0:T(8,128)S(1)}, f32[40,384]{1,0:T(8,128)S(1)}, u32[]{:S(2)}, u32[]{:S(2)}) collective-permute-start(f32[40,384]{1,0:T(8,128)S(1)} %get-tuple-element.95.z_ref.refs_0_.refs_12_), channel_id=1, source_target_pairs={{0,1},{1,0},{2,3},{3,2},{4,5},{5,4},{6,7},{7,6},{8,9},{9,8},{10,11... | collective-permute-start | bytes 184328 | tf_op jit(solution)/shard_map/ppermute | solution.py:434
  117.7 0.3 local.11
  118.1 0.0 collective-permute-done.11.refs_2_
  118.1 0.5 collective-permute-done.10.refs_1_
  118.6 1.4 %image5.1 = (f32[40,384]{1,0:T(8,128)}, f32[32,128]{1,0:T(8,128)S(1)}) custom-call(f32[40,384]{1,0:T(8,128)S(1)} %get-tuple-element.95.z_ref.refs_0_.refs_12_, f32[40,384]{1,0:T(8,128)S(1)} %collective-permute-done.10.refs_1_, f32[40,384]{1,0:T(8,128)S(1)} %collective-permute-done.11.refs_2_, bf16[2,256,256]{2,1,0:T(8,128)(2,1)S(1)} %get-tuple-element.60.hot_ref.refs_3_, ...), custom_call_target="tpu_custom_call" | custom-call | tf_op jit(solution)/shard_map/image5/pallas_call | solution.py:363
  120.1 11.8 %all_to_all.83 = f32[32,1,128]{2,1,0:T(1,128)S(1)} all-to-all(f32[32,1,128]{2,1,0:T(1,128)S(1)} %bitcast.38), channel_id=1, replica_groups=mesh['dom'=8,'grp'=4] {'dom','grp'}, dimensions={0} | all-to-all | bytes 32768 | tf_op jit(solution)/shard_map/all_to_all | solution.py:414
  131.8 1.6 %finish.1 = (f32[6,35,64]{2,1,0:T(8,128)}, f32[7,6]{1,0:T(8,128)}) custom-call(f32[32,128]{1,0:T(8,128)S(1)} %bitcast.37, f32[1,128]{1,0:T(1,128)S(1)} %get-tuple-element.100.refs_1_, f32[1,128]{1,0:T(1,128)S(1)} %get-tuple-element.101.refs_2_, f32[1,128]{1,0:T(1,128)S(1)} %get-tuple-element.102.refs_3_, f32[1,128]{1,0:T(1,128)S(1)} %get-tuple-element.103.refs_4_, ...), custom_call_target="tpu_custom_call" | custom-call | tf_op jit(solution)/shard_map/finish/pallas_call | solution.py:363
Async XLA Ops:
  20.4 3.0 %collective-permute-start.1 = (f32[80,384]{1,0:T(8,128)S(1)}, f32[80,384]{1,0:T(8,128)S(1)}, u32[]{:S(2)}, u32[]{:S(2)}) collective-permute-start(f32[80,384]{1,0:T(8,128)S(1)} %get-tuple-element.59.z_ref.refs_0_.refs_7_), channel_id=1, source_target_pairs={{1,2},{3,4},{5,6},{7,8},{9,10},{11,12},{13,14},{15,16},{17,18},{19... | collective-permute-start | bytes 368648 | tf_op jit(solution)/shard_map/ppermute | solution.py:433
  21.1 2.9 %collective-permute-start = (f32[80,384]{1,0:T(8,128)S(1)}, f32[80,384]{1,0:T(8,128)S(1)}, u32[]{:S(2)}, u32[]{:S(2)}) collective-permute-start(f32[80,384]{1,0:T(8,128)S(1)} %get-tuple-element.59.z_ref.refs_0_.refs_7_), channel_id=1, source_target_pairs={{0,1},{1,0},{2,3},{3,2},{4,5},{5,4},{6,7},{7,6},{8,9},{9,8},{10,11... | collective-permute-start | bytes 368648 | tf_op jit(solution)/shard_map/ppermute | solution.py:434
  40.7 3.0 %collective-permute-start.3 = (f32[40,384]{1,0:T(8,128)S(1)}, f32[40,384]{1,0:T(8,128)S(1)}, u32[]{:S(2)}, u32[]{:S(2)}) collective-permute-start(f32[40,384]{1,0:T(8,128)S(1)} %get-tuple-element.71.z_ref.refs_0_.refs_8_), channel_id=1, source_target_pairs={{1,2},{3,4},{5,6},{7,8},{9,10},{11,12},{13,14},{15,16},{17,18},{19... | collective-permute-start | bytes 184328 | tf_op jit(solution)/shard_map/ppermute | solution.py:433
  41.3 2.9 %collective-permute-start.2 = (f32[40,384]{1,0:T(8,128)S(1)}, f32[40,384]{1,0:T(8,128)S(1)}, u32[]{:S(2)}, u32[]{:S(2)}) collective-permute-start(f32[40,384]{1,0:T(8,128)S(1)} %get-tuple-element.71.z_ref.refs_0_.refs_8_), channel_id=1, source_target_pairs={{0,1},{1,0},{2,3},{3,2},{4,5},{5,4},{6,7},{7,6},{8,9},{9,8},{10,11... | collective-permute-start | bytes 184328 | tf_op jit(solution)/shard_map/ppermute | solution.py:434
  59.3 3.0 %collective-permute-start.5 = (f32[40,384]{1,0:T(8,128)S(1)}, f32[40,384]{1,0:T(8,128)S(1)}, u32[]{:S(2)}, u32[]{:S(2)}) collective-permute-start(f32[40,384]{1,0:T(8,128)S(1)} %get-tuple-element.77.z_ref.refs_0_.refs_9_), channel_id=1, source_target_pairs={{1,2},{3,4},{5,6},{7,8},{9,10},{11,12},{13,14},{15,16},{17,18},{19... | collective-permute-start | bytes 184328 | tf_op jit(solution)/shard_map/ppermute | solution.py:433
  59.9 2.9 %collective-permute-start.4 = (f32[40,384]{1,0:T(8,128)S(1)}, f32[40,384]{1,0:T(8,128)S(1)}, u32[]{:S(2)}, u32[]{:S(2)}) collective-permute-start(f32[40,384]{1,0:T(8,128)S(1)} %get-tuple-element.77.z_ref.refs_0_.refs_9_), channel_id=1, source_target_pairs={{0,1},{1,0},{2,3},{3,2},{4,5},{5,4},{6,7},{7,6},{8,9},{9,8},{10,11... | collective-permute-start | bytes 184328 | tf_op jit(solution)/shard_map/ppermute | solution.py:434
  77.9 3.0 %collective-permute-start.7 = (f32[40,384]{1,0:T(8,128)S(1)}, f32[40,384]{1,0:T(8,128)S(1)}, u32[]{:S(2)}, u32[]{:S(2)}) collective-permute-start(f32[40,384]{1,0:T(8,128)S(1)} %get-tuple-element.83.z_ref.refs_0_.refs_10_), channel_id=1, source_target_pairs={{1,2},{3,4},{5,6},{7,8},{9,10},{11,12},{13,14},{15,16},{17,18},{19... | collective-permute-start | bytes 184328 | tf_op jit(solution)/shard_map/ppermute | solution.py:433
  78.5 2.9 %collective-permute-start.6 = (f32[40,384]{1,0:T(8,128)S(1)}, f32[40,384]{1,0:T(8,128)S(1)}, u32[]{:S(2)}, u32[]{:S(2)}) collective-permute-start(f32[40,384]{1,0:T(8,128)S(1)} %get-tuple-element.83.z_ref.refs_0_.refs_10_), channel_id=1, source_target_pairs={{0,1},{1,0},{2,3},{3,2},{4,5},{5,4},{6,7},{7,6},{8,9},{9,8},{10,11... | collective-permute-start | bytes 184328 | tf_op jit(solution)/shard_map/ppermute | solution.py:434
  96.5 3.0 %collective-permute-start.9 = (f32[40,384]{1,0:T(8,128)S(1)}, f32[40,384]{1,0:T(8,128)S(1)}, u32[]{:S(2)}, u32[]{:S(2)}) collective-permute-start(f32[40,384]{1,0:T(8,128)S(1)} %get-tuple-element.89.z_ref.refs_0_.refs_11_), channel_id=1, source_target_pairs={{1,2},{3,4},{5,6},{7,8},{9,10},{11,12},{13,14},{15,16},{17,18},{19... | collective-permute-start | bytes 184328 | tf_op jit(solution)/shard_map/ppermute | solution.py:433
  97.2 2.9 %collective-permute-start.8 = (f32[40,384]{1,0:T(8,128)S(1)}, f32[40,384]{1,0:T(8,128)S(1)}, u32[]{:S(2)}, u32[]{:S(2)}) collective-permute-start(f32[40,384]{1,0:T(8,128)S(1)} %get-tuple-element.89.z_ref.refs_0_.refs_11_), channel_id=1, source_target_pairs={{0,1},{1,0},{2,3},{3,2},{4,5},{5,4},{6,7},{7,6},{8,9},{9,8},{10,11... | collective-permute-start | bytes 184328 | tf_op jit(solution)/shard_map/ppermute | solution.py:434
  115.1 3.0 %collective-permute-start.11 = (f32[40,384]{1,0:T(8,128)S(1)}, f32[40,384]{1,0:T(8,128)S(1)}, u32[]{:S(2)}, u32[]{:S(2)}) collective-permute-start(f32[40,384]{1,0:T(8,128)S(1)} %get-tuple-element.95.z_ref.refs_0_.refs_12_), channel_id=1, source_target_pairs={{1,2},{3,4},{5,6},{7,8},{9,10},{11,12},{13,14},{15,16},{17,18},{19... | collective-permute-start | bytes 184328 | tf_op jit(solution)/shard_map/ppermute | solution.py:433
  115.8 2.9 %collective-permute-start.10 = (f32[40,384]{1,0:T(8,128)S(1)}, f32[40,384]{1,0:T(8,128)S(1)}, u32[]{:S(2)}, u32[]{:S(2)}) collective-permute-start(f32[40,384]{1,0:T(8,128)S(1)} %get-tuple-element.95.z_ref.refs_0_.refs_12_), channel_id=1, source_target_pairs={{0,1},{1,0},{2,3},{3,2},{4,5},{5,4},{6,7},{7,6},{8,9},{9,8},{10,11... | collective-permute-start | bytes 184328 | tf_op jit(solution)/shard_map/ppermute | solution.py:434

commit v5 on v4

--- a/solution.py
+++ b/solution.py
@@ -97,7 +97,7 @@
     blocks.start()
     fetch(list(zip(args, held)), sems)
     (res_ref, orders_ref, state_ref, nbr_ref, face_ref, orient_ref, source_ref, flux_ref, geo_ref, stiff_ref, trace_ref) = held
-    start_ref, mask_ref, part_ref, state2_ref, hot_ref, coup_ref, sel_ref, own_ref, near_ref, back_ref = outs[:10]
+    start_ref, mask_ref, part_ref, state2_ref, hot_ref, coup_ref, turn_ref, own_ref, near_ref, back_ref = outs[:10]
     nv, nb, ne, nq, nbp, nqp = sz.nv, sz.nb, sz.ne, sz.nq, sz.nbp, sz.nqp
     orders = orders_ref[...]
     count = (orders + 1) * (orders + 2) * (orders + 3) // 6
@@ -111,7 +111,7 @@
 
     me = me_ref[0]
     nbr = nbr_ref[...]
-    rel = jnp.where(nbr >= 0, nbr - me * ne + ne, -4 * ne)
+    rel = nbr - me * ne + ne
     face, orient = face_ref[...], orient_ref[...]
     flip = (orient >= 3).astype(jnp.int32)
     choice, turn = flip * 4 + face, orient - 3 * flip
@@ -119,17 +119,14 @@
     def by_face(x):
         return jnp.concatenate([x[f : f + 1] for f in range(4)], axis=1)
 
-    sel_ref[...] = jnp.concatenate([by_face(choice), by_face(turn)], axis=0)
-    cols = by_face(rel)
-    rows = iota((4 * ne, 4 * ne), 0)
+    turn_ref[...] = by_face(turn)
+    cols = by_face(jnp.where(nbr >= 0, choice * 4 * ne + rel, -1))
+    rows = iota((8 * ne, 4 * ne), 0)
     block = rows // ne
-    inner = rows - block * ne
+    code = block * 4 * ne + rows - block * ne
     chip_side = jnp.where(lax.rem(me, 2) == 0, 2, 0)
-    for parity in range(2):
-        own_block, chip_block, far_block = parity, 1 - parity, 2 + parity
-        side = jnp.where(block == own_block, 1, jnp.where(block == chip_block, chip_side, 2 - chip_side))
-        code = jnp.where(block == 5 - far_block, -ne, side * ne + inner)
-        hot_ref[parity] = (code == cols).astype(F32).astype(BF16)
+    for source, side in enumerate((1, chip_side, 2 - chip_side)):
+        hot_ref[source] = (code + side * ne == cols).astype(F32).astype(BF16)
 
     for k in range(3):
         pieces = []
@@ -223,6 +220,99 @@
     return jnp.concatenate([x[:, shift:], x[:, :shift]], axis=1)
 
 
+def gather(sz, sources, hot_refs, near_ref):
+    nqp, ne, pair = sz.nqp, sz.ne, sz.pair
+    low_half = iota((1, pair), 1) < ne
+    lhs = []
+    for source in sources:
+        every = dot(near_ref[...], stack_rhs(split3(source), 0))
+        rows = []
+        for v in range(sz.nv):
+            column = every[:, v // 2 * pair : (v // 2 + 1) * pair]
+            turned = pltpu.roll(column, ne, 1)
+            pieces = []
+            for g in range(0, 8, 2):
+                first, second = (slice((g + i) * nqp, (g + i + 1) * nqp) for i in range(2))
+                if v % 2 == 0:
+                    pieces.append(jnp.where(low_half, column[first], turned[second]))
+                else:
+                    pieces.append(jnp.where(low_half, turned[first], column[second]))
+            rows.append(jnp.concatenate(pieces, axis=1))
+        lhs.append(jnp.concatenate(rows, axis=0))
+    lhs = split3(jnp.concatenate(lhs, axis=1))
+    hot = jnp.concatenate([ref[...] for ref in hot_refs], axis=0)
+    got = dot(jnp.concatenate(lhs, axis=0).astype(BF16), hot)
+    size = sz.nv * nqp
+    return got[:size] + got[size : 2 * size] + got[2 * size :]
+
+
+def to_faces(sz, seen, turn):
+    nqp, ne, pair = sz.nqp, sz.ne, sz.pair
+    low_half = iota((1, pair), 1) < ne
+    nq, third = sz.nq, sz.nq // 3
+    turned = []
+    for v in range(sz.nv):
+        tr = seen[v * nqp : (v + 1) * nqp]
+        fill = tr[nq:]
+        once = jnp.concatenate([tr[third:nq], tr[:third], fill], axis=0)
+        twice = jnp.concatenate([tr[2 * third : nq], tr[: 2 * third], fill], axis=0)
+        turned.append(jnp.where(turn == 0, tr, jnp.where(turn == 1, once, twice)))
+    result = []
+    for f in range(4):
+        start = f // 2 * pair
+        blocks = []
+        for p in range(sz.lanes // pair):
+            first, second = (turned[2 * p + i][:, start : start + pair] for i in range(2))
+            if f % 2 == 0:
+                second = pltpu.roll(second, ne, 1)
+            else:
+                first = pltpu.roll(first, ne, 1)
+            blocks.append(jnp.where(low_half, first, second))
+        result.append(jnp.concatenate(blocks, axis=1))
+    return jnp.concatenate(result, axis=0)
+
+
+def spread(row, i):
+    return jnp.broadcast_to(row[:, i : i + 1], (1, 128))
+
+
+def rotate_column(step, row, square, turns_ref):
+    entries = [spread(row, i) for i in range(step + 2)]
+    if square:
+        rest = entries[step + 1]
+        for h in entries[:-1]:
+            rest = rest - h * h
+        entries[step + 1] = jnp.sqrt(rest + EPSILON)
+    column = list(entries)
+    for i in range(step):
+        cosine, sine = turns_ref[2 * i : 2 * i + 1, :], turns_ref[2 * i + 1 : 2 * i + 2, :]
+        top, low = column[i], column[i + 1]
+        column[i] = cosine * top + sine * low
+        column[i + 1] = cosine * low - sine * top
+    lead, below = column[step], column[step + 1]
+    radius = jnp.sqrt(lead * lead + below * below)
+    cosine, sine = lead / radius, below / radius
+    column[step] = cosine * lead + sine * below
+    return entries, column, cosine, sine
+
+
+def direction(sz, search, column, earlier):
+    def across(x):
+        return jnp.concatenate([x] * (sz.lanes // 128), axis=1)
+
+    total = search
+    for r, ref in zip(column, earlier):
+        total = total - across(r) * ref[...]
+    return total * across(1.0 / column[len(earlier)]), across
+
+
+def fill_column(step, entries, hess):
+    row_id, col_id = iota(hess.shape, 0), iota(hess.shape, 1)
+    for i, entry in enumerate(entries):
+        hess = jnp.where((row_id == i) & (col_id == step), entry[:, : hess.shape[1]], hess)
+    return hess
+
+
 def local_kernel(sz, z_ref, own_ref, coup_ref, vol_ref, tr_ref):
     search = z_ref[: sz.nbp]
     out = dot(own_ref[...], stack_rhs(split3(search), 0))
@@ -236,127 +326,72 @@
     vol_ref[...] = acc
 
 
-def neighbour_traces(sz, own, chip, far, hot_ref, near_ref, sel_ref):
-    nbp, nqp, ne, pair = sz.nbp, sz.nqp, sz.ne, sz.pair
-    pairs, cols = sz.lanes // pair, 4 * ne
-    low_half = iota((1, pair), 1) < ne
-    owns, chips, fars = split3(own), split3(chip), split3(far)
-    lhs = ([], [])
-    for n in range(3):
-        for p in range(pairs):
-            mine, theirs, away = (x[n][:, p * pair : (p + 1) * pair] for x in (owns, chips, fars))
-            theirs = pltpu.roll(theirs, ne, 1)
-            lhs[0].append(jnp.concatenate([jnp.where(low_half, mine, theirs), away], axis=1))
-            lhs[1].append(jnp.concatenate([jnp.where(low_half, theirs, mine), away], axis=1))
-    got = [dot(jnp.concatenate(lhs[i], axis=0).astype(BF16), hot_ref[i]) for i in range(2)]
-    picked = [
-        jnp.concatenate(
-            [got[v % 2][(n * pairs + v // 2) * nbp : (n * pairs + v // 2 + 1) * nbp] for v in range(sz.nv)], axis=1
-        )
-        for n in range(3)
-    ]
-    every = dot(near_ref[...], stack_rhs(picked, 0))
-    choice, turn = sel_ref[0:1, :], sel_ref[1:2, :]
-    is_choice = [choice == g for g in range(8)]
-    nq, third = sz.nq, sz.nq // 3
-    seen = []
+def column_kernel(sz, step, *refs):
+    head_ref, z_ref, turns_ref, hess_ref, sum_ref = refs[:5]
+    earlier = refs[5 : 5 + step]
+    turns_out, hess_out, sum_out, dir_ref = refs[5 + step :]
+    entries, column, cosine, sine = rotate_column(step, head_ref[...], False, turns_ref)
+    new, across = direction(sz, z_ref[: sz.nbp], column, earlier)
+    dir_ref[...] = new
+    last = turns_ref.shape[0] - 1
+    right = spread(turns_ref[last:, :], 0) if step == 0 else turns_ref[last:, :]
+    value = across(cosine * right) * new
+    if step == 0:
+        sum_out[...] = value
+        hess = jnp.zeros(hess_out.shape, F32)
+        turns_out[...] = jnp.zeros(turns_out.shape, F32)
+    else:
+        sum_out[...] = sum_ref[...] + value
+        hess = hess_ref[...]
+        turns_out[...] = turns_ref[...]
+    hess_out[...] = fill_column(step, entries, hess)
+    turns_out[2 * step : 2 * step + 1, :] = cosine
+    turns_out[2 * step + 1 : 2 * step + 2, :] = sine
+    turns_out[turns_out.shape[0] - 1 :, :] = -(sine * right)
+
+
+def finish_kernel(sz, *refs):
+    red_ref, z_ref, turns_ref, hess_ref, sum_ref = refs[:5]
+    step = ITERS - 1
+    earlier = refs[5 : 5 + step]
+    out_ref, hess_out = refs[5 + step :]
+    row = jnp.sum(red_ref[...], axis=0, keepdims=True)
+    entries, column, cosine, sine = rotate_column(step, row, True, turns_ref)
+    new, across = direction(sz, z_ref[...], column, earlier)
+    last = turns_ref.shape[0] - 1
+    total = sum_ref[...] + across(cosine * turns_ref[last:, :]) * new
     for v in range(sz.nv):
-        mine = every[:, v * cols : (v + 1) * cols]
-        tr = mine[:nqp]
-        for g in range(1, 8):
-            tr = jnp.where(is_choice[g], mine[g * nqp : (g + 1) * nqp], tr)
-        fill = tr[nq:]
-        once = jnp.concatenate([tr[third:nq], tr[:third], fill], axis=0)
-        twice = jnp.concatenate([tr[2 * third : nq], tr[: 2 * third], fill], axis=0)
-        seen.append(jnp.where(turn == 0, tr, jnp.where(turn == 1, once, twice)))
-    result = []
-    for f in range(4):
-        start = f // 2 * pair
-        blocks = []
-        for p in range(pairs):
-            first, second = (seen[2 * p + i][:, start : start + pair] for i in range(2))
-            if f % 2 == 0:
-                second = pltpu.roll(second, ne, 1)
-            else:
-                first = pltpu.roll(first, ne, 1)
-            blocks.append(jnp.where(low_half, first, second))
-        result.append(jnp.concatenate(blocks, axis=1))
-    return jnp.concatenate(result, axis=0)
-
-
-def gain_kernel(sz, z_ref, chip_ref, far_ref, hot_ref, near_ref, own_ref, sel_ref, gain_ref):
+        out_ref[v] = total[: sz.nb, v * sz.ne : (v + 1) * sz.ne]
+    hess_out[...] = fill_column(step, entries, hess_ref[...])[: ITERS + 1, :ITERS]
+
+
+def near_kernel(sz, z_ref, chip_ref, hot_ref, near_ref, *outs):
     nbp = sz.nbp
-    state = z_ref[nbp:]
-    tr = dot(own_ref[: 4 * sz.nqp], stack_rhs(split3(state), 0))
-    other = neighbour_traces(sz, state, chip_ref[nbp:], far_ref[nbp:], hot_ref, near_ref, sel_ref)
-    gain_ref[...] = 1.0 + 0.5 * jnp.abs(tr + other)
+    for i, out_ref in enumerate(outs):
+        sources = [ref[i * nbp : (i + 1) * nbp] for ref in (z_ref, chip_ref)]
+        out_ref[...] = gather(sz, sources, [hot_ref.at[0], hot_ref.at[1]], near_ref)
+
+
+def gain_kernel(sz, z_ref, far_ref, hot_ref, near_ref, own_ref, turn_ref, seen_ref, gain_ref):
+    nbp = sz.nbp
+    tr = dot(own_ref[: 4 * sz.nqp], stack_rhs(split3(z_ref[nbp:]), 0))
+    seen = seen_ref[...] + gather(sz, [far_ref[nbp:]], [hot_ref.at[2]], near_ref)
+    gain_ref[...] = 1.0 + 0.5 * jnp.abs(tr + to_faces(sz, seen, turn_ref[...]))
 
 
 def image_kernel(sz, step, *refs):
-    z_ref, chip_ref, far_ref, hot_ref, near_ref, sel_ref, gain_ref, back_ref, vol_ref, tr_ref, mask_ref = refs[:11]
-    basis = refs[11 : 12 + step]
-    w_ref, part_ref = refs[12 + step :]
-    nbp = sz.nbp
-    other = neighbour_traces(sz, z_ref[:nbp], chip_ref[:nbp], far_ref[:nbp], hot_ref, near_ref, sel_ref)
+    far_ref, hot_ref, near_ref, turn_ref, seen_ref, gain_ref, back_ref, vol_ref, tr_ref, mask_ref = refs[:10]
+    basis = refs[10 : 11 + step]
+    part_ref = refs[11 + step]
+    seen = seen_ref[...] + gather(sz, [far_ref[: sz.nbp]], [hot_ref.at[2]], near_ref)
+    other = to_faces(sz, seen, turn_ref[...])
     flux = gain_ref[...] * (tr_ref[...] - other)
     face = dot(back_ref[...], stack_rhs(split3(flux), 0))
     image = (vol_ref[...] + face) * mask_ref[...]
-    w_ref[...] = image
+    if step < ITERS - 1:
+        refs[12 + step][...] = image
     values = [full_sum(b[...] * image) for b in basis] + [full_sum(image * image)]
     part_ref[...] = partial_rows(values, sz.peers)
-
-
-def finish_kernel(sz, *refs):
-    red_ref, heads, searches = refs[0], refs[1 : 1 + ITERS], refs[1 + ITERS : 1 + 2 * ITERS]
-    out_ref, hess_ref = refs[1 + 2 * ITERS :]
-    lane = iota((1, 128), 1)
-
-    def entry(row, i):
-        return jnp.sum(jnp.where(lane == i, row, 0.0), axis=1, keepdims=True)
-
-    start_value = entry(heads[0][...], 0)
-    zero = jnp.zeros((1, 1), F32)
-    upper = [[zero] * ITERS for _ in range(ITERS + 1)]
-    for k in range(ITERS - 1):
-        row = heads[k + 1][...]
-        for i in range(k + 2):
-            upper[i][k] = entry(row, i)
-    scalars = total_scalars(red_ref[...], ITERS + 1)
-    square = scalars[ITERS]
-    for i in range(ITERS):
-        upper[i][ITERS - 1] = scalars[i]
-        square = square - scalars[i] * scalars[i]
-    upper[ITERS][ITERS - 1] = jnp.sqrt(square + EPSILON)
-    shape = hess_ref.shape
-    row_id, col_id = iota(shape, 0), iota(shape, 1)
-    hess = jnp.zeros(shape, F32)
-    for i in range(ITERS + 1):
-        for k in range(max(i - 1, 0), ITERS):
-            hess = jnp.where((row_id == i) & (col_id == k), upper[i][k], hess)
-    hess_ref[...] = hess
-    right = [start_value] + [zero] * ITERS
-    for k in range(ITERS):
-        lead, below = upper[k][k], upper[k + 1][k]
-        radius = jnp.sqrt(lead * lead + below * below)
-        cosine, sine = lead / radius, below / radius
-        for j in range(k, ITERS):
-            top, low = upper[k][j], upper[k + 1][j]
-            upper[k][j] = cosine * top + sine * low
-            upper[k + 1][j] = cosine * low - sine * top
-        top, low = right[k], right[k + 1]
-        right[k] = cosine * top + sine * low
-        right[k + 1] = cosine * low - sine * top
-    coeffs = [None] * ITERS
-    for k in reversed(range(ITERS)):
-        acc = right[k]
-        for j in range(k + 1, ITERS):
-            acc = acc - upper[k][j] * coeffs[j]
-        coeffs[k] = acc / upper[k][k]
-    total = coeffs[0] * searches[0][: sz.nbp]
-    for k in range(1, ITERS):
-        total = total + coeffs[k] * searches[k][: sz.nbp]
-    for v in range(sz.nv):
-        out_ref[v] = total[: sz.nb, v * sz.ne : (v + 1) * sz.ne]
 
 
 def call(kernel, name, out_shape, *args, specs=None, scratch=(), limit=24 * 2**20):
@@ -393,14 +428,14 @@
         residual_in, orders.reshape(1, ne), state_coeffs, neighbours, neighbour_face, orientation, source, flux_jacobian,
         geometry, stiffness, jnp.transpose(trace_matrix, (1, 0, 2)),
     ]
-    start, mask, part, state, hot, coup, sel, own, near, back, blocks = call(
+    start, mask, part, state, hot, coup, turn, own, near, back, blocks = call(
         functools.partial(init_kernel, sz),
         "init",
         (
             wide, wide, parts, wide,
-            shape(2, 4 * ne, 4 * ne, dtype=BF16),
+            shape(3, 8 * ne, 4 * ne, dtype=BF16),
             shape(4, nv, lanes),
-            shape(2, 4 * ne, dtype=jnp.int32),
+            shape(1, 4 * ne, dtype=jnp.int32),
             shape(4 * nqp + 3 * nbp, 6 * nbp, dtype=BF16),
             shape(8 * nqp, 6 * nbp, dtype=BF16),
             shape(nbp, 24 * nqp, dtype=BF16),
@@ -417,37 +452,48 @@
     odd = range(1, peers - 1, 2)
     off_chip = [(i, i + 1) for i in odd] + [(i + 1, i) for i in odd]
 
-    heads, searches, basis = [], [], []
+    basis, directions = [], []
     vec, gain = start, None
+    turns = hess = total = None
+    face_shape, seen_shape = shape(4 * nqp, lanes), shape(nv * nqp, 4 * ne)
+    state_shapes = (shape(2 * ITERS + 4, 128), shape(8, 128), wide, wide)
     for k in range(ITERS):
         red = exchange(part)
         kernel = functools.partial(precond_kernel, sz, k) if k else functools.partial(precond_start_kernel, sz)
         extra = basis if k else [state]
+        previous = None if k == 0 else search
         search, new, head = call(
             kernel, f"precond{k}", (shape(nbp if k else 2 * nbp, lanes), wide, shape(1, 128)),
             red, vec, mask, blocks, *extra,
         )
         basis = basis + [new]
-        heads.append(head)
-        searches.append(search)
         far = lax.ppermute(search, AXES, off_chip)
         chip = lax.ppermute(search, AXES, on_chip)
-        vol, tr = call(
-            functools.partial(local_kernel, sz), "local", (wide, shape(4 * nqp, lanes)), search, own, coup
+        vol, tr = call(functools.partial(local_kernel, sz), "local", (wide, face_shape), search, own, coup)
+        if k == 0:
+            turns, hess, total = head, head, head
+        else:
+            turns, hess, total, new = call(
+                functools.partial(column_kernel, sz, k - 1), f"column{k}", state_shapes,
+                head, previous, turns, hess, total, *directions,
+            )
+            directions = directions + [new]
+        seen = call(
+            functools.partial(near_kernel, sz), "near", (seen_shape,) * (1 if k else 2), search, chip, hot, near
         )
         if k == 0:
             gain = call(
-                functools.partial(gain_kernel, sz), "gain", shape(4 * nqp, lanes),
-                search, chip, far, hot, near, own, sel,
+                functools.partial(gain_kernel, sz), "gain", face_shape, search, far, hot, near, own, turn, seen[1]
             )
-        vec, part = call(
-            functools.partial(image_kernel, sz, k), f"image{k}", (wide, parts),
-            search, chip, far, hot, near, sel, gain, back, vol, tr, mask, *basis,
+        outs = call(
+            functools.partial(image_kernel, sz, k), f"image{k}", (parts, wide) if k < ITERS - 1 else (parts,),
+            far, hot, near, turn, seen[0], gain, back, vol, tr, mask, *basis,
         )
+        part, vec = outs if k < ITERS - 1 else (outs[0], None)
     red = exchange(part)
     return call(
         functools.partial(finish_kernel, sz), "finish", (shape(nv, nb, ne), shape(ITERS + 1, ITERS)),
-        red, *heads, *searches,
+        red, search, turns, hess, total, *directions,
     )
 
 

time: 134 us -> 134 us (level)
  starting transfers between devices: 15.7 us -> 11 us
  waiting for transfers between devices: 3.3 us -> 7.85 us
  Pallas kernels: 27.8 us -> 31.4 us
  blocking collectives: 85.8 us -> 82.5 us
    ppermute x6, starting transfers between devices: 11.7 us -> 0.43 us  [body(): chip = lax.ppermute(search, AXES, on_chip)]
    all_to_all x0 -> x1, starting transfers between devices: none -> 6.58 us  [exchange(): return lax.all_to_all(rows, AXES, 0, 0, tiled=True)]
    all_to_all x0 -> x1, waiting for transfers between devices: none -> 6.49 us  [exchange(): return lax.all_to_all(rows, AXES, 0, 0, tiled=True)]
    pallas_call x21 -> x32, Pallas kernels: 27.8 us -> 31.4 us  [call(): pl.pallas_call(kernel, name=name, out_shape=out_shape, in_specs=specs or...]
    all_to_all x7 -> x6, blocking collectives: 85.8 us -> 82.5 us  [exchange(): return lax.all_to_all(rows, AXES, 0, 0, tiled=True)]
    ppermute x6, waiting for transfers between devices: 3.29 us -> 1.34 us  [body(): chip = lax.ppermute(search, AXES, on_chip)]
  transfers between devices with their start and end apart: 12 -> 13, of which waited for: 6 -> 7; matrix products, arithmetic and copies ran while one was open for 0% -> 0% of each run, Pallas kernels for 2% -> 5%
where the time goes in v5:
time: 134 us
  blocking collectives  82.5 us (62%)
  Pallas kernels  31.4 us (23%)
  starting transfers between devices  11 us (8%)
  waiting for transfers between devices  7.85 us (6%)
    all_to_all x6, blocking collectives, exchange(): return lax.all_to_all(rows, AXES, 0, 0, tiled=True)  82.5 us
    pallas_call x32, Pallas kernels, call(): pl.pallas_call(kernel, name=name, out_shape=out_shape, in_specs=specs or...  31.4 us
    all_to_all x1, starting transfers between devices, exchange(): return lax.all_to_all(rows, AXES, 0, 0, tiled=True)  6.58 us
    all_to_all x1, waiting for transfers between devices, exchange(): return lax.all_to_all(rows, AXES, 0, 0, tiled=True)  6.49 us
    ppermute x6, starting transfers between devices, body(): far = lax.ppermute(search, AXES, off_chip)  3.99 us
  transfers between devices with their start and end apart: 13, of which 7 were waited for; matrix products, arithmetic and copies ran while one was open for 0% of the time, Pallas kernels for 5%

profile of v5, /device:TPU:0, one launch (start us, length us, event | category | flops | bytes accessed | tf_op | source)
XLA Modules:
  0.0 133.7 jit_solution(14591844566218472037)
XLA Ops:
  0.6 3.4 %init.1 = (f32[40,384]{1,0:T(8,128)S(1)}, f32[40,384]{1,0:T(8,128)S(1)}, f32[32,128]{1,0:T(8,128)S(1)}, f32[40,384]{1,0:T(8,128)S(1)}, bf16[3,512,256]{2,1,0:T(8...) custom-call(s32[1]{0:T(128)} %bitcast.me_ref, ...), custom_call_target="tpu_custom_call" | custom-call | tf_op jit(solution)/shard_map/init/pallas_call | solution.py:398
  4.0 14.3 %all_to_all.77 = f32[32,1,128]{2,1,0:T(1,128)S(1)} all-to-all(f32[32,1,128]{2,1,0:T(1,128)S(1)} %bitcast.38), channel_id=1, replica_groups=mesh['dom'=8,'grp'=4] {'dom','grp'}, dimensions={0} | all-to-all | bytes 32768 | tf_op jit(solution)/shard_map/all_to_all | solution.py:449
  18.3 2.3 %precond0.1 = (f32[80,384]{1,0:T(8,128)S(1)}, f32[40,384]{1,0:T(8,128)S(1)}, f32[1,128]{1,0:T(1,128)S(1)}) custom-call(f32[32,128]{1,0:T(8,128)S(1)} %bitcast.32, f32[40,384]{1,0:T(8,128)S(1)} %get-tuple-element.76.vec_ref, f32[40,384]{1,0:T(8,128)S(1)} %get-tuple-element.77.mask_ref.refs_9_.refs_2_, ...), custom_call_target="tpu_custom_call" | custom-call | tf_op jit(solution)/shard_map/precond0/pallas_call | solution.py:398
  20.7 0.1 collective-permute-start.1
  20.7 0.7 collective-permute-start
  21.4 0.3 local.6
  21.8 0.3 collective-permute-done.1.chip_ref
  22.1 0.8 near.6
  22.8 0.0 collective-permute-done.far_ref.refs_0_
  22.8 0.6 gain.1.refs_5_
  23.4 0.8 image0.1
  24.2 14.0 %all_to_all.78 = f32[32,1,128]{2,1,0:T(1,128)S(1)} all-to-all(f32[32,1,128]{2,1,0:T(1,128)S(1)} %bitcast.39), channel_id=1, replica_groups=mesh['dom'=8,'grp'=4] {'dom','grp'}, dimensions={0} | all-to-all | bytes 32768 | tf_op jit(solution)/shard_map/all_to_all | solution.py:449
  38.2 2.5 %precond1.1 = (f32[40,384]{1,0:T(8,128)S(1)}, f32[40,384]{1,0:T(8,128)S(1)}, f32[1,128]{1,0:T(1,128)S(1)}) custom-call(f32[32,128]{1,0:T(8,128)S(1)} %bitcast.33, f32[40,384]{1,0:T(8,128)S(1)} %get-tuple-element.93.refs_1_, f32[40,384]{1,0:T(8,128)S(1)} %get-tuple-element.77.mask_ref.refs_9_.refs_2_, ...), custom_call_target="tpu_custom_call" | custom-call | tf_op jit(solution)/shard_map/precond1/pallas_call | solution.py:398
  40.7 0.1 collective-permute-start.3
  40.7 0.7 collective-permute-start.2
  41.4 0.3 local.7
  41.8 0.2 collective-permute-done.3.chip_ref
  42.0 0.6 near.7.refs_4_
  42.5 0.0 collective-permute-done.2.refs_0_
  42.6 0.8 image1.1
  43.4 13.6 %all_to_all.79 = f32[32,1,128]{2,1,0:T(1,128)S(1)} all-to-all(f32[32,1,128]{2,1,0:T(1,128)S(1)} %bitcast.40), channel_id=1, replica_groups=mesh['dom'=8,'grp'=4] {'dom','grp'}, dimensions={0} | all-to-all | bytes 32768 | tf_op jit(solution)/shard_map/all_to_all | solution.py:449
  57.0 2.5 %precond2.1 = (f32[40,384]{1,0:T(8,128)S(1)}, f32[40,384]{1,0:T(8,128)S(1)}, f32[1,128]{1,0:T(1,128)S(1)}) custom-call(f32[32,128]{1,0:T(8,128)S(1)} %bitcast.34, f32[40,384]{1,0:T(8,128)S(1)} %get-tuple-element.99.refs_1_, f32[40,384]{1,0:T(8,128)S(1)} %get-tuple-element.77.mask_ref.refs_9_.refs_2_, ...), custom_call_target="tpu_custom_call" | custom-call | tf_op jit(solution)/shard_map/precond2/pallas_call | solution.py:398
  59.4 0.1 collective-permute-start.5
  59.5 0.7 collective-permute-start.4
  60.2 0.3 local.8
  60.5 0.2 collective-permute-done.5.chip_ref
  60.7 0.6 near.8.refs_4_
  61.3 0.0 collective-permute-done.4.refs_0_
  61.3 0.8 image2.1
  62.2 13.6 %all_to_all.80 = f32[32,1,128]{2,1,0:T(1,128)S(1)} all-to-all(f32[32,1,128]{2,1,0:T(1,128)S(1)} %bitcast.41), channel_id=1, replica_groups=mesh['dom'=8,'grp'=4] {'dom','grp'}, dimensions={0} | all-to-all | bytes 32768 | tf_op jit(solution)/shard_map/all_to_all | solution.py:449
  75.7 2.5 %precond3.1 = (f32[40,384]{1,0:T(8,128)S(1)}, f32[40,384]{1,0:T(8,128)S(1)}, f32[1,128]{1,0:T(1,128)S(1)}) custom-call(f32[32,128]{1,0:T(8,128)S(1)} %bitcast.35, f32[40,384]{1,0:T(8,128)S(1)} %get-tuple-element.105.refs_1_, f32[40,384]{1,0:T(8,128)S(1)} %get-tuple-element.77.mask_ref.refs_9_.refs_2_, ...), custom_call_target="tpu_custom_call" | custom-call | tf_op jit(solution)/shard_map/precond3/pallas_call | solution.py:398
  78.2 0.1 collective-permute-start.7
  78.3 0.7 collective-permute-start.6
  79.0 0.3 local.9
  79.3 0.2 collective-permute-done.7.chip_ref
  79.5 0.6 near.9.refs_4_
  80.1 0.0 collective-permute-done.6.refs_0_
  80.1 0.8 image3.1
  81.0 13.6 %all_to_all.81 = f32[32,1,128]{2,1,0:T(1,128)S(1)} all-to-all(f32[32,1,128]{2,1,0:T(1,128)S(1)} %bitcast.42), channel_id=1, replica_groups=mesh['dom'=8,'grp'=4] {'dom','grp'}, dimensions={0} | all-to-all | bytes 32768 | tf_op jit(solution)/shard_map/all_to_all | solution.py:449
  94.5 2.5 %precond4.1 = (f32[40,384]{1,0:T(8,128)S(1)}, f32[40,384]{1,0:T(8,128)S(1)}, f32[1,128]{1,0:T(1,128)S(1)}) custom-call(f32[32,128]{1,0:T(8,128)S(1)} %bitcast.36, f32[40,384]{1,0:T(8,128)S(1)} %get-tuple-element.111.refs_1_, f32[40,384]{1,0:T(8,128)S(1)} %get-tuple-element.77.mask_ref.refs_9_.refs_2_, ...), custom_call_target="tpu_custom_call" | custom-call | tf_op jit(solution)/shard_map/precond4/pallas_call | solution.py:398
  97.0 0.1 collective-permute-start.9
  97.1 0.7 collective-permute-start.8
  97.7 0.3 local.10
  98.1 0.2 collective-permute-done.9.chip_ref
  98.3 0.6 near.10.refs_4_
  98.9 0.0 collective-permute-done.8.refs_0_
  98.9 0.9 image4.1
  99.7 13.6 %all_to_all.82 = f32[32,1,128]{2,1,0:T(1,128)S(1)} all-to-all(f32[32,1,128]{2,1,0:T(1,128)S(1)} %bitcast.43), channel_id=1, replica_groups=mesh['dom'=8,'grp'=4] {'dom','grp'}, dimensions={0} | all-to-all | bytes 32768 | tf_op jit(solution)/shard_map/all_to_all | solution.py:449
  113.3 2.5 %precond5.1 = (f32[40,384]{1,0:T(8,128)S(1)}, f32[40,384]{1,0:T(8,128)S(1)}, f32[1,128]{1,0:T(1,128)S(1)}) custom-call(f32[32,128]{1,0:T(8,128)S(1)} %bitcast.31, f32[40,384]{1,0:T(8,128)S(1)} %get-tuple-element.117.refs_1_, f32[40,384]{1,0:T(8,128)S(1)} %get-tuple-element.77.mask_ref.refs_9_.refs_2_, ...), custom_call_target="tpu_custom_call" | custom-call | tf_op jit(solution)/shard_map/precond5/pallas_call | solution.py:398
  115.8 0.1 collective-permute-start.11
  115.8 0.7 collective-permute-start.10
  116.5 0.3 local.11
  116.9 0.2 collective-permute-done.11.chip_ref
  117.1 0.6 near.11.refs_4_
  117.7 0.0 collective-permute-done.10.refs_0_
  117.7 1.5 %image5.1 = f32[32,128]{1,0:T(8,128)} custom-call(f32[40,384]{1,0:T(8,128)S(1)} %collective-permute-done.10.refs_0_, bf16[3,512,256]{2,1,0:T(8,128)(2,1)S(1)} %get-tuple-element.81.hot_ref.refs_1_, bf16[128,240]{1,0:T(8,128)(2,1)S(1)} %get-tuple-element.82.near_ref.refs_2_, s32[1,256]{1,0:T(1,128)S(1)} %get-tuple-element.83.turn_ref.refs_3_, ...), custom_call_target="tpu_custom_call" | custom-call | tf_op jit(solution)/shard_map/image5/pallas_call | solution.py:398
  119.1 6.6 %all-to-all-start.6 = ((f32[32,1,128]{2,1,0:T(1,128)}), f32[32,1,128]{2,1,0:T(1,128)S(1)}, u32[]{:S(2)}, u32[]{:S(2)}) async-start(f32[32,1,128]{2,1,0:T(1,128)} %bitcast.22), calls=%async_computation.6 | async-start | bytes 32768 | tf_op jit(solution)/shard_map/all_to_all | solution.py:449
  125.7 0.1 column1.1
  125.8 0.1 column2.1
  126.0 0.1 column3.1
  126.1 0.1 column4.1
  126.2 0.1 column5.1
  126.3 6.5 %all-to-all-done.6 = f32[32,1,128]{2,1,0:T(1,128)S(1)} async-done(((f32[32,1,128]{2,1,0:T(1,128)}), f32[32,1,128]{2,1,0:T(1,128)S(1)}, u32[]{:S(2)}, u32[]{:S(2)}) %all-to-all-start.6) | async-done | bytes 16416 | tf_op jit(solution)/shard_map/all_to_all | solution.py:449
  132.8 0.9 finish.1
Async XLA Ops:
  20.7 1.4 %collective-permute-start.1 = (f32[80,384]{1,0:T(8,128)S(1)}, f32[80,384]{1,0:T(8,128)S(1)}, u32[]{:S(2)}, u32[]{:S(2)}) collective-permute-start(f32[80,384]{1,0:T(8,128)S(1)} %get-tuple-element.80.z_ref.refs_1_), channel_id=1, source_target_pairs={{0,1},{1,0},{2,3},{3,2},{4,5},{5,4},{6,7},{7,6},{8,9},{9,8},{10,11... | collective-permute-start | bytes 368648 | tf_op jit(solution)/shard_map/ppermute | solution.py:471
  20.7 2.1 %collective-permute-start = (f32[80,384]{1,0:T(8,128)S(1)}, f32[80,384]{1,0:T(8,128)S(1)}, u32[]{:S(2)}, u32[]{:S(2)}) collective-permute-start(f32[80,384]{1,0:T(8,128)S(1)} %get-tuple-element.80.z_ref.refs_1_), channel_id=1, source_target_pairs={{1,2},{3,4},{5,6},{7,8},{9,10},{11,12},{13,14},{15,16},{17,18},{19... | collective-permute-start | bytes 368648 | tf_op jit(solution)/shard_map/ppermute | solution.py:470
  40.7 1.3 collective-permute-start.3
  40.7 1.8 %collective-permute-start.2 = (f32[40,384]{1,0:T(8,128)S(1)}, f32[40,384]{1,0:T(8,128)S(1)}, u32[]{:S(2)}, u32[]{:S(2)}) collective-permute-start(f32[40,384]{1,0:T(8,128)S(1)} %get-tuple-element.94.z_ref.refs_1_), channel_id=1, source_target_pairs={{1,2},{3,4},{5,6},{7,8},{9,10},{11,12},{13,14},{15,16},{17,18},{19... | collective-permute-start | bytes 184328 | tf_op jit(solution)/shard_map/ppermute | solution.py:470
  59.4 1.3 collective-permute-start.5
  59.5 1.8 %collective-permute-start.4 = (f32[40,384]{1,0:T(8,128)S(1)}, f32[40,384]{1,0:T(8,128)S(1)}, u32[]{:S(2)}, u32[]{:S(2)}) collective-permute-start(f32[40,384]{1,0:T(8,128)S(1)} %get-tuple-element.100.z_ref.refs_1_), channel_id=1, source_target_pairs={{1,2},{3,4},{5,6},{7,8},{9,10},{11,12},{13,14},{15,16},{17,18},{19... | collective-permute-start | bytes 184328 | tf_op jit(solution)/shard_map/ppermute | solution.py:470
  78.2 1.3 collective-permute-start.7
  78.3 1.8 %collective-permute-start.6 = (f32[40,384]{1,0:T(8,128)S(1)}, f32[40,384]{1,0:T(8,128)S(1)}, u32[]{:S(2)}, u32[]{:S(2)}) collective-permute-start(f32[40,384]{1,0:T(8,128)S(1)} %get-tuple-element.106.z_ref.refs_1_), channel_id=1, source_target_pairs={{1,2},{3,4},{5,6},{7,8},{9,10},{11,12},{13,14},{15,16},{17,18},{19... | collective-permute-start | bytes 184328 | tf_op jit(solution)/shard_map/ppermute | solution.py:470
  97.0 1.3 collective-permute-start.9
  97.1 1.8 %collective-permute-start.8 = (f32[40,384]{1,0:T(8,128)S(1)}, f32[40,384]{1,0:T(8,128)S(1)}, u32[]{:S(2)}, u32[]{:S(2)}) collective-permute-start(f32[40,384]{1,0:T(8,128)S(1)} %get-tuple-element.112.z_ref.refs_1_), channel_id=1, source_target_pairs={{1,2},{3,4},{5,6},{7,8},{9,10},{11,12},{13,14},{15,16},{17,18},{19... | collective-permute-start | bytes 184328 | tf_op jit(solution)/shard_map/ppermute | solution.py:470
  115.8 1.3 collective-permute-start.11
  115.8 1.8 %collective-permute-start.10 = (f32[40,384]{1,0:T(8,128)S(1)}, f32[40,384]{1,0:T(8,128)S(1)}, u32[]{:S(2)}, u32[]{:S(2)}) collective-permute-start(f32[40,384]{1,0:T(8,128)S(1)} %get-tuple-element.118.z_ref.refs_1_), channel_id=1, source_target_pairs={{1,2},{3,4},{5,6},{7,8},{9,10},{11,12},{13,14},{15,16},{17,18},{19... | collective-permute-start | bytes 184328 | tf_op jit(solution)/shard_map/ppermute | solution.py:470
  119.1 13.7 %all-to-all-start.6 = ((f32[32,1,128]{2,1,0:T(1,128)}), f32[32,1,128]{2,1,0:T(1,128)S(1)}, u32[]{:S(2)}, u32[]{:S(2)}) async-start(f32[32,1,128]{2,1,0:T(1,128)} %bitcast.22), calls=%async_computation.6 | async-start | bytes 32768 | tf_op jit(solution)/shard_map/all_to_all | solution.py:449

commit v6 on v5

--- a/solution.py
+++ b/solution.py
@@ -60,6 +60,7 @@
         self.width = nv * nb
         self.kwidth = ceil_to(self.width, 128)
         self.pair = 2 * ne
+        self.split = self.width * ne * 3 // 5 // CHUNK * CHUNK
 
 
 def to_wide(read, sz):
@@ -93,7 +94,7 @@
 
 def init_kernel(sz, me_ref, p_hbm, *refs):
     args, outs, held, sems, p_sem = refs[:11], refs[11:22], refs[22:33], refs[33], refs[34]
-    blocks = pltpu.make_async_copy(p_hbm, outs[10], p_sem)
+    blocks = pltpu.make_async_copy(p_hbm.at[:, : sz.split], outs[10], p_sem)
     blocks.start()
     fetch(list(zip(args, held)), sems)
     (res_ref, orders_ref, state_ref, nbr_ref, face_ref, orient_ref, source_ref, flux_ref, geo_ref, stiff_ref, trace_ref) = held
@@ -158,7 +159,7 @@
     blocks.wait()
 
 
-def apply_blocks(sz, vec, mask, blocks_ref):
+def apply_blocks(sz, vec, mask, blocks):
     nb, ne, nv, width = sz.nb, sz.ne, sz.nv, sz.width
     tall = jnp.concatenate([vec[:nb, v * ne : (v + 1) * ne] for v in range(nv)], axis=0)
     turned = pad_rows(tall, CHUNK).T
@@ -177,7 +178,7 @@
         entry = iota(size, 1) + low - (iota(size, 0) + 8 * first) * width
         lhs = jnp.where((entry >= 0) & (entry < width), turned[8 * first : 8 * last, : high - low], 0.0)
         out = lax.dot_general(
-            lhs.astype(BF16), blocks_ref[:, low:high], (((1,), (1,)), ((), ())), preferred_element_type=F32
+            lhs.astype(BF16), blocks(low, high), (((1,), (1,)), ((), ())), preferred_element_type=F32
         )
         for g in range(first, last):
             acc[g] = acc[g] + out[8 * (g - first) : 8 * (g - first + 1)]
@@ -187,19 +188,41 @@
     return pad_rows(wide, sz.nbp) * mask
 
 
-def precond_start_kernel(sz, red_ref, vec_ref, mask_ref, blocks_ref, state_ref, z_ref, v_ref, h_ref):
+def columns(sz, first_ref, rest_ref):
+    def read(low, high):
+        if high <= sz.split:
+            return first_ref[:, low:high]
+        return rest_ref[:, low - sz.split : high - sz.split]
+
+    return read
+
+
+def precond_start_kernel(
+    sz, red_ref, vec_ref, mask_ref, first_ref, state_ref, p_hbm, z_ref, v_ref, h_ref, rest_ref, sem
+):
+    rest = pltpu.make_async_copy(p_hbm.at[:, sz.split :], rest_ref, sem)
+    rest.start()
     norm = jnp.sqrt(total_scalars(red_ref[...], 1)[0] + EPSILON)
     new = vec_ref[...] * (1.0 / norm)
     v_ref[...] = new
     h_ref[...] = partial_rows([norm], 1)
-    z_ref[: sz.nbp] = apply_blocks(sz, new, mask_ref[...], blocks_ref)
+    stored = columns(sz, first_ref, rest_ref)
+    waited = []
+
+    def read(low, high):
+        if high > sz.split and not waited:
+            rest.wait()
+            waited.append(True)
+        return stored(low, high)
+
+    z_ref[: sz.nbp] = apply_blocks(sz, new, mask_ref[...], read)
     z_ref[sz.nbp :] = state_ref[...]
 
 
 def precond_kernel(sz, step, *refs):
-    red_ref, vec_ref, mask_ref, blocks_ref = refs[:4]
-    basis = refs[4 : 4 + step]
-    z_ref, v_ref, h_ref = refs[4 + step :]
+    red_ref, vec_ref, mask_ref, first_ref, rest_ref = refs[:5]
+    basis = refs[5 : 5 + step]
+    z_ref, v_ref, h_ref = refs[5 + step :]
     vec = vec_ref[...]
     scalars = total_scalars(red_ref[...], step + 1)
     proj, square = scalars[:step], scalars[step]
@@ -210,7 +233,7 @@
     new = vec * (1.0 / norm)
     v_ref[...] = new
     h_ref[...] = partial_rows(proj + [norm], 1)
-    z_ref[...] = apply_blocks(sz, new, mask_ref[...], blocks_ref)
+    z_ref[...] = apply_blocks(sz, new, mask_ref[...], columns(sz, first_ref, rest_ref))
 
 
 def roll_blocks(x, blocks, ne):
@@ -365,6 +388,11 @@
     hess_out[...] = fill_column(step, entries, hess_ref[...])[: ITERS + 1, :ITERS]
 
 
+def near_column_kernel(sz, step, *refs):
+    near_kernel(sz, *refs[:4], refs[8 + step])
+    column_kernel(sz, step - 1, *refs[4 : 8 + step], *refs[9 + step :])
+
+
 def near_kernel(sz, z_ref, chip_ref, hot_ref, near_ref, *outs):
     nbp = sz.nbp
     for i, out_ref in enumerate(outs):
@@ -372,26 +400,26 @@
         out_ref[...] = gather(sz, sources, [hot_ref.at[0], hot_ref.at[1]], near_ref)
 
 
-def gain_kernel(sz, z_ref, far_ref, hot_ref, near_ref, own_ref, turn_ref, seen_ref, gain_ref):
-    nbp = sz.nbp
-    tr = dot(own_ref[: 4 * sz.nqp], stack_rhs(split3(z_ref[nbp:]), 0))
-    seen = seen_ref[...] + gather(sz, [far_ref[nbp:]], [hot_ref.at[2]], near_ref)
-    gain_ref[...] = 1.0 + 0.5 * jnp.abs(tr + to_faces(sz, seen, turn_ref[...]))
-
-
 def image_kernel(sz, step, *refs):
     far_ref, hot_ref, near_ref, turn_ref, seen_ref, gain_ref, back_ref, vol_ref, tr_ref, mask_ref = refs[:10]
-    basis = refs[10 : 11 + step]
-    part_ref = refs[11 + step]
-    seen = seen_ref[...] + gather(sz, [far_ref[: sz.nbp]], [hot_ref.at[2]], near_ref)
-    other = to_faces(sz, seen, turn_ref[...])
-    flux = gain_ref[...] * (tr_ref[...] - other)
+    basis, refs = refs[10 : 11 + step], refs[11 + step :]
+    nbp, turn = sz.nbp, turn_ref[...]
+    if step == 0:
+        z_ref, own_ref, refs = refs[0], refs[1], refs[2:]
+        own = dot(own_ref[: 4 * sz.nqp], stack_rhs(split3(z_ref[nbp:]), 0))
+        seen = gain_ref[...] + gather(sz, [far_ref[nbp:]], [hot_ref.at[2]], near_ref)
+        gain = 1.0 + 0.5 * jnp.abs(own + to_faces(sz, seen, turn))
+        refs[2][...] = gain
+    else:
+        gain = gain_ref[...]
+    seen = seen_ref[...] + gather(sz, [far_ref[:nbp]], [hot_ref.at[2]], near_ref)
+    flux = gain * (tr_ref[...] - to_faces(sz, seen, turn))
     face = dot(back_ref[...], stack_rhs(split3(flux), 0))
     image = (vol_ref[...] + face) * mask_ref[...]
     if step < ITERS - 1:
-        refs[12 + step][...] = image
+        refs[1][...] = image
     values = [full_sum(b[...] * image) for b in basis] + [full_sum(image * image)]
-    part_ref[...] = partial_rows(values, sz.peers)
+    refs[0][...] = partial_rows(values, sz.peers)
 
 
 def call(kernel, name, out_shape, *args, specs=None, scratch=(), limit=24 * 2**20):
@@ -423,12 +451,12 @@
     lanes, nbp, nqp = sz.lanes, sz.nbp, sz.nqp
     me = lax.axis_index(AXES).astype(jnp.int32).reshape(1)
     wide = shape(nbp, lanes)
-    parts = shape(peers, 128)
+    parts = pltpu.VMEM((peers, 128), F32)
     fetched = [
         residual_in, orders.reshape(1, ne), state_coeffs, neighbours, neighbour_face, orientation, source, flux_jacobian,
         geometry, stiffness, jnp.transpose(trace_matrix, (1, 0, 2)),
     ]
-    start, mask, part, state, hot, coup, turn, own, near, back, blocks = call(
+    start, mask, part, state, hot, coup, turn, own, near, back, first = call(
         functools.partial(init_kernel, sz),
         "init",
         (
@@ -439,7 +467,7 @@
             shape(4 * nqp + 3 * nbp, 6 * nbp, dtype=BF16),
             shape(8 * nqp, 6 * nbp, dtype=BF16),
             shape(nbp, 24 * nqp, dtype=BF16),
-            shape(*precond.shape, dtype=BF16),
+            shape(sz.width, sz.split, dtype=BF16),
         ),
         me, *[pltpu.with_memory_space_constraint(a, pltpu.HBM) for a in [precond] + fetched],
         specs=[SMEM] + [ANY] * (1 + len(fetched)), scratch=copied(fetched) + [pltpu.SemaphoreType.DMA],
@@ -459,37 +487,42 @@
     state_shapes = (shape(2 * ITERS + 4, 128), shape(8, 128), wide, wide)
     for k in range(ITERS):
         red = exchange(part)
-        kernel = functools.partial(precond_kernel, sz, k) if k else functools.partial(precond_start_kernel, sz)
-        extra = basis if k else [state]
         previous = None if k == 0 else search
-        search, new, head = call(
-            kernel, f"precond{k}", (shape(nbp if k else 2 * nbp, lanes), wide, shape(1, 128)),
-            red, vec, mask, blocks, *extra,
-        )
+        if k == 0:
+            search, new, head, rest = call(
+                functools.partial(precond_start_kernel, sz), "precond0",
+                (shape(2 * nbp, lanes), wide, shape(1, 128), shape(sz.width, precond.shape[1] - sz.split, dtype=BF16)),
+                red, vec, mask, first, state, pltpu.with_memory_space_constraint(precond, pltpu.HBM),
+                specs=[VMEM] * 5 + [ANY], scratch=[pltpu.SemaphoreType.DMA],
+            )
+        else:
+            search, new, head = call(
+                functools.partial(precond_kernel, sz, k), f"precond{k}", (wide, wide, shape(1, 128)),
+                red, vec, mask, first, rest, *basis,
+            )
         basis = basis + [new]
         far = lax.ppermute(search, AXES, off_chip)
         chip = lax.ppermute(search, AXES, on_chip)
         vol, tr = call(functools.partial(local_kernel, sz), "local", (wide, face_shape), search, own, coup)
         if k == 0:
             turns, hess, total = head, head, head
+            seen, gain = call(
+                functools.partial(near_kernel, sz), "near", (seen_shape, seen_shape), search, chip, hot, near
+            )
         else:
-            turns, hess, total, new = call(
-                functools.partial(column_kernel, sz, k - 1), f"column{k}", state_shapes,
-                head, previous, turns, hess, total, *directions,
+            seen, turns, hess, total, new = call(
+                functools.partial(near_column_kernel, sz, k), f"near{k}", (seen_shape,) + state_shapes,
+                search, chip, hot, near, head, previous, turns, hess, total, *directions,
             )
             directions = directions + [new]
-        seen = call(
-            functools.partial(near_kernel, sz), "near", (seen_shape,) * (1 if k else 2), search, chip, hot, near
+        extra = basis + ([search, own] if k == 0 else [])
+        shapes = (parts,) if k == ITERS - 1 else (parts, wide, face_shape)[: 3 if k == 0 else 2]
+        outs = call(
+            functools.partial(image_kernel, sz, k), f"image{k}", shapes,
+            far, hot, near, turn, seen, gain, back, vol, tr, mask, *extra,
         )
-        if k == 0:
-            gain = call(
-                functools.partial(gain_kernel, sz), "gain", face_shape, search, far, hot, near, own, turn, seen[1]
-            )
-        outs = call(
-            functools.partial(image_kernel, sz, k), f"image{k}", (parts, wide) if k < ITERS - 1 else (parts,),
-            far, hot, near, turn, seen[0], gain, back, vol, tr, mask, *basis,
-        )
-        part, vec = outs if k < ITERS - 1 else (outs[0], None)
+        part, vec = outs[0], outs[1 % len(outs)]
+        gain = outs[2] if k == 0 else gain
     red = exchange(part)
     return call(
         functools.partial(finish_kernel, sz), "finish", (shape(nv, nb, ne), shape(ITERS + 1, ITERS)),

time: 134 us -> 134 us (level)
  blocking collectives: 82.5 us -> 96.1 us
  starting transfers between devices: 11 us -> 4.42 us
  waiting for transfers between devices: 7.85 us -> 1.35 us
    all_to_all x6 -> x7, blocking collectives: 82.5 us -> 96.1 us  [exchange(): return lax.all_to_all(rows, AXES, 0, 0, tiled=True)]
    all_to_all x1 -> x0, starting transfers between devices: 6.58 us -> none  [exchange(): return lax.all_to_all(rows, AXES, 0, 0, tiled=True)]
    all_to_all x1 -> x0, waiting for transfers between devices: 6.49 us -> none  [exchange(): return lax.all_to_all(rows, AXES, 0, 0, tiled=True)]
    pallas_call x32 -> x26, Pallas kernels: 31.4 us -> 30.9 us  [call(): pl.pallas_call(kernel, name=name, out_shape=out_shape, in_specs=specs or...]
  transfers between devices with their start and end apart: 13 -> 12, of which waited for: 7 -> 6; matrix products, arithmetic and copies ran while one was open for 0% -> 0% of each run, Pallas kernels for 5% -> 4%
where the time goes in v6:
time: 134 us
  blocking collectives  96.1 us (72%)
  Pallas kernels  30.9 us (23%)
  starting transfers between devices  4.42 us (3%)
  waiting for transfers between devices  1.35 us (1%)
    all_to_all x7, blocking collectives, exchange(): return lax.all_to_all(rows, AXES, 0, 0, tiled=True)  96.1 us
    pallas_call x26, Pallas kernels, call(): pl.pallas_call(kernel, name=name, out_shape=out_shape, in_specs=specs or...  30.9 us
    ppermute x6, starting transfers between devices, body(): far = lax.ppermute(search, AXES, off_chip)  3.99 us
  transfers between devices with their start and end apart: 12, of which 6 were waited for; matrix products, arithmetic and copies ran while one was open for 0% of the time, Pallas kernels for 4%

profile of v6, /device:TPU:0, one launch (start us, length us, event | category | flops | bytes accessed | tf_op | source)
XLA Modules:
  0.0 133.7 jit_solution(15136778216793483603)
XLA Ops:
  0.6 2.7 %init.1 = (f32[40,384]{1,0:T(8,128)S(1)}, f32[40,384]{1,0:T(8,128)S(1)}, f32[32,128]{1,0:T(8,128)S(1)}, f32[40,384]{1,0:T(8,128)S(1)}, bf16[3,512,256]{2,1,0:T(8...) custom-call(s32[1]{0:T(128)} %bitcast.me_ref, ...), custom_call_target="tpu_custom_call" | custom-call | tf_op jit(solution)/shard_map/init/pallas_call | solution.py:426
  3.4 14.3 %all_to_all.77 = f32[32,1,128]{2,1,0:T(1,128)S(1)} all-to-all(f32[32,1,128]{2,1,0:T(1,128)S(1)} %bitcast.39), channel_id=1, replica_groups=mesh['dom'=8,'grp'=4] {'dom','grp'}, dimensions={0} | all-to-all | bytes 32768 | tf_op jit(solution)/shard_map/all_to_all | solution.py:477
  17.7 4.1 %precond0.1 = (f32[80,384]{1,0:T(8,128)S(1)}, f32[40,384]{1,0:T(8,128)S(1)}, f32[1,128]{1,0:T(1,128)S(1)}, bf16[210,5504]{1,0:T(8,128)(2,1)S(1)}) custom-call(f32[32,128]{1,0:T(8,128)S(1)} %bitcast.33, f32[40,384]{1,0:T(8,128)S(1)} %get-tuple-element.83.vec_ref, f32[40,384]{1,0:T(8,128)S(1)} %get-tuple-element.84.mask_ref.refs_9_.refs_2_, ...), custom_call_target="tpu_custom_call" | custom-call | tf_op jit(solution)/shard_map/precond0/pallas_call | solution.py:426
  21.8 0.1 collective-permute-start.1
  21.9 0.7 collective-permute-start
  22.5 0.3 local.6
  22.9 0.3 collective-permute-done.1.chip_ref
  23.2 0.8 near.1
  23.9 0.0 collective-permute-done.refs_0_
  24.0 1.0 image0.1
  25.0 13.9 %all_to_all.78 = f32[32,1,128]{2,1,0:T(1,128)S(1)} all-to-all(f32[32,1,128]{2,1,0:T(1,128)S(1)} %bitcast.40), channel_id=1, replica_groups=mesh['dom'=8,'grp'=4] {'dom','grp'}, dimensions={0} | all-to-all | bytes 32768 | tf_op jit(solution)/shard_map/all_to_all | solution.py:477
  38.9 2.5 %precond1.1 = (f32[40,384]{1,0:T(8,128)S(1)}, f32[40,384]{1,0:T(8,128)S(1)}, f32[1,128]{1,0:T(1,128)S(1)}) custom-call(f32[32,128]{1,0:T(8,128)S(1)} %bitcast.37, f32[40,384]{1,0:T(8,128)S(1)} %get-tuple-element.100.refs_1_, f32[40,384]{1,0:T(8,128)S(1)} %get-tuple-element.84.mask_ref.refs_9_.refs_2_, ...), custom_call_target="tpu_custom_call" | custom-call | tf_op jit(solution)/shard_map/precond1/pallas_call | solution.py:426
  41.4 0.1 collective-permute-start.3
  41.5 0.7 collective-permute-start.2
  42.1 0.3 local.7
  42.5 0.2 collective-permute-done.3.refs_1_
  42.7 0.6 near1.1
  43.3 0.0 collective-permute-done.2.refs_0_
  43.3 0.8 image1.1
  44.1 13.6 %all_to_all.79 = f32[32,1,128]{2,1,0:T(1,128)S(1)} all-to-all(f32[32,1,128]{2,1,0:T(1,128)S(1)} %bitcast.41), channel_id=1, replica_groups=mesh['dom'=8,'grp'=4] {'dom','grp'}, dimensions={0} | all-to-all | bytes 32768 | tf_op jit(solution)/shard_map/all_to_all | solution.py:477
  57.7 2.5 %precond2.1 = (f32[40,384]{1,0:T(8,128)S(1)}, f32[40,384]{1,0:T(8,128)S(1)}, f32[1,128]{1,0:T(1,128)S(1)}) custom-call(f32[32,128]{1,0:T(8,128)S(1)} %bitcast.34, f32[40,384]{1,0:T(8,128)S(1)} %get-tuple-element.111.refs_1_, f32[40,384]{1,0:T(8,128)S(1)} %get-tuple-element.84.mask_ref.refs_9_.refs_2_, ...), custom_call_target="tpu_custom_call" | custom-call | tf_op jit(solution)/shard_map/precond2/pallas_call | solution.py:426
  60.1 0.1 collective-permute-start.5
  60.2 0.7 collective-permute-start.4
  60.9 0.3 local.8
  61.2 0.2 collective-permute-done.5.refs_1_
  61.5 0.6 near2.1
  62.0 0.0 collective-permute-done.4.refs_0_
  62.1 0.8 image2.1
  62.9 13.6 %all_to_all.80 = f32[32,1,128]{2,1,0:T(1,128)S(1)} all-to-all(f32[32,1,128]{2,1,0:T(1,128)S(1)} %bitcast.42), channel_id=1, replica_groups=mesh['dom'=8,'grp'=4] {'dom','grp'}, dimensions={0} | all-to-all | bytes 32768 | tf_op jit(solution)/shard_map/all_to_all | solution.py:477
  76.5 2.5 %precond3.1 = (f32[40,384]{1,0:T(8,128)S(1)}, f32[40,384]{1,0:T(8,128)S(1)}, f32[1,128]{1,0:T(1,128)S(1)}) custom-call(f32[32,128]{1,0:T(8,128)S(1)} %bitcast.35, f32[40,384]{1,0:T(8,128)S(1)} %get-tuple-element.123.refs_1_, f32[40,384]{1,0:T(8,128)S(1)} %get-tuple-element.84.mask_ref.refs_9_.refs_2_, ...), custom_call_target="tpu_custom_call" | custom-call | tf_op jit(solution)/shard_map/precond3/pallas_call | solution.py:426
  78.9 0.1 collective-permute-start.7
  79.0 0.7 collective-permute-start.6
  79.7 0.3 local.9
  80.0 0.2 collective-permute-done.7.refs_1_
  80.2 0.6 near3.1
  80.8 0.0 collective-permute-done.6.refs_0_
  80.8 0.8 image3.1
  81.7 13.6 %all_to_all.81 = f32[32,1,128]{2,1,0:T(1,128)S(1)} all-to-all(f32[32,1,128]{2,1,0:T(1,128)S(1)} %bitcast.43), channel_id=1, replica_groups=mesh['dom'=8,'grp'=4] {'dom','grp'}, dimensions={0} | all-to-all | bytes 32768 | tf_op jit(solution)/shard_map/all_to_all | solution.py:477
  95.2 2.5 %precond4.1 = (f32[40,384]{1,0:T(8,128)S(1)}, f32[40,384]{1,0:T(8,128)S(1)}, f32[1,128]{1,0:T(1,128)S(1)}) custom-call(f32[32,128]{1,0:T(8,128)S(1)} %bitcast.36, f32[40,384]{1,0:T(8,128)S(1)} %get-tuple-element.135.refs_1_, f32[40,384]{1,0:T(8,128)S(1)} %get-tuple-element.84.mask_ref.refs_9_.refs_2_, ...), custom_call_target="tpu_custom_call" | custom-call | tf_op jit(solution)/shard_map/precond4/pallas_call | solution.py:426
  97.7 0.1 collective-permute-start.9
  97.8 0.7 collective-permute-start.8
  98.5 0.3 local.10
  98.8 0.2 collective-permute-done.9.refs_1_
  99.0 0.6 near4.1
  99.6 0.0 collective-permute-done.8.refs_0_
  99.6 0.9 image4.1
  100.5 13.6 %all_to_all.82 = f32[32,1,128]{2,1,0:T(1,128)S(1)} all-to-all(f32[32,1,128]{2,1,0:T(1,128)S(1)} %bitcast.44), channel_id=1, replica_groups=mesh['dom'=8,'grp'=4] {'dom','grp'}, dimensions={0} | all-to-all | bytes 32768 | tf_op jit(solution)/shard_map/all_to_all | solution.py:477
  114.0 2.5 %precond5.1 = (f32[40,384]{1,0:T(8,128)S(1)}, f32[40,384]{1,0:T(8,128)S(1)}, f32[1,128]{1,0:T(1,128)S(1)}) custom-call(f32[32,128]{1,0:T(8,128)S(1)} %bitcast.32, f32[40,384]{1,0:T(8,128)S(1)} %get-tuple-element.147.refs_1_, f32[40,384]{1,0:T(8,128)S(1)} %get-tuple-element.84.mask_ref.refs_9_.refs_2_, ...), custom_call_target="tpu_custom_call" | custom-call | tf_op jit(solution)/shard_map/precond5/pallas_call | solution.py:426
  116.5 0.1 collective-permute-start.11
  116.6 0.7 collective-permute-start.10
  117.2 0.3 local.11
  117.6 0.2 collective-permute-done.11.refs_1_
  117.8 0.6 near5.1
  118.4 0.0 collective-permute-done.10.refs_0_
  118.4 0.9 image5.1
  119.3 13.6 %all_to_all.83 = f32[32,1,128]{2,1,0:T(1,128)S(1)} all-to-all(f32[32,1,128]{2,1,0:T(1,128)S(1)} %bitcast.31), channel_id=1, replica_groups=mesh['dom'=8,'grp'=4] {'dom','grp'}, dimensions={0} | all-to-all | bytes 32768 | tf_op jit(solution)/shard_map/all_to_all | solution.py:477
  132.8 0.9 finish.1
Async XLA Ops:
  21.8 1.4 %collective-permute-start.1 = (f32[80,384]{1,0:T(8,128)S(1)}, f32[80,384]{1,0:T(8,128)S(1)}, u32[]{:S(2)}, u32[]{:S(2)}) collective-permute-start(f32[80,384]{1,0:T(8,128)S(1)} %get-tuple-element.87.z_ref.refs_11_.refs_5_), channel_id=1, source_target_pairs={{0,1},{1,0},{2,3},{3,2},{4,5},{5,4},{6,7},{7,6},{8,9},{9,8},{10,11... | collective-permute-start | bytes 368648 | tf_op jit(solution)/shard_map/ppermute | solution.py:505
  21.9 2.1 %collective-permute-start = (f32[80,384]{1,0:T(8,128)S(1)}, f32[80,384]{1,0:T(8,128)S(1)}, u32[]{:S(2)}, u32[]{:S(2)}) collective-permute-start(f32[80,384]{1,0:T(8,128)S(1)} %get-tuple-element.87.z_ref.refs_11_.refs_5_), channel_id=1, source_target_pairs={{1,2},{3,4},{5,6},{7,8},{9,10},{11,12},{13,14},{15,16},{17,18},{19... | collective-permute-start | bytes 368648 | tf_op jit(solution)/shard_map/ppermute | solution.py:504
  41.4 1.3 collective-permute-start.3
  41.5 1.8 %collective-permute-start.2 = (f32[40,384]{1,0:T(8,128)S(1)}, f32[40,384]{1,0:T(8,128)S(1)}, u32[]{:S(2)}, u32[]{:S(2)}) collective-permute-start(f32[40,384]{1,0:T(8,128)S(1)} %get-tuple-element.102.refs_0_.z_ref.refs_5_), channel_id=1, source_target_pairs={{1,2},{3,4},{5,6},{7,8},{9,10},{11,12},{13,14},{15,16},{17,18},{19... | collective-permute-start | bytes 184328 | tf_op jit(solution)/shard_map/ppermute | solution.py:504
  60.1 1.3 collective-permute-start.5
  60.2 1.8 %collective-permute-start.4 = (f32[40,384]{1,0:T(8,128)S(1)}, f32[40,384]{1,0:T(8,128)S(1)}, u32[]{:S(2)}, u32[]{:S(2)}) collective-permute-start(f32[40,384]{1,0:T(8,128)S(1)} %get-tuple-element.112.refs_0_.z_ref.refs_5_), channel_id=1, source_target_pairs={{1,2},{3,4},{5,6},{7,8},{9,10},{11,12},{13,14},{15,16},{17,18},{19... | collective-permute-start | bytes 184328 | tf_op jit(solution)/shard_map/ppermute | solution.py:504
  78.9 1.3 collective-permute-start.7
  79.0 1.8 %collective-permute-start.6 = (f32[40,384]{1,0:T(8,128)S(1)}, f32[40,384]{1,0:T(8,128)S(1)}, u32[]{:S(2)}, u32[]{:S(2)}) collective-permute-start(f32[40,384]{1,0:T(8,128)S(1)} %get-tuple-element.124.refs_0_.z_ref.refs_5_), channel_id=1, source_target_pairs={{1,2},{3,4},{5,6},{7,8},{9,10},{11,12},{13,14},{15,16},{17,18},{19... | collective-permute-start | bytes 184328 | tf_op jit(solution)/shard_map/ppermute | solution.py:504
  97.7 1.3 collective-permute-start.9
  97.8 1.8 %collective-permute-start.8 = (f32[40,384]{1,0:T(8,128)S(1)}, f32[40,384]{1,0:T(8,128)S(1)}, u32[]{:S(2)}, u32[]{:S(2)}) collective-permute-start(f32[40,384]{1,0:T(8,128)S(1)} %get-tuple-element.136.refs_0_.z_ref.refs_5_), channel_id=1, source_target_pairs={{1,2},{3,4},{5,6},{7,8},{9,10},{11,12},{13,14},{15,16},{17,18},{19... | collective-permute-start | bytes 184328 | tf_op jit(solution)/shard_map/ppermute | solution.py:504
  116.5 1.3 collective-permute-start.11
  116.6 1.8 %collective-permute-start.10 = (f32[40,384]{1,0:T(8,128)S(1)}, f32[40,384]{1,0:T(8,128)S(1)}, u32[]{:S(2)}, u32[]{:S(2)}) collective-permute-start(f32[40,384]{1,0:T(8,128)S(1)} %get-tuple-element.148.refs_0_.z_ref.refs_1_), channel_id=1, source_target_pairs={{1,2},{3,4},{5,6},{7,8},{9,10},{11,12},{13,14},{15,16},{17,18},{19... | collective-permute-start | bytes 184328 | tf_op jit(solution)/shard_map/ppermute | solution.py:504

commit v7 on v6

--- a/solution.py
+++ b/solution.py
@@ -60,7 +60,6 @@
         self.width = nv * nb
         self.kwidth = ceil_to(self.width, 128)
         self.pair = 2 * ne
-        self.split = self.width * ne * 3 // 5 // CHUNK * CHUNK
 
 
 def to_wide(read, sz):
@@ -88,15 +87,16 @@
     copies = [pltpu.make_async_copy(src, dst, sems.at[i]) for i, (src, dst) in enumerate(pairs)]
     for copy in copies:
         copy.start()
-    for copy in copies:
-        copy.wait()
+    return copies
 
 
 def init_kernel(sz, me_ref, p_hbm, *refs):
     args, outs, held, sems, p_sem = refs[:11], refs[11:22], refs[22:33], refs[33], refs[34]
-    blocks = pltpu.make_async_copy(p_hbm.at[:, : sz.split], outs[10], p_sem)
+    small = fetch(list(zip(args, held)), sems)
+    blocks = pltpu.make_async_copy(p_hbm, outs[10], p_sem)
     blocks.start()
-    fetch(list(zip(args, held)), sems)
+    for copy in small:
+        copy.wait()
     (res_ref, orders_ref, state_ref, nbr_ref, face_ref, orient_ref, source_ref, flux_ref, geo_ref, stiff_ref, trace_ref) = held
     start_ref, mask_ref, part_ref, state2_ref, hot_ref, coup_ref, turn_ref, own_ref, near_ref, back_ref = outs[:10]
     nv, nb, ne, nq, nbp, nqp = sz.nv, sz.nb, sz.ne, sz.nq, sz.nbp, sz.nqp
@@ -159,7 +159,7 @@
     blocks.wait()
 
 
-def apply_blocks(sz, vec, mask, blocks):
+def apply_blocks(sz, vec, mask, blocks_ref):
     nb, ne, nv, width = sz.nb, sz.ne, sz.nv, sz.width
     tall = jnp.concatenate([vec[:nb, v * ne : (v + 1) * ne] for v in range(nv)], axis=0)
     turned = pad_rows(tall, CHUNK).T
@@ -178,7 +178,7 @@
         entry = iota(size, 1) + low - (iota(size, 0) + 8 * first) * width
         lhs = jnp.where((entry >= 0) & (entry < width), turned[8 * first : 8 * last, : high - low], 0.0)
         out = lax.dot_general(
-            lhs.astype(BF16), blocks(low, high), (((1,), (1,)), ((), ())), preferred_element_type=F32
+            lhs.astype(BF16), blocks_ref[:, low:high], (((1,), (1,)), ((), ())), preferred_element_type=F32
         )
         for g in range(first, last):
             acc[g] = acc[g] + out[8 * (g - first) : 8 * (g - first + 1)]
@@ -188,41 +188,19 @@
     return pad_rows(wide, sz.nbp) * mask
 
 
-def columns(sz, first_ref, rest_ref):
-    def read(low, high):
-        if high <= sz.split:
-            return first_ref[:, low:high]
-        return rest_ref[:, low - sz.split : high - sz.split]
-
-    return read
-
-
-def precond_start_kernel(
-    sz, red_ref, vec_ref, mask_ref, first_ref, state_ref, p_hbm, z_ref, v_ref, h_ref, rest_ref, sem
-):
-    rest = pltpu.make_async_copy(p_hbm.at[:, sz.split :], rest_ref, sem)
-    rest.start()
+def precond_start_kernel(sz, red_ref, vec_ref, mask_ref, blocks_ref, state_ref, z_ref, v_ref, h_ref):
     norm = jnp.sqrt(total_scalars(red_ref[...], 1)[0] + EPSILON)
     new = vec_ref[...] * (1.0 / norm)
     v_ref[...] = new
     h_ref[...] = partial_rows([norm], 1)
-    stored = columns(sz, first_ref, rest_ref)
-    waited = []
-
-    def read(low, high):
-        if high > sz.split and not waited:
-            rest.wait()
-            waited.append(True)
-        return stored(low, high)
-
-    z_ref[: sz.nbp] = apply_blocks(sz, new, mask_ref[...], read)
+    z_ref[: sz.nbp] = apply_blocks(sz, new, mask_ref[...], blocks_ref)
     z_ref[sz.nbp :] = state_ref[...]
 
 
 def precond_kernel(sz, step, *refs):
-    red_ref, vec_ref, mask_ref, first_ref, rest_ref = refs[:5]
-    basis = refs[5 : 5 + step]
-    z_ref, v_ref, h_ref = refs[5 + step :]
+    red_ref, vec_ref, mask_ref, blocks_ref = refs[:4]
+    basis = refs[4 : 4 + step]
+    z_ref, v_ref, h_ref = refs[4 + step :]
     vec = vec_ref[...]
     scalars = total_scalars(red_ref[...], step + 1)
     proj, square = scalars[:step], scalars[step]
@@ -233,7 +211,7 @@
     new = vec * (1.0 / norm)
     v_ref[...] = new
     h_ref[...] = partial_rows(proj + [norm], 1)
-    z_ref[...] = apply_blocks(sz, new, mask_ref[...], columns(sz, first_ref, rest_ref))
+    z_ref[...] = apply_blocks(sz, new, mask_ref[...], blocks_ref)
 
 
 def roll_blocks(x, blocks, ne):
@@ -456,7 +434,7 @@
         residual_in, orders.reshape(1, ne), state_coeffs, neighbours, neighbour_face, orientation, source, flux_jacobian,
         geometry, stiffness, jnp.transpose(trace_matrix, (1, 0, 2)),
     ]
-    start, mask, part, state, hot, coup, turn, own, near, back, first = call(
+    start, mask, part, state, hot, coup, turn, own, near, back, blocks = call(
         functools.partial(init_kernel, sz),
         "init",
         (
@@ -467,7 +445,7 @@
             shape(4 * nqp + 3 * nbp, 6 * nbp, dtype=BF16),
             shape(8 * nqp, 6 * nbp, dtype=BF16),
             shape(nbp, 24 * nqp, dtype=BF16),
-            shape(sz.width, sz.split, dtype=BF16),
+            shape(*precond.shape, dtype=BF16),
         ),
         me, *[pltpu.with_memory_space_constraint(a, pltpu.HBM) for a in [precond] + fetched],
         specs=[SMEM] + [ANY] * (1 + len(fetched)), scratch=copied(fetched) + [pltpu.SemaphoreType.DMA],
@@ -489,16 +467,14 @@
         red = exchange(part)
         previous = None if k == 0 else search
         if k == 0:
-            search, new, head, rest = call(
-                functools.partial(precond_start_kernel, sz), "precond0",
-                (shape(2 * nbp, lanes), wide, shape(1, 128), shape(sz.width, precond.shape[1] - sz.split, dtype=BF16)),
-                red, vec, mask, first, state, pltpu.with_memory_space_constraint(precond, pltpu.HBM),
-                specs=[VMEM] * 5 + [ANY], scratch=[pltpu.SemaphoreType.DMA],
+            search, new, head = call(
+                functools.partial(precond_start_kernel, sz), "precond0", (shape(2 * nbp, lanes), wide, shape(1, 128)),
+                red, vec, mask, blocks, state,
             )
         else:
             search, new, head = call(
                 functools.partial(precond_kernel, sz, k), f"precond{k}", (wide, wide, shape(1, 128)),
-                red, vec, mask, first, rest, *basis,
+                red, vec, mask, blocks, *basis,
             )
         basis = basis + [new]
         far = lax.ppermute(search, AXES, off_chip)

time: 134 us -> 133 us (level)
  Pallas kernels: 30.9 us -> 29.5 us
    pallas_call x26, Pallas kernels: 30.9 us -> 29.5 us  [call(): pl.pallas_call(kernel, name=name, out_shape=out_shape, in_specs=specs or...]
where the time goes in v7:
time: 133 us; the launch traced here: 132 us
  blocking collectives  96.1 us (72%)
  Pallas kernels  29.5 us (22%)
  starting transfers between devices  4.42 us (3%)
  waiting for transfers between devices  1.37 us (1%)
    all_to_all x7, blocking collectives, exchange(): return lax.all_to_all(rows, AXES, 0, 0, tiled=True)  96.1 us
    pallas_call x26, Pallas kernels, call(): pl.pallas_call(kernel, name=name, out_shape=out_shape, in_specs=specs or...  29.5 us
    ppermute x6, starting transfers between devices, body(): far = lax.ppermute(search, AXES, off_chip)  3.99 us
  transfers between devices with their start and end apart: 12, of which 6 were waited for; matrix products, arithmetic and copies ran while one was open for 0% of the time, Pallas kernels for 4%

profile of v7, /device:TPU:0, one launch (start us, length us, event | category | flops | bytes accessed | tf_op | source)
XLA Modules:
  0.0 132.2 jit_solution(15769202186861135758)
XLA Ops:
  0.6 3.0 %init.1 = (f32[40,384]{1,0:T(8,128)S(1)}, f32[40,384]{1,0:T(8,128)S(1)}, f32[32,128]{1,0:T(8,128)S(1)}, f32[40,384]{1,0:T(8,128)S(1)}, bf16[3,512,256]{2,1,0:T(8...) custom-call(s32[1]{0:T(128)} %bitcast.me_ref, ...), custom_call_target="tpu_custom_call" | custom-call | tf_op jit(solution)/shard_map/init/pallas_call | solution.py:404
  3.7 14.3 %all_to_all.77 = f32[32,1,128]{2,1,0:T(1,128)S(1)} all-to-all(f32[32,1,128]{2,1,0:T(1,128)S(1)} %bitcast.39), channel_id=1, replica_groups=mesh['dom'=8,'grp'=4] {'dom','grp'}, dimensions={0} | all-to-all | bytes 32768 | tf_op jit(solution)/shard_map/all_to_all | solution.py:455
  18.0 2.3 %precond0.1 = (f32[80,384]{1,0:T(8,128)S(1)}, f32[40,384]{1,0:T(8,128)S(1)}, f32[1,128]{1,0:T(1,128)S(1)}) custom-call(f32[32,128]{1,0:T(8,128)S(1)} %bitcast.33, f32[40,384]{1,0:T(8,128)S(1)} %get-tuple-element.82.vec_ref, f32[40,384]{1,0:T(8,128)S(1)} %get-tuple-element.83.mask_ref.refs_9_.refs_2_, ...), custom_call_target="tpu_custom_call" | custom-call | tf_op jit(solution)/shard_map/precond0/pallas_call | solution.py:404
  20.4 0.1 collective-permute-start.1
  20.4 0.7 collective-permute-start
  21.1 0.3 local.6
  21.5 0.3 collective-permute-done.1.chip_ref
  21.8 0.8 near.1
  22.5 0.0 collective-permute-done.refs_0_
  22.5 1.0 image0.1
  23.5 14.0 %all_to_all.78 = f32[32,1,128]{2,1,0:T(1,128)S(1)} all-to-all(f32[32,1,128]{2,1,0:T(1,128)S(1)} %bitcast.40), channel_id=1, replica_groups=mesh['dom'=8,'grp'=4] {'dom','grp'}, dimensions={0} | all-to-all | bytes 32768 | tf_op jit(solution)/shard_map/all_to_all | solution.py:455
  37.5 2.4 %precond1.1 = (f32[40,384]{1,0:T(8,128)S(1)}, f32[40,384]{1,0:T(8,128)S(1)}, f32[1,128]{1,0:T(1,128)S(1)}) custom-call(f32[32,128]{1,0:T(8,128)S(1)} %bitcast.37, f32[40,384]{1,0:T(8,128)S(1)} %get-tuple-element.99.refs_1_, f32[40,384]{1,0:T(8,128)S(1)} %get-tuple-element.83.mask_ref.refs_9_.refs_2_, ...), custom_call_target="tpu_custom_call" | custom-call | tf_op jit(solution)/shard_map/precond1/pallas_call | solution.py:404
  39.9 0.1 collective-permute-start.3
  40.0 0.7 collective-permute-start.2
  40.7 0.3 local.7
  41.0 0.2 collective-permute-done.3.refs_1_
  41.3 0.6 near1.1
  41.8 0.0 collective-permute-done.2.refs_0_
  41.9 0.8 image1.1
  42.7 13.6 %all_to_all.79 = f32[32,1,128]{2,1,0:T(1,128)S(1)} all-to-all(f32[32,1,128]{2,1,0:T(1,128)S(1)} %bitcast.41), channel_id=1, replica_groups=mesh['dom'=8,'grp'=4] {'dom','grp'}, dimensions={0} | all-to-all | bytes 32768 | tf_op jit(solution)/shard_map/all_to_all | solution.py:455
  56.3 2.5 %precond2.1 = (f32[40,384]{1,0:T(8,128)S(1)}, f32[40,384]{1,0:T(8,128)S(1)}, f32[1,128]{1,0:T(1,128)S(1)}) custom-call(f32[32,128]{1,0:T(8,128)S(1)} %bitcast.34, f32[40,384]{1,0:T(8,128)S(1)} %get-tuple-element.109.refs_1_, f32[40,384]{1,0:T(8,128)S(1)} %get-tuple-element.83.mask_ref.refs_9_.refs_2_, ...), custom_call_target="tpu_custom_call" | custom-call | tf_op jit(solution)/shard_map/precond2/pallas_call | solution.py:404
  58.7 0.1 collective-permute-start.5
  58.8 0.7 collective-permute-start.4
  59.5 0.3 local.8
  59.8 0.2 collective-permute-done.5.refs_1_
  60.0 0.6 near2.1
  60.6 0.0 collective-permute-done.4.refs_0_
  60.6 0.8 image2.1
  61.5 13.6 %all_to_all.80 = f32[32,1,128]{2,1,0:T(1,128)S(1)} all-to-all(f32[32,1,128]{2,1,0:T(1,128)S(1)} %bitcast.42), channel_id=1, replica_groups=mesh['dom'=8,'grp'=4] {'dom','grp'}, dimensions={0} | all-to-all | bytes 32768 | tf_op jit(solution)/shard_map/all_to_all | solution.py:455
  75.0 2.5 %precond3.1 = (f32[40,384]{1,0:T(8,128)S(1)}, f32[40,384]{1,0:T(8,128)S(1)}, f32[1,128]{1,0:T(1,128)S(1)}) custom-call(f32[32,128]{1,0:T(8,128)S(1)} %bitcast.35, f32[40,384]{1,0:T(8,128)S(1)} %get-tuple-element.121.refs_1_, f32[40,384]{1,0:T(8,128)S(1)} %get-tuple-element.83.mask_ref.refs_9_.refs_2_, ...), custom_call_target="tpu_custom_call" | custom-call | tf_op jit(solution)/shard_map/precond3/pallas_call | solution.py:404
  77.5 0.1 collective-permute-start.7
  77.6 0.7 collective-permute-start.6
  78.2 0.3 local.9
  78.6 0.2 collective-permute-done.7.refs_1_
  78.8 0.6 near3.1
  79.4 0.0 collective-permute-done.6.refs_0_
  79.4 0.8 image3.1
  80.2 13.6 %all_to_all.81 = f32[32,1,128]{2,1,0:T(1,128)S(1)} all-to-all(f32[32,1,128]{2,1,0:T(1,128)S(1)} %bitcast.43), channel_id=1, replica_groups=mesh['dom'=8,'grp'=4] {'dom','grp'}, dimensions={0} | all-to-all | bytes 32768 | tf_op jit(solution)/shard_map/all_to_all | solution.py:455
  93.8 2.5 %precond4.1 = (f32[40,384]{1,0:T(8,128)S(1)}, f32[40,384]{1,0:T(8,128)S(1)}, f32[1,128]{1,0:T(1,128)S(1)}) custom-call(f32[32,128]{1,0:T(8,128)S(1)} %bitcast.36, f32[40,384]{1,0:T(8,128)S(1)} %get-tuple-element.133.refs_1_, f32[40,384]{1,0:T(8,128)S(1)} %get-tuple-element.83.mask_ref.refs_9_.refs_2_, ...), custom_call_target="tpu_custom_call" | custom-call | tf_op jit(solution)/shard_map/precond4/pallas_call | solution.py:404
  96.3 0.1 collective-permute-start.9
  96.3 0.7 collective-permute-start.8
  97.0 0.3 local.10
  97.4 0.2 collective-permute-done.9.refs_1_
  97.6 0.6 near4.1
  98.2 0.0 collective-permute-done.8.refs_0_
  98.2 0.9 image4.1
  99.0 13.6 %all_to_all.82 = f32[32,1,128]{2,1,0:T(1,128)S(1)} all-to-all(f32[32,1,128]{2,1,0:T(1,128)S(1)} %bitcast.44), channel_id=1, replica_groups=mesh['dom'=8,'grp'=4] {'dom','grp'}, dimensions={0} | all-to-all | bytes 32768 | tf_op jit(solution)/shard_map/all_to_all | solution.py:455
  112.6 2.5 %precond5.1 = (f32[40,384]{1,0:T(8,128)S(1)}, f32[40,384]{1,0:T(8,128)S(1)}, f32[1,128]{1,0:T(1,128)S(1)}) custom-call(f32[32,128]{1,0:T(8,128)S(1)} %bitcast.32, f32[40,384]{1,0:T(8,128)S(1)} %get-tuple-element.145.refs_1_, f32[40,384]{1,0:T(8,128)S(1)} %get-tuple-element.83.mask_ref.refs_9_.refs_2_, ...), custom_call_target="tpu_custom_call" | custom-call | tf_op jit(solution)/shard_map/precond5/pallas_call | solution.py:404
  115.1 0.1 collective-permute-start.11
  115.1 0.7 collective-permute-start.10
  115.8 0.3 local.11
  116.2 0.2 collective-permute-done.11.refs_1_
  116.4 0.6 near5.1
  117.0 0.0 collective-permute-done.10.refs_0_
  117.0 0.9 image5.1
  117.8 13.6 %all_to_all.83 = f32[32,1,128]{2,1,0:T(1,128)S(1)} all-to-all(f32[32,1,128]{2,1,0:T(1,128)S(1)} %bitcast.31), channel_id=1, replica_groups=mesh['dom'=8,'grp'=4] {'dom','grp'}, dimensions={0} | all-to-all | bytes 32768 | tf_op jit(solution)/shard_map/all_to_all | solution.py:455
  131.4 0.9 finish.1
Async XLA Ops:
  20.4 1.4 %collective-permute-start.1 = (f32[80,384]{1,0:T(8,128)S(1)}, f32[80,384]{1,0:T(8,128)S(1)}, u32[]{:S(2)}, u32[]{:S(2)}) collective-permute-start(f32[80,384]{1,0:T(8,128)S(1)} %get-tuple-element.86.z_ref.refs_11_.refs_5_), channel_id=1, source_target_pairs={{0,1},{1,0},{2,3},{3,2},{4,5},{5,4},{6,7},{7,6},{8,9},{9,8},{10,11... | collective-permute-start | bytes 368648 | tf_op jit(solution)/shard_map/ppermute | solution.py:481
  20.4 2.1 %collective-permute-start = (f32[80,384]{1,0:T(8,128)S(1)}, f32[80,384]{1,0:T(8,128)S(1)}, u32[]{:S(2)}, u32[]{:S(2)}) collective-permute-start(f32[80,384]{1,0:T(8,128)S(1)} %get-tuple-element.86.z_ref.refs_11_.refs_5_), channel_id=1, source_target_pairs={{1,2},{3,4},{5,6},{7,8},{9,10},{11,12},{13,14},{15,16},{17,18},{19... | collective-permute-start | bytes 368648 | tf_op jit(solution)/shard_map/ppermute | solution.py:480
  39.9 1.3 collective-permute-start.3
  40.0 1.8 %collective-permute-start.2 = (f32[40,384]{1,0:T(8,128)S(1)}, f32[40,384]{1,0:T(8,128)S(1)}, u32[]{:S(2)}, u32[]{:S(2)}) collective-permute-start(f32[40,384]{1,0:T(8,128)S(1)} %get-tuple-element.100.refs_0_.z_ref.refs_5_), channel_id=1, source_target_pairs={{1,2},{3,4},{5,6},{7,8},{9,10},{11,12},{13,14},{15,16},{17,18},{19... | collective-permute-start | bytes 184328 | tf_op jit(solution)/shard_map/ppermute | solution.py:480
  58.7 1.3 collective-permute-start.5
  58.8 1.8 %collective-permute-start.4 = (f32[40,384]{1,0:T(8,128)S(1)}, f32[40,384]{1,0:T(8,128)S(1)}, u32[]{:S(2)}, u32[]{:S(2)}) collective-permute-start(f32[40,384]{1,0:T(8,128)S(1)} %get-tuple-element.110.refs_0_.z_ref.refs_5_), channel_id=1, source_target_pairs={{1,2},{3,4},{5,6},{7,8},{9,10},{11,12},{13,14},{15,16},{17,18},{19... | collective-permute-start | bytes 184328 | tf_op jit(solution)/shard_map/ppermute | solution.py:480
  77.5 1.3 collective-permute-start.7
  77.6 1.8 %collective-permute-start.6 = (f32[40,384]{1,0:T(8,128)S(1)}, f32[40,384]{1,0:T(8,128)S(1)}, u32[]{:S(2)}, u32[]{:S(2)}) collective-permute-start(f32[40,384]{1,0:T(8,128)S(1)} %get-tuple-element.122.refs_0_.z_ref.refs_5_), channel_id=1, source_target_pairs={{1,2},{3,4},{5,6},{7,8},{9,10},{11,12},{13,14},{15,16},{17,18},{19... | collective-permute-start | bytes 184328 | tf_op jit(solution)/shard_map/ppermute | solution.py:480
  96.3 1.3 collective-permute-start.9
  96.3 1.8 %collective-permute-start.8 = (f32[40,384]{1,0:T(8,128)S(1)}, f32[40,384]{1,0:T(8,128)S(1)}, u32[]{:S(2)}, u32[]{:S(2)}) collective-permute-start(f32[40,384]{1,0:T(8,128)S(1)} %get-tuple-element.134.refs_0_.z_ref.refs_5_), channel_id=1, source_target_pairs={{1,2},{3,4},{5,6},{7,8},{9,10},{11,12},{13,14},{15,16},{17,18},{19... | collective-permute-start | bytes 184328 | tf_op jit(solution)/shard_map/ppermute | solution.py:480
  115.1 1.3 collective-permute-start.11
  115.1 1.8 %collective-permute-start.10 = (f32[40,384]{1,0:T(8,128)S(1)}, f32[40,384]{1,0:T(8,128)S(1)}, u32[]{:S(2)}, u32[]{:S(2)}) collective-permute-start(f32[40,384]{1,0:T(8,128)S(1)} %get-tuple-element.146.refs_0_.z_ref.refs_1_), channel_id=1, source_target_pairs={{1,2},{3,4},{5,6},{7,8},{9,10},{11,12},{13,14},{15,16},{17,18},{19... | collective-permute-start | bytes 184328 | tf_op jit(solution)/shard_map/ppermute | solution.py:480

commit v8 on v7

--- a/solution.py
+++ b/solution.py
@@ -13,6 +13,7 @@
 F32 = jnp.float32
 BF16 = jnp.bfloat16
 CHUNK = 256
+SIDE_TILES = 2
 VMEM = pl.BlockSpec(memory_space=pltpu.VMEM)
 ANY = pl.BlockSpec(memory_space=pl.ANY)
 SMEM = pl.BlockSpec(memory_space=pltpu.SMEM)
@@ -169,21 +170,35 @@
     row = iota((ne, 1), 0)
     for bit in (1, 2, 4):
         turned = jnp.where((row & bit) != 0, pltpu.roll(turned, bit * width % CHUNK, 1), turned)
-    total = ne * width
-    acc = [jnp.zeros((8, width), F32)] * (ne // 8)
+    total, main = ne * width, (width // 16 - SIDE_TILES) * 16
+    side_rows = width - main
+    acc = [jnp.zeros((8, main), F32)] * (ne // 8)
+    side = jnp.zeros((side_rows, ne), F32)
+    side_acc = jnp.zeros((side_rows, 128), F32)
+    lane = iota((1, ne), 1)
     for low in range(0, total, CHUNK):
         high = min(low + CHUNK, total)
         first, last = low // width // 8, (high - 1) // width // 8 + 1
         size = (8 * (last - first), high - low)
         entry = iota(size, 1) + low - (iota(size, 0) + 8 * first) * width
-        lhs = jnp.where((entry >= 0) & (entry < width), turned[8 * first : 8 * last, : high - low], 0.0)
+        lhs = jnp.where((entry >= 0) & (entry < width), turned[8 * first : 8 * last, : high - low], 0.0).astype(BF16)
         out = lax.dot_general(
-            lhs.astype(BF16), blocks_ref[:, low:high], (((1,), (1,)), ((), ())), preferred_element_type=F32
+            lhs, blocks_ref[:main, low:high], (((1,), (1,)), ((), ())), preferred_element_type=F32
         )
         for g in range(first, last):
             acc[g] = acc[g] + out[8 * (g - first) : 8 * (g - first + 1)]
+        rows = lhs.astype(F32)
+        for start in range(low, high, 128):
+            tile = blocks_ref[main:, start : start + 128].astype(F32)
+            for e in range(start // width, (start + 127) // width + 1):
+                values = rows[e - 8 * first : e - 8 * first + 1, start - low : start - low + 128]
+                side_acc = side_acc + tile * values
+                if (e + 1) * width <= start + 128:
+                    side = jnp.where(lane == e, jnp.sum(side_acc, axis=1, keepdims=True), side)
+                    side_acc = jnp.zeros((side_rows, 128), F32)
     done = jnp.concatenate(acc, axis=0)
-    done = jnp.concatenate([done, jnp.zeros((ne, CHUNK - width), F32)], axis=1).T
+    done = jnp.concatenate([done, jnp.zeros((ne, CHUNK - main), F32)], axis=1).T
+    done = jnp.concatenate([done[:main], side], axis=0)
     wide = jnp.concatenate([done[v * nb : (v + 1) * nb] for v in range(nv)], axis=1)
     return pad_rows(wide, sz.nbp) * mask
 

time: 133 us -> 132 us (level)
  no operation moved by 1% of the time
where the time goes in v8:
time: 132 us; the launch traced here: 131 us
  blocking collectives  96.1 us (73%)
  Pallas kernels  28.4 us (22%)
  starting transfers between devices  4.41 us (3%)
  waiting for transfers between devices  1.36 us (1%)
    all_to_all x7, blocking collectives, exchange(): return lax.all_to_all(rows, AXES, 0, 0, tiled=True)  96.1 us
    pallas_call x26, Pallas kernels, call(): pl.pallas_call(kernel, name=name, out_shape=out_shape, in_specs=specs or...  28.4 us
    ppermute x6, starting transfers between devices, body(): far = lax.ppermute(search, AXES, off_chip)  3.99 us
  transfers between devices with their start and end apart: 12, of which 6 were waited for; matrix products, arithmetic and copies ran while one was open for 0% of the time, Pallas kernels for 4%

profile of v8, /device:TPU:0, one launch (start us, length us, event | category | flops | bytes accessed | tf_op | source)
XLA Modules:
  0.0 131.1 jit_solution(12318711235982736392)
XLA Ops:
  0.6 3.0 %init.1 = (f32[40,384]{1,0:T(8,128)S(1)}, f32[40,384]{1,0:T(8,128)S(1)}, f32[32,128]{1,0:T(8,128)S(1)}, f32[40,384]{1,0:T(8,128)S(1)}, bf16[3,512,256]{2,1,0:T(8...) custom-call(s32[1]{0:T(128)} %bitcast.me_ref, ...), custom_call_target="tpu_custom_call" | custom-call | tf_op jit(solution)/shard_map/init/pallas_call | solution.py:419
  3.7 14.3 %all_to_all.77 = f32[32,1,128]{2,1,0:T(1,128)S(1)} all-to-all(f32[32,1,128]{2,1,0:T(1,128)S(1)} %bitcast.39), channel_id=1, replica_groups=mesh['dom'=8,'grp'=4] {'dom','grp'}, dimensions={0} | all-to-all | bytes 32768 | tf_op jit(solution)/shard_map/all_to_all | solution.py:470
  18.0 2.2 %precond0.1 = (f32[80,384]{1,0:T(8,128)S(1)}, f32[40,384]{1,0:T(8,128)S(1)}, f32[1,128]{1,0:T(1,128)S(1)}) custom-call(f32[32,128]{1,0:T(8,128)S(1)} %bitcast.33, f32[40,384]{1,0:T(8,128)S(1)} %get-tuple-element.82.vec_ref, f32[40,384]{1,0:T(8,128)S(1)} %get-tuple-element.83.mask_ref.refs_9_.refs_2_, ...), custom_call_target="tpu_custom_call" | custom-call | tf_op jit(solution)/shard_map/precond0/pallas_call | solution.py:419
  20.2 0.1 collective-permute-start.1
  20.2 0.7 collective-permute-start
  20.9 0.3 local.6
  21.3 0.3 collective-permute-done.1.chip_ref
  21.6 0.8 near.1
  22.3 0.0 collective-permute-done.refs_0_
  22.3 1.0 image0.1
  23.3 14.0 %all_to_all.78 = f32[32,1,128]{2,1,0:T(1,128)S(1)} all-to-all(f32[32,1,128]{2,1,0:T(1,128)S(1)} %bitcast.40), channel_id=1, replica_groups=mesh['dom'=8,'grp'=4] {'dom','grp'}, dimensions={0} | all-to-all | bytes 32768 | tf_op jit(solution)/shard_map/all_to_all | solution.py:470
  37.3 2.3 %precond1.1 = (f32[40,384]{1,0:T(8,128)S(1)}, f32[40,384]{1,0:T(8,128)S(1)}, f32[1,128]{1,0:T(1,128)S(1)}) custom-call(f32[32,128]{1,0:T(8,128)S(1)} %bitcast.37, f32[40,384]{1,0:T(8,128)S(1)} %get-tuple-element.99.refs_1_, f32[40,384]{1,0:T(8,128)S(1)} %get-tuple-element.83.mask_ref.refs_9_.refs_2_, ...), custom_call_target="tpu_custom_call" | custom-call | tf_op jit(solution)/shard_map/precond1/pallas_call | solution.py:419
  39.6 0.1 collective-permute-start.3
  39.6 0.7 collective-permute-start.2
  40.3 0.3 local.7
  40.7 0.2 collective-permute-done.3.refs_1_
  40.9 0.6 near1.1
  41.5 0.0 collective-permute-done.2.refs_0_
  41.5 0.8 image1.1
  42.3 13.6 %all_to_all.79 = f32[32,1,128]{2,1,0:T(1,128)S(1)} all-to-all(f32[32,1,128]{2,1,0:T(1,128)S(1)} %bitcast.41), channel_id=1, replica_groups=mesh['dom'=8,'grp'=4] {'dom','grp'}, dimensions={0} | all-to-all | bytes 32768 | tf_op jit(solution)/shard_map/all_to_all | solution.py:470
  55.9 2.3 %precond2.1 = (f32[40,384]{1,0:T(8,128)S(1)}, f32[40,384]{1,0:T(8,128)S(1)}, f32[1,128]{1,0:T(1,128)S(1)}) custom-call(f32[32,128]{1,0:T(8,128)S(1)} %bitcast.34, f32[40,384]{1,0:T(8,128)S(1)} %get-tuple-element.109.refs_1_, f32[40,384]{1,0:T(8,128)S(1)} %get-tuple-element.83.mask_ref.refs_9_.refs_2_, ...), custom_call_target="tpu_custom_call" | custom-call | tf_op jit(solution)/shard_map/precond2/pallas_call | solution.py:419
  58.2 0.1 collective-permute-start.5
  58.2 0.7 collective-permute-start.4
  58.9 0.3 local.8
  59.3 0.2 collective-permute-done.5.refs_1_
  59.5 0.6 near2.1
  60.1 0.0 collective-permute-done.4.refs_0_
  60.1 0.8 image2.1
  60.9 13.6 %all_to_all.80 = f32[32,1,128]{2,1,0:T(1,128)S(1)} all-to-all(f32[32,1,128]{2,1,0:T(1,128)S(1)} %bitcast.42), channel_id=1, replica_groups=mesh['dom'=8,'grp'=4] {'dom','grp'}, dimensions={0} | all-to-all | bytes 32768 | tf_op jit(solution)/shard_map/all_to_all | solution.py:470
  74.5 2.3 %precond3.1 = (f32[40,384]{1,0:T(8,128)S(1)}, f32[40,384]{1,0:T(8,128)S(1)}, f32[1,128]{1,0:T(1,128)S(1)}) custom-call(f32[32,128]{1,0:T(8,128)S(1)} %bitcast.35, f32[40,384]{1,0:T(8,128)S(1)} %get-tuple-element.121.refs_1_, f32[40,384]{1,0:T(8,128)S(1)} %get-tuple-element.83.mask_ref.refs_9_.refs_2_, ...), custom_call_target="tpu_custom_call" | custom-call | tf_op jit(solution)/shard_map/precond3/pallas_call | solution.py:419
  76.8 0.1 collective-permute-start.7
  76.8 0.7 collective-permute-start.6
  77.5 0.3 local.9
  77.9 0.2 collective-permute-done.7.refs_1_
  78.1 0.6 near3.1
  78.7 0.0 collective-permute-done.6.refs_0_
  78.7 0.8 image3.1
  79.5 13.6 %all_to_all.81 = f32[32,1,128]{2,1,0:T(1,128)S(1)} all-to-all(f32[32,1,128]{2,1,0:T(1,128)S(1)} %bitcast.43), channel_id=1, replica_groups=mesh['dom'=8,'grp'=4] {'dom','grp'}, dimensions={0} | all-to-all | bytes 32768 | tf_op jit(solution)/shard_map/all_to_all | solution.py:470
  93.1 2.3 %precond4.1 = (f32[40,384]{1,0:T(8,128)S(1)}, f32[40,384]{1,0:T(8,128)S(1)}, f32[1,128]{1,0:T(1,128)S(1)}) custom-call(f32[32,128]{1,0:T(8,128)S(1)} %bitcast.36, f32[40,384]{1,0:T(8,128)S(1)} %get-tuple-element.133.refs_1_, f32[40,384]{1,0:T(8,128)S(1)} %get-tuple-element.83.mask_ref.refs_9_.refs_2_, ...), custom_call_target="tpu_custom_call" | custom-call | tf_op jit(solution)/shard_map/precond4/pallas_call | solution.py:419
  95.4 0.1 collective-permute-start.9
  95.4 0.7 collective-permute-start.8
  96.1 0.3 local.10
  96.5 0.2 collective-permute-done.9.refs_1_
  96.7 0.6 near4.1
  97.2 0.0 collective-permute-done.8.refs_0_
  97.3 0.9 image4.1
  98.1 13.6 %all_to_all.82 = f32[32,1,128]{2,1,0:T(1,128)S(1)} all-to-all(f32[32,1,128]{2,1,0:T(1,128)S(1)} %bitcast.44), channel_id=1, replica_groups=mesh['dom'=8,'grp'=4] {'dom','grp'}, dimensions={0} | all-to-all | bytes 32768 | tf_op jit(solution)/shard_map/all_to_all | solution.py:470
  111.7 2.3 %precond5.1 = (f32[40,384]{1,0:T(8,128)S(1)}, f32[40,384]{1,0:T(8,128)S(1)}, f32[1,128]{1,0:T(1,128)S(1)}) custom-call(f32[32,128]{1,0:T(8,128)S(1)} %bitcast.32, f32[40,384]{1,0:T(8,128)S(1)} %get-tuple-element.145.refs_1_, f32[40,384]{1,0:T(8,128)S(1)} %get-tuple-element.83.mask_ref.refs_9_.refs_2_, ...), custom_call_target="tpu_custom_call" | custom-call | tf_op jit(solution)/shard_map/precond5/pallas_call | solution.py:419
  113.9 0.1 collective-permute-start.11
  114.0 0.7 collective-permute-start.10
  114.7 0.3 local.11
  115.1 0.2 collective-permute-done.11.refs_1_
  115.3 0.6 near5.1
  115.8 0.0 collective-permute-done.10.refs_0_
  115.9 0.9 image5.1
  116.7 13.6 %all_to_all.83 = f32[32,1,128]{2,1,0:T(1,128)S(1)} all-to-all(f32[32,1,128]{2,1,0:T(1,128)S(1)} %bitcast.31), channel_id=1, replica_groups=mesh['dom'=8,'grp'=4] {'dom','grp'}, dimensions={0} | all-to-all | bytes 32768 | tf_op jit(solution)/shard_map/all_to_all | solution.py:470
  130.3 0.9 finish.1
Async XLA Ops:
  20.2 1.4 %collective-permute-start.1 = (f32[80,384]{1,0:T(8,128)S(1)}, f32[80,384]{1,0:T(8,128)S(1)}, u32[]{:S(2)}, u32[]{:S(2)}) collective-permute-start(f32[80,384]{1,0:T(8,128)S(1)} %get-tuple-element.86.z_ref.refs_11_.refs_5_), channel_id=1, source_target_pairs={{0,1},{1,0},{2,3},{3,2},{4,5},{5,4},{6,7},{7,6},{8,9},{9,8},{10,11... | collective-permute-start | bytes 368648 | tf_op jit(solution)/shard_map/ppermute | solution.py:496
  20.2 2.1 %collective-permute-start = (f32[80,384]{1,0:T(8,128)S(1)}, f32[80,384]{1,0:T(8,128)S(1)}, u32[]{:S(2)}, u32[]{:S(2)}) collective-permute-start(f32[80,384]{1,0:T(8,128)S(1)} %get-tuple-element.86.z_ref.refs_11_.refs_5_), channel_id=1, source_target_pairs={{1,2},{3,4},{5,6},{7,8},{9,10},{11,12},{13,14},{15,16},{17,18},{19... | collective-permute-start | bytes 368648 | tf_op jit(solution)/shard_map/ppermute | solution.py:495
  39.6 1.3 %collective-permute-start.3 = (f32[40,384]{1,0:T(8,128)S(1)}, f32[40,384]{1,0:T(8,128)S(1)}, u32[]{:S(2)}, u32[]{:S(2)}) collective-permute-start(f32[40,384]{1,0:T(8,128)S(1)} %get-tuple-element.100.refs_0_.z_ref.refs_5_), channel_id=1, source_target_pairs={{0,1},{1,0},{2,3},{3,2},{4,5},{5,4},{6,7},{7,6},{8,9},{9,8},{10,11... | collective-permute-start | bytes 184328 | tf_op jit(solution)/shard_map/ppermute | solution.py:496
  39.6 1.8 %collective-permute-start.2 = (f32[40,384]{1,0:T(8,128)S(1)}, f32[40,384]{1,0:T(8,128)S(1)}, u32[]{:S(2)}, u32[]{:S(2)}) collective-permute-start(f32[40,384]{1,0:T(8,128)S(1)} %get-tuple-element.100.refs_0_.z_ref.refs_5_), channel_id=1, source_target_pairs={{1,2},{3,4},{5,6},{7,8},{9,10},{11,12},{13,14},{15,16},{17,18},{19... | collective-permute-start | bytes 184328 | tf_op jit(solution)/shard_map/ppermute | solution.py:495
  58.2 1.3 %collective-permute-start.5 = (f32[40,384]{1,0:T(8,128)S(1)}, f32[40,384]{1,0:T(8,128)S(1)}, u32[]{:S(2)}, u32[]{:S(2)}) collective-permute-start(f32[40,384]{1,0:T(8,128)S(1)} %get-tuple-element.110.refs_0_.z_ref.refs_5_), channel_id=1, source_target_pairs={{0,1},{1,0},{2,3},{3,2},{4,5},{5,4},{6,7},{7,6},{8,9},{9,8},{10,11... | collective-permute-start | bytes 184328 | tf_op jit(solution)/shard_map/ppermute | solution.py:496
  58.2 1.8 %collective-permute-start.4 = (f32[40,384]{1,0:T(8,128)S(1)}, f32[40,384]{1,0:T(8,128)S(1)}, u32[]{:S(2)}, u32[]{:S(2)}) collective-permute-start(f32[40,384]{1,0:T(8,128)S(1)} %get-tuple-element.110.refs_0_.z_ref.refs_5_), channel_id=1, source_target_pairs={{1,2},{3,4},{5,6},{7,8},{9,10},{11,12},{13,14},{15,16},{17,18},{19... | collective-permute-start | bytes 184328 | tf_op jit(solution)/shard_map/ppermute | solution.py:495
  76.8 1.3 %collective-permute-start.7 = (f32[40,384]{1,0:T(8,128)S(1)}, f32[40,384]{1,0:T(8,128)S(1)}, u32[]{:S(2)}, u32[]{:S(2)}) collective-permute-start(f32[40,384]{1,0:T(8,128)S(1)} %get-tuple-element.122.refs_0_.z_ref.refs_5_), channel_id=1, source_target_pairs={{0,1},{1,0},{2,3},{3,2},{4,5},{5,4},{6,7},{7,6},{8,9},{9,8},{10,11... | collective-permute-start | bytes 184328 | tf_op jit(solution)/shard_map/ppermute | solution.py:496
  76.8 1.8 %collective-permute-start.6 = (f32[40,384]{1,0:T(8,128)S(1)}, f32[40,384]{1,0:T(8,128)S(1)}, u32[]{:S(2)}, u32[]{:S(2)}) collective-permute-start(f32[40,384]{1,0:T(8,128)S(1)} %get-tuple-element.122.refs_0_.z_ref.refs_5_), channel_id=1, source_target_pairs={{1,2},{3,4},{5,6},{7,8},{9,10},{11,12},{13,14},{15,16},{17,18},{19... | collective-permute-start | bytes 184328 | tf_op jit(solution)/shard_map/ppermute | solution.py:495
  95.4 1.3 %collective-permute-start.9 = (f32[40,384]{1,0:T(8,128)S(1)}, f32[40,384]{1,0:T(8,128)S(1)}, u32[]{:S(2)}, u32[]{:S(2)}) collective-permute-start(f32[40,384]{1,0:T(8,128)S(1)} %get-tuple-element.134.refs_0_.z_ref.refs_5_), channel_id=1, source_target_pairs={{0,1},{1,0},{2,3},{3,2},{4,5},{5,4},{6,7},{7,6},{8,9},{9,8},{10,11... | collective-permute-start | bytes 184328 | tf_op jit(solution)/shard_map/ppermute | solution.py:496
  95.4 1.8 %collective-permute-start.8 = (f32[40,384]{1,0:T(8,128)S(1)}, f32[40,384]{1,0:T(8,128)S(1)}, u32[]{:S(2)}, u32[]{:S(2)}) collective-permute-start(f32[40,384]{1,0:T(8,128)S(1)} %get-tuple-element.134.refs_0_.z_ref.refs_5_), channel_id=1, source_target_pairs={{1,2},{3,4},{5,6},{7,8},{9,10},{11,12},{13,14},{15,16},{17,18},{19... | collective-permute-start | bytes 184328 | tf_op jit(solution)/shard_map/ppermute | solution.py:495
  113.9 1.3 %collective-permute-start.11 = (f32[40,384]{1,0:T(8,128)S(1)}, f32[40,384]{1,0:T(8,128)S(1)}, u32[]{:S(2)}, u32[]{:S(2)}) collective-permute-start(f32[40,384]{1,0:T(8,128)S(1)} %get-tuple-element.146.refs_0_.z_ref.refs_1_), channel_id=1, source_target_pairs={{0,1},{1,0},{2,3},{3,2},{4,5},{5,4},{6,7},{7,6},{8,9},{9,8},{10,11... | collective-permute-start | bytes 184328 | tf_op jit(solution)/shard_map/ppermute | solution.py:496
  114.0 1.8 %collective-permute-start.10 = (f32[40,384]{1,0:T(8,128)S(1)}, f32[40,384]{1,0:T(8,128)S(1)}, u32[]{:S(2)}, u32[]{:S(2)}) collective-permute-start(f32[40,384]{1,0:T(8,128)S(1)} %get-tuple-element.146.refs_0_.z_ref.refs_1_), channel_id=1, source_target_pairs={{1,2},{3,4},{5,6},{7,8},{9,10},{11,12},{13,14},{15,16},{17,18},{19... | collective-permute-start | bytes 184328 | tf_op jit(solution)/shard_map/ppermute | solution.py:495

commit v9 on v8

--- a/solution.py
+++ b/solution.py
@@ -13,7 +13,7 @@
 F32 = jnp.float32
 BF16 = jnp.bfloat16
 CHUNK = 256
-SIDE_TILES = 2
+SIDE_TILES = 3
 VMEM = pl.BlockSpec(memory_space=pltpu.VMEM)
 ANY = pl.BlockSpec(memory_space=pl.ANY)
 SMEM = pl.BlockSpec(memory_space=pltpu.SMEM)
@@ -170,6 +170,7 @@
     row = iota((ne, 1), 0)
     for bit in (1, 2, 4):
         turned = jnp.where((row & bit) != 0, pltpu.roll(turned, bit * width % CHUNK, 1), turned)
+    turned = turned.astype(BF16).astype(F32)
     total, main = ne * width, (width // 16 - SIDE_TILES) * 16
     side_rows = width - main
     acc = [jnp.zeros((8, main), F32)] * (ne // 8)
@@ -181,17 +182,16 @@
         first, last = low // width // 8, (high - 1) // width // 8 + 1
         size = (8 * (last - first), high - low)
         entry = iota(size, 1) + low - (iota(size, 0) + 8 * first) * width
-        lhs = jnp.where((entry >= 0) & (entry < width), turned[8 * first : 8 * last, : high - low], 0.0).astype(BF16)
+        lhs = jnp.where((entry >= 0) & (entry < width), turned[8 * first : 8 * last, : high - low], 0.0)
         out = lax.dot_general(
-            lhs, blocks_ref[:main, low:high], (((1,), (1,)), ((), ())), preferred_element_type=F32
+            lhs.astype(BF16), blocks_ref[:main, low:high], (((1,), (1,)), ((), ())), preferred_element_type=F32
         )
         for g in range(first, last):
             acc[g] = acc[g] + out[8 * (g - first) : 8 * (g - first + 1)]
-        rows = lhs.astype(F32)
         for start in range(low, high, 128):
             tile = blocks_ref[main:, start : start + 128].astype(F32)
             for e in range(start // width, (start + 127) // width + 1):
-                values = rows[e - 8 * first : e - 8 * first + 1, start - low : start - low + 128]
+                values = lhs[e - 8 * first : e - 8 * first + 1, start - low : start - low + 128]
                 side_acc = side_acc + tile * values
                 if (e + 1) * width <= start + 128:
                     side = jnp.where(lane == e, jnp.sum(side_acc, axis=1, keepdims=True), side)

time: 132 us -> 131 us (level)
  no operation moved by 1% of the time
where the time goes in v9:
time: 131 us
  blocking collectives  96.1 us (73%)
  Pallas kernels  27.9 us (21%)
  starting transfers between devices  4.41 us (3%)
  waiting for transfers between devices  1.36 us (1%)
    all_to_all x7, blocking collectives, exchange(): return lax.all_to_all(rows, AXES, 0, 0, tiled=True)  96.1 us
    pallas_call x26, Pallas kernels, call(): pl.pallas_call(kernel, name=name, out_shape=out_shape, in_specs=specs or...  27.9 us
    ppermute x6, starting transfers between devices, body(): far = lax.ppermute(search, AXES, off_chip)  3.99 us
  transfers between devices with their start and end apart: 12, of which 6 were waited for; matrix products, arithmetic and copies ran while one was open for 0% of the time, Pallas kernels for 4%

profile of v9, /device:TPU:0, one launch (start us, length us, event | category | flops | bytes accessed | tf_op | source)
XLA Modules:
  0.0 130.7 jit_solution(12280385755350772560)
XLA Ops:
  0.6 3.0 %init.1 = (f32[40,384]{1,0:T(8,128)S(1)}, f32[40,384]{1,0:T(8,128)S(1)}, f32[32,128]{1,0:T(8,128)S(1)}, f32[40,384]{1,0:T(8,128)S(1)}, bf16[3,512,256]{2,1,0:T(8...) custom-call(s32[1]{0:T(128)} %bitcast.me_ref, ...), custom_call_target="tpu_custom_call" | custom-call | tf_op jit(solution)/shard_map/init/pallas_call | solution.py:419
  3.7 14.3 %all_to_all.77 = f32[32,1,128]{2,1,0:T(1,128)S(1)} all-to-all(f32[32,1,128]{2,1,0:T(1,128)S(1)} %bitcast.39), channel_id=1, replica_groups=mesh['dom'=8,'grp'=4] {'dom','grp'}, dimensions={0} | all-to-all | bytes 32768 | tf_op jit(solution)/shard_map/all_to_all | solution.py:470
  18.0 2.1 %precond0.1 = (f32[80,384]{1,0:T(8,128)S(1)}, f32[40,384]{1,0:T(8,128)S(1)}, f32[1,128]{1,0:T(1,128)S(1)}) custom-call(f32[32,128]{1,0:T(8,128)S(1)} %bitcast.33, f32[40,384]{1,0:T(8,128)S(1)} %get-tuple-element.82.vec_ref, f32[40,384]{1,0:T(8,128)S(1)} %get-tuple-element.83.mask_ref.refs_9_.refs_2_, ...), custom_call_target="tpu_custom_call" | custom-call | tf_op jit(solution)/shard_map/precond0/pallas_call | solution.py:419
  20.1 0.1 collective-permute-start.1
  20.2 0.7 collective-permute-start
  20.8 0.3 local.6
  21.2 0.3 collective-permute-done.1.chip_ref
  21.5 0.8 near.1
  22.2 0.0 collective-permute-done.refs_0_
  22.3 1.0 image0.1
  23.3 14.0 %all_to_all.78 = f32[32,1,128]{2,1,0:T(1,128)S(1)} all-to-all(f32[32,1,128]{2,1,0:T(1,128)S(1)} %bitcast.40), channel_id=1, replica_groups=mesh['dom'=8,'grp'=4] {'dom','grp'}, dimensions={0} | all-to-all | bytes 32768 | tf_op jit(solution)/shard_map/all_to_all | solution.py:470
  37.2 2.2 %precond1.1 = (f32[40,384]{1,0:T(8,128)S(1)}, f32[40,384]{1,0:T(8,128)S(1)}, f32[1,128]{1,0:T(1,128)S(1)}) custom-call(f32[32,128]{1,0:T(8,128)S(1)} %bitcast.37, f32[40,384]{1,0:T(8,128)S(1)} %get-tuple-element.99.refs_1_, f32[40,384]{1,0:T(8,128)S(1)} %get-tuple-element.83.mask_ref.refs_9_.refs_2_, ...), custom_call_target="tpu_custom_call" | custom-call | tf_op jit(solution)/shard_map/precond1/pallas_call | solution.py:419
  39.4 0.1 collective-permute-start.3
  39.5 0.7 collective-permute-start.2
  40.2 0.3 local.7
  40.5 0.2 collective-permute-done.3.refs_1_
  40.7 0.6 near1.1
  41.3 0.0 collective-permute-done.2.refs_0_
  41.3 0.8 image1.1
  42.2 13.6 %all_to_all.79 = f32[32,1,128]{2,1,0:T(1,128)S(1)} all-to-all(f32[32,1,128]{2,1,0:T(1,128)S(1)} %bitcast.41), channel_id=1, replica_groups=mesh['dom'=8,'grp'=4] {'dom','grp'}, dimensions={0} | all-to-all | bytes 32768 | tf_op jit(solution)/shard_map/all_to_all | solution.py:470
  55.7 2.2 %precond2.1 = (f32[40,384]{1,0:T(8,128)S(1)}, f32[40,384]{1,0:T(8,128)S(1)}, f32[1,128]{1,0:T(1,128)S(1)}) custom-call(f32[32,128]{1,0:T(8,128)S(1)} %bitcast.34, f32[40,384]{1,0:T(8,128)S(1)} %get-tuple-element.109.refs_1_, f32[40,384]{1,0:T(8,128)S(1)} %get-tuple-element.83.mask_ref.refs_9_.refs_2_, ...), custom_call_target="tpu_custom_call" | custom-call | tf_op jit(solution)/shard_map/precond2/pallas_call | solution.py:419
  57.9 0.1 collective-permute-start.5
  58.0 0.7 collective-permute-start.4
  58.7 0.3 local.8
  59.0 0.2 collective-permute-done.5.refs_1_
  59.2 0.6 near2.1
  59.8 0.0 collective-permute-done.4.refs_0_
  59.8 0.8 image2.1
  60.7 13.6 %all_to_all.80 = f32[32,1,128]{2,1,0:T(1,128)S(1)} all-to-all(f32[32,1,128]{2,1,0:T(1,128)S(1)} %bitcast.42), channel_id=1, replica_groups=mesh['dom'=8,'grp'=4] {'dom','grp'}, dimensions={0} | all-to-all | bytes 32768 | tf_op jit(solution)/shard_map/all_to_all | solution.py:470
  74.3 2.2 %precond3.1 = (f32[40,384]{1,0:T(8,128)S(1)}, f32[40,384]{1,0:T(8,128)S(1)}, f32[1,128]{1,0:T(1,128)S(1)}) custom-call(f32[32,128]{1,0:T(8,128)S(1)} %bitcast.35, f32[40,384]{1,0:T(8,128)S(1)} %get-tuple-element.121.refs_1_, f32[40,384]{1,0:T(8,128)S(1)} %get-tuple-element.83.mask_ref.refs_9_.refs_2_, ...), custom_call_target="tpu_custom_call" | custom-call | tf_op jit(solution)/shard_map/precond3/pallas_call | solution.py:419
  76.4 0.1 collective-permute-start.7
  76.5 0.7 collective-permute-start.6
  77.2 0.3 local.9
  77.5 0.2 collective-permute-done.7.refs_1_
  77.8 0.6 near3.1
  78.3 0.0 collective-permute-done.6.refs_0_
  78.3 0.8 image3.1
  79.2 13.6 %all_to_all.81 = f32[32,1,128]{2,1,0:T(1,128)S(1)} all-to-all(f32[32,1,128]{2,1,0:T(1,128)S(1)} %bitcast.43), channel_id=1, replica_groups=mesh['dom'=8,'grp'=4] {'dom','grp'}, dimensions={0} | all-to-all | bytes 32768 | tf_op jit(solution)/shard_map/all_to_all | solution.py:470
  92.8 2.2 %precond4.1 = (f32[40,384]{1,0:T(8,128)S(1)}, f32[40,384]{1,0:T(8,128)S(1)}, f32[1,128]{1,0:T(1,128)S(1)}) custom-call(f32[32,128]{1,0:T(8,128)S(1)} %bitcast.36, f32[40,384]{1,0:T(8,128)S(1)} %get-tuple-element.133.refs_1_, f32[40,384]{1,0:T(8,128)S(1)} %get-tuple-element.83.mask_ref.refs_9_.refs_2_, ...), custom_call_target="tpu_custom_call" | custom-call | tf_op jit(solution)/shard_map/precond4/pallas_call | solution.py:419
  95.0 0.1 collective-permute-start.9
  95.0 0.7 collective-permute-start.8
  95.7 0.3 local.10
  96.1 0.2 collective-permute-done.9.refs_1_
  96.3 0.6 near4.1
  96.9 0.0 collective-permute-done.8.refs_0_
  96.9 0.9 image4.1
  97.7 13.6 %all_to_all.82 = f32[32,1,128]{2,1,0:T(1,128)S(1)} all-to-all(f32[32,1,128]{2,1,0:T(1,128)S(1)} %bitcast.44), channel_id=1, replica_groups=mesh['dom'=8,'grp'=4] {'dom','grp'}, dimensions={0} | all-to-all | bytes 32768 | tf_op jit(solution)/shard_map/all_to_all | solution.py:470
  111.3 2.2 %precond5.1 = (f32[40,384]{1,0:T(8,128)S(1)}, f32[40,384]{1,0:T(8,128)S(1)}, f32[1,128]{1,0:T(1,128)S(1)}) custom-call(f32[32,128]{1,0:T(8,128)S(1)} %bitcast.32, f32[40,384]{1,0:T(8,128)S(1)} %get-tuple-element.145.refs_1_, f32[40,384]{1,0:T(8,128)S(1)} %get-tuple-element.83.mask_ref.refs_9_.refs_2_, ...), custom_call_target="tpu_custom_call" | custom-call | tf_op jit(solution)/shard_map/precond5/pallas_call | solution.py:419
  113.5 0.1 collective-permute-start.11
  113.5 0.7 collective-permute-start.10
  114.2 0.3 local.11
  114.6 0.2 collective-permute-done.11.refs_1_
  114.8 0.6 near5.1
  115.4 0.0 collective-permute-done.10.refs_0_
  115.4 0.9 image5.1
  116.2 13.6 %all_to_all.83 = f32[32,1,128]{2,1,0:T(1,128)S(1)} all-to-all(f32[32,1,128]{2,1,0:T(1,128)S(1)} %bitcast.31), channel_id=1, replica_groups=mesh['dom'=8,'grp'=4] {'dom','grp'}, dimensions={0} | all-to-all | bytes 32768 | tf_op jit(solution)/shard_map/all_to_all | solution.py:470
  129.8 0.9 finish.1
Async XLA Ops:
  20.1 1.4 %collective-permute-start.1 = (f32[80,384]{1,0:T(8,128)S(1)}, f32[80,384]{1,0:T(8,128)S(1)}, u32[]{:S(2)}, u32[]{:S(2)}) collective-permute-start(f32[80,384]{1,0:T(8,128)S(1)} %get-tuple-element.86.z_ref.refs_11_.refs_5_), channel_id=1, source_target_pairs={{0,1},{1,0},{2,3},{3,2},{4,5},{5,4},{6,7},{7,6},{8,9},{9,8},{10,11... | collective-permute-start | bytes 368648 | tf_op jit(solution)/shard_map/ppermute | solution.py:496
  20.2 2.1 %collective-permute-start = (f32[80,384]{1,0:T(8,128)S(1)}, f32[80,384]{1,0:T(8,128)S(1)}, u32[]{:S(2)}, u32[]{:S(2)}) collective-permute-start(f32[80,384]{1,0:T(8,128)S(1)} %get-tuple-element.86.z_ref.refs_11_.refs_5_), channel_id=1, source_target_pairs={{1,2},{3,4},{5,6},{7,8},{9,10},{11,12},{13,14},{15,16},{17,18},{19... | collective-permute-start | bytes 368648 | tf_op jit(solution)/shard_map/ppermute | solution.py:495
  39.4 1.3 %collective-permute-start.3 = (f32[40,384]{1,0:T(8,128)S(1)}, f32[40,384]{1,0:T(8,128)S(1)}, u32[]{:S(2)}, u32[]{:S(2)}) collective-permute-start(f32[40,384]{1,0:T(8,128)S(1)} %get-tuple-element.100.refs_0_.z_ref.refs_5_), channel_id=1, source_target_pairs={{0,1},{1,0},{2,3},{3,2},{4,5},{5,4},{6,7},{7,6},{8,9},{9,8},{10,11... | collective-permute-start | bytes 184328 | tf_op jit(solution)/shard_map/ppermute | solution.py:496
  39.5 1.8 %collective-permute-start.2 = (f32[40,384]{1,0:T(8,128)S(1)}, f32[40,384]{1,0:T(8,128)S(1)}, u32[]{:S(2)}, u32[]{:S(2)}) collective-permute-start(f32[40,384]{1,0:T(8,128)S(1)} %get-tuple-element.100.refs_0_.z_ref.refs_5_), channel_id=1, source_target_pairs={{1,2},{3,4},{5,6},{7,8},{9,10},{11,12},{13,14},{15,16},{17,18},{19... | collective-permute-start | bytes 184328 | tf_op jit(solution)/shard_map/ppermute | solution.py:495
  57.9 1.3 %collective-permute-start.5 = (f32[40,384]{1,0:T(8,128)S(1)}, f32[40,384]{1,0:T(8,128)S(1)}, u32[]{:S(2)}, u32[]{:S(2)}) collective-permute-start(f32[40,384]{1,0:T(8,128)S(1)} %get-tuple-element.110.refs_0_.z_ref.refs_5_), channel_id=1, source_target_pairs={{0,1},{1,0},{2,3},{3,2},{4,5},{5,4},{6,7},{7,6},{8,9},{9,8},{10,11... | collective-permute-start | bytes 184328 | tf_op jit(solution)/shard_map/ppermute | solution.py:496
  58.0 1.8 %collective-permute-start.4 = (f32[40,384]{1,0:T(8,128)S(1)}, f32[40,384]{1,0:T(8,128)S(1)}, u32[]{:S(2)}, u32[]{:S(2)}) collective-permute-start(f32[40,384]{1,0:T(8,128)S(1)} %get-tuple-element.110.refs_0_.z_ref.refs_5_), channel_id=1, source_target_pairs={{1,2},{3,4},{5,6},{7,8},{9,10},{11,12},{13,14},{15,16},{17,18},{19... | collective-permute-start | bytes 184328 | tf_op jit(solution)/shard_map/ppermute | solution.py:495
  76.4 1.3 %collective-permute-start.7 = (f32[40,384]{1,0:T(8,128)S(1)}, f32[40,384]{1,0:T(8,128)S(1)}, u32[]{:S(2)}, u32[]{:S(2)}) collective-permute-start(f32[40,384]{1,0:T(8,128)S(1)} %get-tuple-element.122.refs_0_.z_ref.refs_5_), channel_id=1, source_target_pairs={{0,1},{1,0},{2,3},{3,2},{4,5},{5,4},{6,7},{7,6},{8,9},{9,8},{10,11... | collective-permute-start | bytes 184328 | tf_op jit(solution)/shard_map/ppermute | solution.py:496
  76.5 1.8 %collective-permute-start.6 = (f32[40,384]{1,0:T(8,128)S(1)}, f32[40,384]{1,0:T(8,128)S(1)}, u32[]{:S(2)}, u32[]{:S(2)}) collective-permute-start(f32[40,384]{1,0:T(8,128)S(1)} %get-tuple-element.122.refs_0_.z_ref.refs_5_), channel_id=1, source_target_pairs={{1,2},{3,4},{5,6},{7,8},{9,10},{11,12},{13,14},{15,16},{17,18},{19... | collective-permute-start | bytes 184328 | tf_op jit(solution)/shard_map/ppermute | solution.py:495
  95.0 1.3 %collective-permute-start.9 = (f32[40,384]{1,0:T(8,128)S(1)}, f32[40,384]{1,0:T(8,128)S(1)}, u32[]{:S(2)}, u32[]{:S(2)}) collective-permute-start(f32[40,384]{1,0:T(8,128)S(1)} %get-tuple-element.134.refs_0_.z_ref.refs_5_), channel_id=1, source_target_pairs={{0,1},{1,0},{2,3},{3,2},{4,5},{5,4},{6,7},{7,6},{8,9},{9,8},{10,11... | collective-permute-start | bytes 184328 | tf_op jit(solution)/shard_map/ppermute | solution.py:496
  95.0 1.8 %collective-permute-start.8 = (f32[40,384]{1,0:T(8,128)S(1)}, f32[40,384]{1,0:T(8,128)S(1)}, u32[]{:S(2)}, u32[]{:S(2)}) collective-permute-start(f32[40,384]{1,0:T(8,128)S(1)} %get-tuple-element.134.refs_0_.z_ref.refs_5_), channel_id=1, source_target_pairs={{1,2},{3,4},{5,6},{7,8},{9,10},{11,12},{13,14},{15,16},{17,18},{19... | collective-permute-start | bytes 184328 | tf_op jit(solution)/shard_map/ppermute | solution.py:495
  113.5 1.3 %collective-permute-start.11 = (f32[40,384]{1,0:T(8,128)S(1)}, f32[40,384]{1,0:T(8,128)S(1)}, u32[]{:S(2)}, u32[]{:S(2)}) collective-permute-start(f32[40,384]{1,0:T(8,128)S(1)} %get-tuple-element.146.refs_0_.z_ref.refs_1_), channel_id=1, source_target_pairs={{0,1},{1,0},{2,3},{3,2},{4,5},{5,4},{6,7},{7,6},{8,9},{9,8},{10,11... | collective-permute-start | bytes 184328 | tf_op jit(solution)/shard_map/ppermute | solution.py:496
  113.5 1.8 %collective-permute-start.10 = (f32[40,384]{1,0:T(8,128)S(1)}, f32[40,384]{1,0:T(8,128)S(1)}, u32[]{:S(2)}, u32[]{:S(2)}) collective-permute-start(f32[40,384]{1,0:T(8,128)S(1)} %get-tuple-element.146.refs_0_.z_ref.refs_1_), channel_id=1, source_target_pairs={{1,2},{3,4},{5,6},{7,8},{9,10},{11,12},{13,14},{15,16},{17,18},{19... | collective-permute-start | bytes 184328 | tf_op jit(solution)/shard_map/ppermute | solution.py:495

commit v10 on v9

--- a/solution.py
+++ b/solution.py
@@ -222,7 +222,7 @@
     for h, b in zip(proj, basis):
         vec = vec - h * b[...]
         square = square - h * h
-    norm = jnp.sqrt(square + EPSILON)
+    norm = jnp.sqrt(jnp.maximum(square, 0.0) + EPSILON)
     new = vec * (1.0 / norm)
     v_ref[...] = new
     h_ref[...] = partial_rows(proj + [norm], 1)
@@ -298,7 +298,7 @@
         rest = entries[step + 1]
         for h in entries[:-1]:
             rest = rest - h * h
-        entries[step + 1] = jnp.sqrt(rest + EPSILON)
+        entries[step + 1] = jnp.sqrt(jnp.maximum(rest, 0.0) + EPSILON)
     column = list(entries)
     for i in range(step):
         cosine, sine = turns_ref[2 * i : 2 * i + 1, :], turns_ref[2 * i + 1 : 2 * i + 2, :]

time: 131 us -> 131 us (level)
  no operation moved by 1% of the time
where the time goes in v10:
time: 131 us
  blocking collectives  96.1 us (73%)
  Pallas kernels  27.9 us (21%)
  starting transfers between devices  4.41 us (3%)
  waiting for transfers between devices  1.36 us (1%)
    all_to_all x7, blocking collectives, exchange(): return lax.all_to_all(rows, AXES, 0, 0, tiled=True)  96.1 us
    pallas_call x26, Pallas kernels, call(): pl.pallas_call(kernel, name=name, out_shape=out_shape, in_specs=specs or...  27.9 us
    ppermute x6, starting transfers between devices, body(): far = lax.ppermute(search, AXES, off_chip)  3.99 us
  transfers between devices with their start and end apart: 12, of which 6 were waited for; matrix products, arithmetic and copies ran while one was open for 0% of the time, Pallas kernels for 4%

profile of v10, /device:TPU:0, one launch (start us, length us, event | category | flops | bytes accessed | tf_op | source)
XLA Modules:
  0.0 130.7 jit_solution(513209756832906785)
XLA Ops:
  0.6 3.0 %init.1 = (f32[40,384]{1,0:T(8,128)S(1)}, f32[40,384]{1,0:T(8,128)S(1)}, f32[32,128]{1,0:T(8,128)S(1)}, f32[40,384]{1,0:T(8,128)S(1)}, bf16[3,512,256]{2,1,0:T(8...) custom-call(s32[1]{0:T(128)} %bitcast.me_ref, ...), custom_call_target="tpu_custom_call" | custom-call | tf_op jit(solution)/shard_map/init/pallas_call | solution.py:419
  3.7 14.3 %all_to_all.77 = f32[32,1,128]{2,1,0:T(1,128)S(1)} all-to-all(f32[32,1,128]{2,1,0:T(1,128)S(1)} %bitcast.39), channel_id=1, replica_groups=mesh['dom'=8,'grp'=4] {'dom','grp'}, dimensions={0} | all-to-all | bytes 32768 | tf_op jit(solution)/shard_map/all_to_all | solution.py:470
  18.0 2.1 %precond0.1 = (f32[80,384]{1,0:T(8,128)S(1)}, f32[40,384]{1,0:T(8,128)S(1)}, f32[1,128]{1,0:T(1,128)S(1)}) custom-call(f32[32,128]{1,0:T(8,128)S(1)} %bitcast.33, f32[40,384]{1,0:T(8,128)S(1)} %get-tuple-element.82.vec_ref, f32[40,384]{1,0:T(8,128)S(1)} %get-tuple-element.83.mask_ref.refs_9_.refs_2_, ...), custom_call_target="tpu_custom_call" | custom-call | tf_op jit(solution)/shard_map/precond0/pallas_call | solution.py:419
  20.1 0.1 collective-permute-start.1
  20.2 0.7 collective-permute-start
  20.8 0.3 local.6
  21.2 0.3 collective-permute-done.1.chip_ref
  21.5 0.8 near.1
  22.2 0.0 collective-permute-done.refs_0_
  22.3 1.0 image0.1
  23.3 14.0 %all_to_all.78 = f32[32,1,128]{2,1,0:T(1,128)S(1)} all-to-all(f32[32,1,128]{2,1,0:T(1,128)S(1)} %bitcast.40), channel_id=1, replica_groups=mesh['dom'=8,'grp'=4] {'dom','grp'}, dimensions={0} | all-to-all | bytes 32768 | tf_op jit(solution)/shard_map/all_to_all | solution.py:470
  37.2 2.2 %precond1.1 = (f32[40,384]{1,0:T(8,128)S(1)}, f32[40,384]{1,0:T(8,128)S(1)}, f32[1,128]{1,0:T(1,128)S(1)}) custom-call(f32[32,128]{1,0:T(8,128)S(1)} %bitcast.37, f32[40,384]{1,0:T(8,128)S(1)} %get-tuple-element.99.refs_1_, f32[40,384]{1,0:T(8,128)S(1)} %get-tuple-element.83.mask_ref.refs_9_.refs_2_, ...), custom_call_target="tpu_custom_call" | custom-call | tf_op jit(solution)/shard_map/precond1/pallas_call | solution.py:419
  39.4 0.1 collective-permute-start.3
  39.5 0.7 collective-permute-start.2
  40.2 0.3 local.7
  40.5 0.2 collective-permute-done.3.refs_1_
  40.7 0.6 near1.1
  41.3 0.0 collective-permute-done.2.refs_0_
  41.3 0.8 image1.1
  42.2 13.6 %all_to_all.79 = f32[32,1,128]{2,1,0:T(1,128)S(1)} all-to-all(f32[32,1,128]{2,1,0:T(1,128)S(1)} %bitcast.41), channel_id=1, replica_groups=mesh['dom'=8,'grp'=4] {'dom','grp'}, dimensions={0} | all-to-all | bytes 32768 | tf_op jit(solution)/shard_map/all_to_all | solution.py:470
  55.7 2.2 %precond2.1 = (f32[40,384]{1,0:T(8,128)S(1)}, f32[40,384]{1,0:T(8,128)S(1)}, f32[1,128]{1,0:T(1,128)S(1)}) custom-call(f32[32,128]{1,0:T(8,128)S(1)} %bitcast.34, f32[40,384]{1,0:T(8,128)S(1)} %get-tuple-element.109.refs_1_, f32[40,384]{1,0:T(8,128)S(1)} %get-tuple-element.83.mask_ref.refs_9_.refs_2_, ...), custom_call_target="tpu_custom_call" | custom-call | tf_op jit(solution)/shard_map/precond2/pallas_call | solution.py:419
  57.9 0.1 collective-permute-start.5
  58.0 0.7 collective-permute-start.4
  58.7 0.3 local.8
  59.0 0.2 collective-permute-done.5.refs_1_
  59.2 0.6 near2.1
  59.8 0.0 collective-permute-done.4.refs_0_
  59.8 0.8 image2.1
  60.7 13.6 %all_to_all.80 = f32[32,1,128]{2,1,0:T(1,128)S(1)} all-to-all(f32[32,1,128]{2,1,0:T(1,128)S(1)} %bitcast.42), channel_id=1, replica_groups=mesh['dom'=8,'grp'=4] {'dom','grp'}, dimensions={0} | all-to-all | bytes 32768 | tf_op jit(solution)/shard_map/all_to_all | solution.py:470
  74.3 2.2 %precond3.1 = (f32[40,384]{1,0:T(8,128)S(1)}, f32[40,384]{1,0:T(8,128)S(1)}, f32[1,128]{1,0:T(1,128)S(1)}) custom-call(f32[32,128]{1,0:T(8,128)S(1)} %bitcast.35, f32[40,384]{1,0:T(8,128)S(1)} %get-tuple-element.121.refs_1_, f32[40,384]{1,0:T(8,128)S(1)} %get-tuple-element.83.mask_ref.refs_9_.refs_2_, ...), custom_call_target="tpu_custom_call" | custom-call | tf_op jit(solution)/shard_map/precond3/pallas_call | solution.py:419
  76.4 0.1 collective-permute-start.7
  76.5 0.7 collective-permute-start.6
  77.2 0.3 local.9
  77.5 0.2 collective-permute-done.7.refs_1_
  77.8 0.6 near3.1
  78.3 0.0 collective-permute-done.6.refs_0_
  78.4 0.8 image3.1
  79.2 13.6 %all_to_all.81 = f32[32,1,128]{2,1,0:T(1,128)S(1)} all-to-all(f32[32,1,128]{2,1,0:T(1,128)S(1)} %bitcast.43), channel_id=1, replica_groups=mesh['dom'=8,'grp'=4] {'dom','grp'}, dimensions={0} | all-to-all | bytes 32768 | tf_op jit(solution)/shard_map/all_to_all | solution.py:470
  92.8 2.2 %precond4.1 = (f32[40,384]{1,0:T(8,128)S(1)}, f32[40,384]{1,0:T(8,128)S(1)}, f32[1,128]{1,0:T(1,128)S(1)}) custom-call(f32[32,128]{1,0:T(8,128)S(1)} %bitcast.36, f32[40,384]{1,0:T(8,128)S(1)} %get-tuple-element.133.refs_1_, f32[40,384]{1,0:T(8,128)S(1)} %get-tuple-element.83.mask_ref.refs_9_.refs_2_, ...), custom_call_target="tpu_custom_call" | custom-call | tf_op jit(solution)/shard_map/precond4/pallas_call | solution.py:419
  95.0 0.1 collective-permute-start.9
  95.0 0.7 collective-permute-start.8
  95.7 0.3 local.10
  96.1 0.2 collective-permute-done.9.refs_1_
  96.3 0.6 near4.1
  96.9 0.0 collective-permute-done.8.refs_0_
  96.9 0.9 image4.1
  97.7 13.6 %all_to_all.82 = f32[32,1,128]{2,1,0:T(1,128)S(1)} all-to-all(f32[32,1,128]{2,1,0:T(1,128)S(1)} %bitcast.44), channel_id=1, replica_groups=mesh['dom'=8,'grp'=4] {'dom','grp'}, dimensions={0} | all-to-all | bytes 32768 | tf_op jit(solution)/shard_map/all_to_all | solution.py:470
  111.3 2.2 %precond5.1 = (f32[40,384]{1,0:T(8,128)S(1)}, f32[40,384]{1,0:T(8,128)S(1)}, f32[1,128]{1,0:T(1,128)S(1)}) custom-call(f32[32,128]{1,0:T(8,128)S(1)} %bitcast.32, f32[40,384]{1,0:T(8,128)S(1)} %get-tuple-element.145.refs_1_, f32[40,384]{1,0:T(8,128)S(1)} %get-tuple-element.83.mask_ref.refs_9_.refs_2_, ...), custom_call_target="tpu_custom_call" | custom-call | tf_op jit(solution)/shard_map/precond5/pallas_call | solution.py:419
  113.5 0.1 collective-permute-start.11
  113.5 0.7 collective-permute-start.10
  114.2 0.3 local.11
  114.6 0.2 collective-permute-done.11.refs_1_
  114.8 0.6 near5.1
  115.4 0.0 collective-permute-done.10.refs_0_
  115.4 0.9 image5.1
  116.2 13.6 %all_to_all.83 = f32[32,1,128]{2,1,0:T(1,128)S(1)} all-to-all(f32[32,1,128]{2,1,0:T(1,128)S(1)} %bitcast.31), channel_id=1, replica_groups=mesh['dom'=8,'grp'=4] {'dom','grp'}, dimensions={0} | all-to-all | bytes 32768 | tf_op jit(solution)/shard_map/all_to_all | solution.py:470
  129.8 0.9 finish.1
Async XLA Ops:
  20.1 1.4 %collective-permute-start.1 = (f32[80,384]{1,0:T(8,128)S(1)}, f32[80,384]{1,0:T(8,128)S(1)}, u32[]{:S(2)}, u32[]{:S(2)}) collective-permute-start(f32[80,384]{1,0:T(8,128)S(1)} %get-tuple-element.86.z_ref.refs_11_.refs_5_), channel_id=1, source_target_pairs={{0,1},{1,0},{2,3},{3,2},{4,5},{5,4},{6,7},{7,6},{8,9},{9,8},{10,11... | collective-permute-start | bytes 368648 | tf_op jit(solution)/shard_map/ppermute | solution.py:496
  20.2 2.1 %collective-permute-start = (f32[80,384]{1,0:T(8,128)S(1)}, f32[80,384]{1,0:T(8,128)S(1)}, u32[]{:S(2)}, u32[]{:S(2)}) collective-permute-start(f32[80,384]{1,0:T(8,128)S(1)} %get-tuple-element.86.z_ref.refs_11_.refs_5_), channel_id=1, source_target_pairs={{1,2},{3,4},{5,6},{7,8},{9,10},{11,12},{13,14},{15,16},{17,18},{19... | collective-permute-start | bytes 368648 | tf_op jit(solution)/shard_map/ppermute | solution.py:495
  39.4 1.3 %collective-permute-start.3 = (f32[40,384]{1,0:T(8,128)S(1)}, f32[40,384]{1,0:T(8,128)S(1)}, u32[]{:S(2)}, u32[]{:S(2)}) collective-permute-start(f32[40,384]{1,0:T(8,128)S(1)} %get-tuple-element.100.refs_0_.z_ref.refs_5_), channel_id=1, source_target_pairs={{0,1},{1,0},{2,3},{3,2},{4,5},{5,4},{6,7},{7,6},{8,9},{9,8},{10,11... | collective-permute-start | bytes 184328 | tf_op jit(solution)/shard_map/ppermute | solution.py:496
  39.5 1.8 %collective-permute-start.2 = (f32[40,384]{1,0:T(8,128)S(1)}, f32[40,384]{1,0:T(8,128)S(1)}, u32[]{:S(2)}, u32[]{:S(2)}) collective-permute-start(f32[40,384]{1,0:T(8,128)S(1)} %get-tuple-element.100.refs_0_.z_ref.refs_5_), channel_id=1, source_target_pairs={{1,2},{3,4},{5,6},{7,8},{9,10},{11,12},{13,14},{15,16},{17,18},{19... | collective-permute-start | bytes 184328 | tf_op jit(solution)/shard_map/ppermute | solution.py:495
  57.9 1.3 %collective-permute-start.5 = (f32[40,384]{1,0:T(8,128)S(1)}, f32[40,384]{1,0:T(8,128)S(1)}, u32[]{:S(2)}, u32[]{:S(2)}) collective-permute-start(f32[40,384]{1,0:T(8,128)S(1)} %get-tuple-element.110.refs_0_.z_ref.refs_5_), channel_id=1, source_target_pairs={{0,1},{1,0},{2,3},{3,2},{4,5},{5,4},{6,7},{7,6},{8,9},{9,8},{10,11... | collective-permute-start | bytes 184328 | tf_op jit(solution)/shard_map/ppermute | solution.py:496
  58.0 1.8 %collective-permute-start.4 = (f32[40,384]{1,0:T(8,128)S(1)}, f32[40,384]{1,0:T(8,128)S(1)}, u32[]{:S(2)}, u32[]{:S(2)}) collective-permute-start(f32[40,384]{1,0:T(8,128)S(1)} %get-tuple-element.110.refs_0_.z_ref.refs_5_), channel_id=1, source_target_pairs={{1,2},{3,4},{5,6},{7,8},{9,10},{11,12},{13,14},{15,16},{17,18},{19... | collective-permute-start | bytes 184328 | tf_op jit(solution)/shard_map/ppermute | solution.py:495
  76.4 1.3 %collective-permute-start.7 = (f32[40,384]{1,0:T(8,128)S(1)}, f32[40,384]{1,0:T(8,128)S(1)}, u32[]{:S(2)}, u32[]{:S(2)}) collective-permute-start(f32[40,384]{1,0:T(8,128)S(1)} %get-tuple-element.122.refs_0_.z_ref.refs_5_), channel_id=1, source_target_pairs={{0,1},{1,0},{2,3},{3,2},{4,5},{5,4},{6,7},{7,6},{8,9},{9,8},{10,11... | collective-permute-start | bytes 184328 | tf_op jit(solution)/shard_map/ppermute | solution.py:496
  76.5 1.8 %collective-permute-start.6 = (f32[40,384]{1,0:T(8,128)S(1)}, f32[40,384]{1,0:T(8,128)S(1)}, u32[]{:S(2)}, u32[]{:S(2)}) collective-permute-start(f32[40,384]{1,0:T(8,128)S(1)} %get-tuple-element.122.refs_0_.z_ref.refs_5_), channel_id=1, source_target_pairs={{1,2},{3,4},{5,6},{7,8},{9,10},{11,12},{13,14},{15,16},{17,18},{19... | collective-permute-start | bytes 184328 | tf_op jit(solution)/shard_map/ppermute | solution.py:495
  95.0 1.3 %collective-permute-start.9 = (f32[40,384]{1,0:T(8,128)S(1)}, f32[40,384]{1,0:T(8,128)S(1)}, u32[]{:S(2)}, u32[]{:S(2)}) collective-permute-start(f32[40,384]{1,0:T(8,128)S(1)} %get-tuple-element.134.refs_0_.z_ref.refs_5_), channel_id=1, source_target_pairs={{0,1},{1,0},{2,3},{3,2},{4,5},{5,4},{6,7},{7,6},{8,9},{9,8},{10,11... | collective-permute-start | bytes 184328 | tf_op jit(solution)/shard_map/ppermute | solution.py:496
  95.0 1.8 %collective-permute-start.8 = (f32[40,384]{1,0:T(8,128)S(1)}, f32[40,384]{1,0:T(8,128)S(1)}, u32[]{:S(2)}, u32[]{:S(2)}) collective-permute-start(f32[40,384]{1,0:T(8,128)S(1)} %get-tuple-element.134.refs_0_.z_ref.refs_5_), channel_id=1, source_target_pairs={{1,2},{3,4},{5,6},{7,8},{9,10},{11,12},{13,14},{15,16},{17,18},{19... | collective-permute-start | bytes 184328 | tf_op jit(solution)/shard_map/ppermute | solution.py:495
  113.5 1.3 %collective-permute-start.11 = (f32[40,384]{1,0:T(8,128)S(1)}, f32[40,384]{1,0:T(8,128)S(1)}, u32[]{:S(2)}, u32[]{:S(2)}) collective-permute-start(f32[40,384]{1,0:T(8,128)S(1)} %get-tuple-element.146.refs_0_.z_ref.refs_1_), channel_id=1, source_target_pairs={{0,1},{1,0},{2,3},{3,2},{4,5},{5,4},{6,7},{7,6},{8,9},{9,8},{10,11... | collective-permute-start | bytes 184328 | tf_op jit(solution)/shard_map/ppermute | solution.py:496
  113.5 1.8 %collective-permute-start.10 = (f32[40,384]{1,0:T(8,128)S(1)}, f32[40,384]{1,0:T(8,128)S(1)}, u32[]{:S(2)}, u32[]{:S(2)}) collective-permute-start(f32[40,384]{1,0:T(8,128)S(1)} %get-tuple-element.146.refs_0_.z_ref.refs_1_), channel_id=1, source_target_pairs={{1,2},{3,4},{5,6},{7,8},{9,10},{11,12},{13,14},{15,16},{17,18},{19... | collective-permute-start | bytes 184328 | tf_op jit(solution)/shard_map/ppermute | solution.py:495

commit v11 on v10

--- a/solution.py
+++ b/solution.py
@@ -76,7 +76,10 @@
 
 
 def full_sum(x):
-    return jnp.sum(jnp.sum(x, axis=0, keepdims=True), axis=1, keepdims=True)
+    tile = sum(
+        x[r : r + 8, c : c + 128] for r in range(0, x.shape[0], 8) for c in range(0, x.shape[1], 128)
+    )
+    return jnp.sum(jnp.sum(tile, axis=1, keepdims=True), axis=0, keepdims=True)
 
 
 def total_scalars(red, count):

time: 131 us -> 131 us (level)
  no operation moved by 1% of the time
where the time goes in v11:
time: 131 us
  blocking collectives  96.1 us (73%)
  Pallas kernels  28 us (21%)
  starting transfers between devices  4.41 us (3%)
  waiting for transfers between devices  1.36 us (1%)
    all_to_all x7, blocking collectives, exchange(): return lax.all_to_all(rows, AXES, 0, 0, tiled=True)  96.1 us
    pallas_call x26, Pallas kernels, call(): pl.pallas_call(kernel, name=name, out_shape=out_shape, in_specs=specs or...  28 us
    ppermute x6, starting transfers between devices, body(): far = lax.ppermute(search, AXES, off_chip)  3.99 us
  transfers between devices with their start and end apart: 12, of which 6 were waited for; matrix products, arithmetic and copies ran while one was open for 0% of the time, Pallas kernels for 4%

profile of v11, /device:TPU:0, one launch (start us, length us, event | category | flops | bytes accessed | tf_op | source)
XLA Modules:
  0.0 130.7 jit_solution(17694887565586293881)
XLA Ops:
  0.6 3.0 %init.1 = (f32[40,384]{1,0:T(8,128)S(1)}, f32[40,384]{1,0:T(8,128)S(1)}, f32[32,128]{1,0:T(8,128)S(1)}, f32[40,384]{1,0:T(8,128)S(1)}, bf16[3,512,256]{2,1,0:T(8...) custom-call(s32[1]{0:T(128)} %bitcast.me_ref, ...), custom_call_target="tpu_custom_call" | custom-call | tf_op jit(solution)/shard_map/init/pallas_call | solution.py:422
  3.7 14.3 %all_to_all.77 = f32[32,1,128]{2,1,0:T(1,128)S(1)} all-to-all(f32[32,1,128]{2,1,0:T(1,128)S(1)} %bitcast.39), channel_id=1, replica_groups=mesh['dom'=8,'grp'=4] {'dom','grp'}, dimensions={0} | all-to-all | bytes 32768 | tf_op jit(solution)/shard_map/all_to_all | solution.py:473
  18.0 2.1 %precond0.1 = (f32[80,384]{1,0:T(8,128)S(1)}, f32[40,384]{1,0:T(8,128)S(1)}, f32[1,128]{1,0:T(1,128)S(1)}) custom-call(f32[32,128]{1,0:T(8,128)S(1)} %bitcast.33, f32[40,384]{1,0:T(8,128)S(1)} %get-tuple-element.82.vec_ref, f32[40,384]{1,0:T(8,128)S(1)} %get-tuple-element.83.mask_ref.refs_9_.refs_2_, ...), custom_call_target="tpu_custom_call" | custom-call | tf_op jit(solution)/shard_map/precond0/pallas_call | solution.py:422
  20.1 0.1 collective-permute-start.1
  20.2 0.7 collective-permute-start
  20.8 0.3 local.6
  21.2 0.3 collective-permute-done.1.chip_ref
  21.5 0.8 near.1
  22.2 0.0 collective-permute-done.refs_0_
  22.3 1.0 image0.1
  23.3 14.0 %all_to_all.78 = f32[32,1,128]{2,1,0:T(1,128)S(1)} all-to-all(f32[32,1,128]{2,1,0:T(1,128)S(1)} %bitcast.40), channel_id=1, replica_groups=mesh['dom'=8,'grp'=4] {'dom','grp'}, dimensions={0} | all-to-all | bytes 32768 | tf_op jit(solution)/shard_map/all_to_all | solution.py:473
  37.2 2.2 %precond1.1 = (f32[40,384]{1,0:T(8,128)S(1)}, f32[40,384]{1,0:T(8,128)S(1)}, f32[1,128]{1,0:T(1,128)S(1)}) custom-call(f32[32,128]{1,0:T(8,128)S(1)} %bitcast.37, f32[40,384]{1,0:T(8,128)S(1)} %get-tuple-element.99.refs_1_, f32[40,384]{1,0:T(8,128)S(1)} %get-tuple-element.83.mask_ref.refs_9_.refs_2_, ...), custom_call_target="tpu_custom_call" | custom-call | tf_op jit(solution)/shard_map/precond1/pallas_call | solution.py:422
  39.4 0.1 collective-permute-start.3
  39.5 0.7 collective-permute-start.2
  40.2 0.3 local.7
  40.5 0.2 collective-permute-done.3.refs_1_
  40.7 0.6 near1.1
  41.3 0.0 collective-permute-done.2.refs_0_
  41.3 0.8 image1.1
  42.2 13.6 %all_to_all.79 = f32[32,1,128]{2,1,0:T(1,128)S(1)} all-to-all(f32[32,1,128]{2,1,0:T(1,128)S(1)} %bitcast.41), channel_id=1, replica_groups=mesh['dom'=8,'grp'=4] {'dom','grp'}, dimensions={0} | all-to-all | bytes 32768 | tf_op jit(solution)/shard_map/all_to_all | solution.py:473
  55.7 2.2 %precond2.1 = (f32[40,384]{1,0:T(8,128)S(1)}, f32[40,384]{1,0:T(8,128)S(1)}, f32[1,128]{1,0:T(1,128)S(1)}) custom-call(f32[32,128]{1,0:T(8,128)S(1)} %bitcast.34, f32[40,384]{1,0:T(8,128)S(1)} %get-tuple-element.109.refs_1_, f32[40,384]{1,0:T(8,128)S(1)} %get-tuple-element.83.mask_ref.refs_9_.refs_2_, ...), custom_call_target="tpu_custom_call" | custom-call | tf_op jit(solution)/shard_map/precond2/pallas_call | solution.py:422
  57.9 0.1 collective-permute-start.5
  58.0 0.7 collective-permute-start.4
  58.7 0.3 local.8
  59.0 0.2 collective-permute-done.5.refs_1_
  59.3 0.6 near2.1
  59.8 0.0 collective-permute-done.4.refs_0_
  59.9 0.9 image2.1
  60.7 13.6 %all_to_all.80 = f32[32,1,128]{2,1,0:T(1,128)S(1)} all-to-all(f32[32,1,128]{2,1,0:T(1,128)S(1)} %bitcast.42), channel_id=1, replica_groups=mesh['dom'=8,'grp'=4] {'dom','grp'}, dimensions={0} | all-to-all | bytes 32768 | tf_op jit(solution)/shard_map/all_to_all | solution.py:473
  74.3 2.2 %precond3.1 = (f32[40,384]{1,0:T(8,128)S(1)}, f32[40,384]{1,0:T(8,128)S(1)}, f32[1,128]{1,0:T(1,128)S(1)}) custom-call(f32[32,128]{1,0:T(8,128)S(1)} %bitcast.35, f32[40,384]{1,0:T(8,128)S(1)} %get-tuple-element.121.refs_1_, f32[40,384]{1,0:T(8,128)S(1)} %get-tuple-element.83.mask_ref.refs_9_.refs_2_, ...), custom_call_target="tpu_custom_call" | custom-call | tf_op jit(solution)/shard_map/precond3/pallas_call | solution.py:422
  76.5 0.1 collective-permute-start.7
  76.5 0.7 collective-permute-start.6
  77.2 0.3 local.9
  77.6 0.2 collective-permute-done.7.refs_1_
  77.8 0.6 near3.1
  78.4 0.0 collective-permute-done.6.refs_0_
  78.4 0.9 image3.1
  79.2 13.6 %all_to_all.81 = f32[32,1,128]{2,1,0:T(1,128)S(1)} all-to-all(f32[32,1,128]{2,1,0:T(1,128)S(1)} %bitcast.43), channel_id=1, replica_groups=mesh['dom'=8,'grp'=4] {'dom','grp'}, dimensions={0} | all-to-all | bytes 32768 | tf_op jit(solution)/shard_map/all_to_all | solution.py:473
  92.8 2.2 %precond4.1 = (f32[40,384]{1,0:T(8,128)S(1)}, f32[40,384]{1,0:T(8,128)S(1)}, f32[1,128]{1,0:T(1,128)S(1)}) custom-call(f32[32,128]{1,0:T(8,128)S(1)} %bitcast.36, f32[40,384]{1,0:T(8,128)S(1)} %get-tuple-element.133.refs_1_, f32[40,384]{1,0:T(8,128)S(1)} %get-tuple-element.83.mask_ref.refs_9_.refs_2_, ...), custom_call_target="tpu_custom_call" | custom-call | tf_op jit(solution)/shard_map/precond4/pallas_call | solution.py:422
  95.0 0.1 collective-permute-start.9
  95.1 0.7 collective-permute-start.8
  95.7 0.3 local.10
  96.1 0.2 collective-permute-done.9.refs_1_
  96.3 0.6 near4.1
  96.9 0.0 collective-permute-done.8.refs_0_
  96.9 0.9 image4.1
  97.8 13.6 %all_to_all.82 = f32[32,1,128]{2,1,0:T(1,128)S(1)} all-to-all(f32[32,1,128]{2,1,0:T(1,128)S(1)} %bitcast.44), channel_id=1, replica_groups=mesh['dom'=8,'grp'=4] {'dom','grp'}, dimensions={0} | all-to-all | bytes 32768 | tf_op jit(solution)/shard_map/all_to_all | solution.py:473
  111.3 2.2 %precond5.1 = (f32[40,384]{1,0:T(8,128)S(1)}, f32[40,384]{1,0:T(8,128)S(1)}, f32[1,128]{1,0:T(1,128)S(1)}) custom-call(f32[32,128]{1,0:T(8,128)S(1)} %bitcast.32, f32[40,384]{1,0:T(8,128)S(1)} %get-tuple-element.145.refs_1_, f32[40,384]{1,0:T(8,128)S(1)} %get-tuple-element.83.mask_ref.refs_9_.refs_2_, ...), custom_call_target="tpu_custom_call" | custom-call | tf_op jit(solution)/shard_map/precond5/pallas_call | solution.py:422
  113.5 0.1 collective-permute-start.11
  113.6 0.7 collective-permute-start.10
  114.3 0.3 local.11
  114.6 0.2 collective-permute-done.11.refs_1_
  114.8 0.6 near5.1
  115.4 0.0 collective-permute-done.10.refs_0_
  115.4 0.9 image5.1
  116.3 13.6 %all_to_all.83 = f32[32,1,128]{2,1,0:T(1,128)S(1)} all-to-all(f32[32,1,128]{2,1,0:T(1,128)S(1)} %bitcast.31), channel_id=1, replica_groups=mesh['dom'=8,'grp'=4] {'dom','grp'}, dimensions={0} | all-to-all | bytes 32768 | tf_op jit(solution)/shard_map/all_to_all | solution.py:473
  129.9 0.9 finish.1
Async XLA Ops:
  20.1 1.4 %collective-permute-start.1 = (f32[80,384]{1,0:T(8,128)S(1)}, f32[80,384]{1,0:T(8,128)S(1)}, u32[]{:S(2)}, u32[]{:S(2)}) collective-permute-start(f32[80,384]{1,0:T(8,128)S(1)} %get-tuple-element.86.z_ref.refs_11_.refs_5_), channel_id=1, source_target_pairs={{0,1},{1,0},{2,3},{3,2},{4,5},{5,4},{6,7},{7,6},{8,9},{9,8},{10,11... | collective-permute-start | bytes 368648 | tf_op jit(solution)/shard_map/ppermute | solution.py:499
  20.2 2.1 %collective-permute-start = (f32[80,384]{1,0:T(8,128)S(1)}, f32[80,384]{1,0:T(8,128)S(1)}, u32[]{:S(2)}, u32[]{:S(2)}) collective-permute-start(f32[80,384]{1,0:T(8,128)S(1)} %get-tuple-element.86.z_ref.refs_11_.refs_5_), channel_id=1, source_target_pairs={{1,2},{3,4},{5,6},{7,8},{9,10},{11,12},{13,14},{15,16},{17,18},{19... | collective-permute-start | bytes 368648 | tf_op jit(solution)/shard_map/ppermute | solution.py:498
  39.4 1.3 %collective-permute-start.3 = (f32[40,384]{1,0:T(8,128)S(1)}, f32[40,384]{1,0:T(8,128)S(1)}, u32[]{:S(2)}, u32[]{:S(2)}) collective-permute-start(f32[40,384]{1,0:T(8,128)S(1)} %get-tuple-element.100.refs_0_.z_ref.refs_5_), channel_id=1, source_target_pairs={{0,1},{1,0},{2,3},{3,2},{4,5},{5,4},{6,7},{7,6},{8,9},{9,8},{10,11... | collective-permute-start | bytes 184328 | tf_op jit(solution)/shard_map/ppermute | solution.py:499
  39.5 1.8 %collective-permute-start.2 = (f32[40,384]{1,0:T(8,128)S(1)}, f32[40,384]{1,0:T(8,128)S(1)}, u32[]{:S(2)}, u32[]{:S(2)}) collective-permute-start(f32[40,384]{1,0:T(8,128)S(1)} %get-tuple-element.100.refs_0_.z_ref.refs_5_), channel_id=1, source_target_pairs={{1,2},{3,4},{5,6},{7,8},{9,10},{11,12},{13,14},{15,16},{17,18},{19... | collective-permute-start | bytes 184328 | tf_op jit(solution)/shard_map/ppermute | solution.py:498
  57.9 1.3 %collective-permute-start.5 = (f32[40,384]{1,0:T(8,128)S(1)}, f32[40,384]{1,0:T(8,128)S(1)}, u32[]{:S(2)}, u32[]{:S(2)}) collective-permute-start(f32[40,384]{1,0:T(8,128)S(1)} %get-tuple-element.110.refs_0_.z_ref.refs_5_), channel_id=1, source_target_pairs={{0,1},{1,0},{2,3},{3,2},{4,5},{5,4},{6,7},{7,6},{8,9},{9,8},{10,11... | collective-permute-start | bytes 184328 | tf_op jit(solution)/shard_map/ppermute | solution.py:499
  58.0 1.8 %collective-permute-start.4 = (f32[40,384]{1,0:T(8,128)S(1)}, f32[40,384]{1,0:T(8,128)S(1)}, u32[]{:S(2)}, u32[]{:S(2)}) collective-permute-start(f32[40,384]{1,0:T(8,128)S(1)} %get-tuple-element.110.refs_0_.z_ref.refs_5_), channel_id=1, source_target_pairs={{1,2},{3,4},{5,6},{7,8},{9,10},{11,12},{13,14},{15,16},{17,18},{19... | collective-permute-start | bytes 184328 | tf_op jit(solution)/shard_map/ppermute | solution.py:498
  76.5 1.3 %collective-permute-start.7 = (f32[40,384]{1,0:T(8,128)S(1)}, f32[40,384]{1,0:T(8,128)S(1)}, u32[]{:S(2)}, u32[]{:S(2)}) collective-permute-start(f32[40,384]{1,0:T(8,128)S(1)} %get-tuple-element.122.refs_0_.z_ref.refs_5_), channel_id=1, source_target_pairs={{0,1},{1,0},{2,3},{3,2},{4,5},{5,4},{6,7},{7,6},{8,9},{9,8},{10,11... | collective-permute-start | bytes 184328 | tf_op jit(solution)/shard_map/ppermute | solution.py:499
  76.5 1.8 %collective-permute-start.6 = (f32[40,384]{1,0:T(8,128)S(1)}, f32[40,384]{1,0:T(8,128)S(1)}, u32[]{:S(2)}, u32[]{:S(2)}) collective-permute-start(f32[40,384]{1,0:T(8,128)S(1)} %get-tuple-element.122.refs_0_.z_ref.refs_5_), channel_id=1, source_target_pairs={{1,2},{3,4},{5,6},{7,8},{9,10},{11,12},{13,14},{15,16},{17,18},{19... | collective-permute-start | bytes 184328 | tf_op jit(solution)/shard_map/ppermute | solution.py:498
  95.0 1.3 %collective-permute-start.9 = (f32[40,384]{1,0:T(8,128)S(1)}, f32[40,384]{1,0:T(8,128)S(1)}, u32[]{:S(2)}, u32[]{:S(2)}) collective-permute-start(f32[40,384]{1,0:T(8,128)S(1)} %get-tuple-element.134.refs_0_.z_ref.refs_5_), channel_id=1, source_target_pairs={{0,1},{1,0},{2,3},{3,2},{4,5},{5,4},{6,7},{7,6},{8,9},{9,8},{10,11... | collective-permute-start | bytes 184328 | tf_op jit(solution)/shard_map/ppermute | solution.py:499
  95.1 1.8 %collective-permute-start.8 = (f32[40,384]{1,0:T(8,128)S(1)}, f32[40,384]{1,0:T(8,128)S(1)}, u32[]{:S(2)}, u32[]{:S(2)}) collective-permute-start(f32[40,384]{1,0:T(8,128)S(1)} %get-tuple-element.134.refs_0_.z_ref.refs_5_), channel_id=1, source_target_pairs={{1,2},{3,4},{5,6},{7,8},{9,10},{11,12},{13,14},{15,16},{17,18},{19... | collective-permute-start | bytes 184328 | tf_op jit(solution)/shard_map/ppermute | solution.py:498
  113.5 1.3 %collective-permute-start.11 = (f32[40,384]{1,0:T(8,128)S(1)}, f32[40,384]{1,0:T(8,128)S(1)}, u32[]{:S(2)}, u32[]{:S(2)}) collective-permute-start(f32[40,384]{1,0:T(8,128)S(1)} %get-tuple-element.146.refs_0_.z_ref.refs_1_), channel_id=1, source_target_pairs={{0,1},{1,0},{2,3},{3,2},{4,5},{5,4},{6,7},{7,6},{8,9},{9,8},{10,11... | collective-permute-start | bytes 184328 | tf_op jit(solution)/shard_map/ppermute | solution.py:499
  113.6 1.8 %collective-permute-start.10 = (f32[40,384]{1,0:T(8,128)S(1)}, f32[40,384]{1,0:T(8,128)S(1)}, u32[]{:S(2)}, u32[]{:S(2)}) collective-permute-start(f32[40,384]{1,0:T(8,128)S(1)} %get-tuple-element.146.refs_0_.z_ref.refs_1_), channel_id=1, source_target_pairs={{1,2},{3,4},{5,6},{7,8},{9,10},{11,12},{13,14},{15,16},{17,18},{19... | collective-permute-start | bytes 184328 | tf_op jit(solution)/shard_map/ppermute | solution.py:498
